TPU v7x, 512 devices: a whole 4x8x8 slice. The times are simulated.
512 devices in a mesh: seq: 64 (over z, y_lo, core), head: 8 (over y_hi, x).
Axes of the slice: x: 4, y: 8 (y_hi: 2, y_lo: 4; y = y_hi * 4 + y_lo), z: 8, core: 2. Of those that a mesh axis runs over, the one named last changes fastest.
Arguments:
- query_in: bfloat16 [24576, 2048], P('seq', 'head'), may hold values from -6 to 6
- key_in: bfloat16 [24576, 2048], P('seq', 'head'), may hold values from -6 to 6
- value_in: bfloat16 [24576, 2048], P('seq', 'head'), may hold values from -6 to 6
- text_keys: bfloat16 [256, 2048], P(None, 'head'), may hold values from -6 to 6
- text_values: bfloat16 [256, 2048], P(None, 'head'), may hold values from -6 to 6
- text_mask: int32 [256], replicated, may hold values 0 or 1
- window_reach: int32 [16, 2], P('head'), may hold values from 0 to 1
- tile_map: int32 [64, 3], replicated, may hold values from 0 to 14, as said below
- out_weight: bfloat16 [2048, 3072], P('head'), may hold values from -0.125 to 0.125
- gate_scale: float32 [3072], replicated, may hold values from -4 to 4
- grad_out: bfloat16 [24576, 3072], P('seq', 'head'), may hold values from -12 to 12
Outputs:
- grad_query: bfloat16 [24576, 2048], P('seq', 'head')
- grad_key: bfloat16 [24576, 2048], P('seq', 'head')
- grad_value: bfloat16 [24576, 2048], P('seq', 'head')
- grad_text_keys: bfloat16 [256, 2048], P(None, 'head')
- grad_text_values: bfloat16 [256, 2048], P(None, 'head')
- grad_gate: float32 [3072], replicated
Inputs may be any that keep to these rules, and one draw needn't show every extreme that they name: `tile_map`: index i of seq sits at grid row i // 8 and grid column i % 8. Its tile row is that grid row, or 7 minus it, plus an offset; its tile column is the grid column, or 7 minus it, plus an offset; the mirroring and the offsets are the same for all indices, and so is the frame coordinate. Of the two offsets, the one of the longer grid dimension (rows when they are equal) is 7, the other 0.
All inputs are finite; a program needn't handle non-finite values.
Results may differ from a plain program's by a relative error of at most 0.02035.
The roundings to bfloat16 on the way count: a program that leaves them out, or rounds other values in their place, can miss the bound.
Values may be sent and summed in bfloat16 or wider, within the bound.
No kernel may reach another device: no remote copies, remote signals or barrier semaphores. Data moves between devices by JAX's collectives and lax.ppermute only.
A program may use at most 64 MiB of HBM per device.

v0:
```python
import functools
import math

import jax
import jax.numpy as jnp
import numpy as np
from jax import lax
from jax.experimental import pallas as pl
from jax.experimental.pallas import tpu as pltpu
from jax.sharding import Mesh
from jax.sharding import PartitionSpec as P


HEAD_DIM = 128
TILE_H = 8
TILE_W = 8
SECTIONS = ((0, 16), (16, 56), (72, 56))
THETA = 256.0
SCALE = HEAD_DIM ** -0.5
LOG2E = math.log2(math.e)
C1 = SCALE * LOG2E
SEQ = ("z", "y", "core")
COL = ("y", "core")
HEAD = ("yhi", "x")
F32 = jnp.float32
BF16 = jnp.bfloat16
NEG = -1e30
VMEM_LIMIT = 66_000_000


def dot_nn(a, b):
    return lax.dot_general(a, b, (((1,), (0,)), ((), ())), preferred_element_type=F32)


def dot_nt(a, b):
    return lax.dot_general(a, b, (((1,), (1,)), ((), ())), preferred_element_type=F32)


def dot_tn(a, b):
    return lax.dot_general(a, b, (((0,), (0,)), ((), ())), preferred_element_type=F32)


def params(*semantics):
    return pltpu.CompilerParams(
        dimension_semantics=semantics or None, vmem_limit_bytes=VMEM_LIMIT
    )


def lane_freqs():
    freqs = np.zeros((8, HEAD_DIM), np.float32)
    for offset, length in SECTIONS:
        half = length // 2
        f = np.float32(THETA) ** (
            np.float32(-2.0) * np.arange(half, dtype=np.float32) / np.float32(length)
        )
        freqs[:, offset : offset + half] = f
        freqs[:, offset + half : offset + length] = f
    return freqs


def partner(x, lane):
    near = jnp.where(lane < 8, pltpu.roll(x, HEAD_DIM - 8, 1), pltpu.roll(x, 8, 1))
    first = ((lane >= 16) & (lane < 44)) | ((lane >= 72) & (lane < 100))
    far = jnp.where(first, pltpu.roll(x, HEAD_DIM - 28, 1), pltpu.roll(x, 28, 1))
    return jnp.where(lane < 16, near, far)


def whole(shape):
    return pl.BlockSpec(shape, lambda *_: (0,) * len(shape))


def smem():
    return pl.BlockSpec(memory_space=pltpu.SMEM)


def rot_kernel(info, freq, q, k, v, q_out, kv_out, cos_out, sin_out):
    tile = q.shape[0]

    @pl.when(pl.program_id(0) == 0)
    def _():
        frames = tile // (TILE_H * TILE_W)
        step = lax.broadcasted_iota(jnp.int32, (8, HEAD_DIM), 0)
        lane = lax.broadcasted_iota(jnp.int32, (8, HEAD_DIM), 1)
        first = (
            (lane < 8) | ((lane >= 16) & (lane < 44)) | ((lane >= 72) & (lane < 100))
        )
        f = freq[...]

        def table(base):
            angle = (base + step).astype(F32) * f
            s = jnp.sin(angle)
            return jnp.cos(angle), jnp.where(first, -s, s)

        cf, sf = table(info[4] * frames)
        cr, sr = table(info[5] * TILE_H)
        cc, sc = table(info[6] * TILE_W)
        for r in range(TILE_H):
            crr = jnp.where(lane < 72, cr[r : r + 1, :], cc)
            srr = jnp.where(lane < 72, sr[r : r + 1, :], sc)
            for t in range(frames):
                at = (t * TILE_H + r) * TILE_W
                cos_out[at : at + TILE_W, :] = jnp.where(lane < 16, cf[t : t + 1, :], crr)
                sin_out[at : at + TILE_W, :] = jnp.where(lane < 16, sf[t : t + 1, :], srr)

    lane = lax.broadcasted_iota(jnp.int32, (tile, HEAD_DIM), 1)
    cos, sin = cos_out[...], sin_out[...]
    for source, target in ((q, q_out), (k, kv_out.at[0])):
        x = source[...].astype(F32)
        target[...] = (x * cos + partner(x, lane) * sin).astype(BF16)
    kv_out[1] = v[...]


def rotate_call(info, q_in, k_in, v_in):
    tile, width = q_in.shape
    heads = width // HEAD_DIM
    half = pl.BlockSpec((tile, HEAD_DIM), lambda h: (0, h))
    table = whole((tile, HEAD_DIM))
    return pl.pallas_call(
        rot_kernel,
        grid=(heads,),
        in_specs=[smem(), whole((8, HEAD_DIM)), half, half, half],
        out_specs=[half, pl.BlockSpec((2, tile, HEAD_DIM), lambda h: (0, 0, h)), table, table],
        out_shape=[
            jax.ShapeDtypeStruct((tile, width), BF16),
            jax.ShapeDtypeStruct((2, tile, width), BF16),
            jax.ShapeDtypeStruct((tile, HEAD_DIM), F32),
            jax.ShapeDtypeStruct((tile, HEAD_DIM), F32),
        ],
        compiler_params=params("arbitrary"),
        name="rot",
    )(info, jnp.asarray(lane_freqs()), q_in, k_in, v_in)


def open_block(info, h, a, b):
    ok = (info[8 + 2 * h] >= abs(a)) & (info[9 + 2 * h] >= abs(b))
    if a:
        row = info[0] + a
        ok = ok & (row >= 0) & (row < info[2])
    if b:
        col = info[1] + b
        ok = ok & (col >= 0) & (col < info[3])
    return ok


def fwd_block(keys, values, extra, q, m, l, acc):
    s = dot_nt(keys, q[...]) * C1
    if extra is not None:
        s = s + extra
    m_old = m[0:1, :]
    m_new = jnp.maximum(m_old, jnp.max(s, axis=0, keepdims=True))
    p = jnp.exp2(s - m_new)
    alpha = jnp.exp2(m_old - m_new)
    m[0:1, :] = m_new
    l[0:1, :] = l[0:1, :] * alpha + jnp.sum(p, axis=0, keepdims=True)
    acc[...] = acc[...] * alpha + dot_tn(values, p.astype(BF16))


def fwd_near_kernel(info, q, own, up, down, tk, tv, bias, acc, m, l):
    h = pl.program_id(0)
    m[...] = jnp.full(m.shape, NEG, F32)
    l[...] = jnp.zeros(l.shape, F32)
    acc[...] = jnp.zeros(acc.shape, F32)
    fwd_block(own[0], own[1], None, q, m, l, acc)
    fwd_block(tk[...], tv[...], bias[...], q, m, l, acc)
    for a, ref in ((-1, up), (1, down)):

        @pl.when(open_block(info, h, a, 0))
        def _(ref=ref):
            fwd_block(ref[0], ref[1], None, q, m, l, acc)


def fwd_side_kernel(info, q, left, right, acc_in, m_in, l_in, ot_out, lse_out, acc, m, l):
    h = pl.program_id(0)
    acc[...] = acc_in[...]
    m[...] = m_in[...]
    l[...] = l_in[...]
    for b, ref in ((-1, left), (1, right)):
        for a in (-1, 0, 1):

            @pl.when(open_block(info, h, a, b))
            def _(ref=ref, a=a):
                fwd_block(ref[a + 1, 0], ref[a + 1, 1], None, q, m, l, acc)

    ot_out[...] = (acc[...] * (1.0 / l[0:1, :])).astype(BF16)
    lse_out[...] = jnp.broadcast_to(m[0:1, :] + jnp.log2(l[0:1, :]), lse_out.shape)


def kv_spec(tile):
    return pl.BlockSpec((2, tile, HEAD_DIM), lambda h: (0, 0, h))


def stack_spec(tile):
    return pl.BlockSpec((3, 2, tile, HEAD_DIM), lambda h: (0, 0, 0, h))


def half_spec(rows):
    return pl.BlockSpec((rows, HEAD_DIM), lambda h: (0, h))


def row_spec(rows, tile):
    return pl.BlockSpec((rows, tile), lambda h: (h, 0))


def fwd_near_call(info, q, own, up, down, text_keys, text_values, bias):
    tile, width = q.shape
    heads = width // HEAD_DIM
    txt = text_keys.shape[0]
    keys = 3 * tile + txt
    stats = jax.ShapeDtypeStruct((8 * heads, tile), F32)
    return pl.pallas_call(
        fwd_near_kernel,
        grid=(heads,),
        in_specs=[smem(), half_spec(tile)]
        + [kv_spec(tile)] * 3
        + [half_spec(txt), half_spec(txt), whole((txt, 1))],
        out_specs=[row_spec(HEAD_DIM, tile), row_spec(8, tile), row_spec(8, tile)],
        out_shape=[jax.ShapeDtypeStruct((width, tile), F32), stats, stats],
        compiler_params=params("arbitrary"),
        cost_estimate=pl.CostEstimate(
            flops=4 * tile * keys * width, bytes_accessed=4 * keys * width, transcendentals=0
        ),
        name="fwd_near",
    )(info, q, own, up, down, text_keys, text_values, bias)


def fwd_side_call(info, q, left, right, acc, m, l):
    tile, width = q.shape
    heads = width // HEAD_DIM
    keys = 6 * tile
    return pl.pallas_call(
        fwd_side_kernel,
        grid=(heads,),
        in_specs=[
            smem(),
            half_spec(tile),
            stack_spec(tile),
            stack_spec(tile),
            row_spec(HEAD_DIM, tile),
            row_spec(8, tile),
            row_spec(8, tile),
        ],
        out_specs=[row_spec(HEAD_DIM, tile), row_spec(8, tile)],
        out_shape=[
            jax.ShapeDtypeStruct((width, tile), BF16),
            jax.ShapeDtypeStruct((8 * heads, tile), F32),
        ],
        scratch_shapes=[
            pltpu.VMEM((HEAD_DIM, tile), F32),
            pltpu.VMEM((8, tile), F32),
            pltpu.VMEM((8, tile), F32),
        ],
        compiler_params=params("arbitrary"),
        cost_estimate=pl.CostEstimate(
            flops=4 * tile * keys * width, bytes_accessed=4 * keys * width, transcendentals=0
        ),
        name="fwd_side",
    )(info, q, left, right, acc, m, l)


def stack_kernel(up, own, down, out):
    out[0] = up[...]
    out[1] = own[...]
    out[2] = down[...]


def stack_call(up, own, down):
    tile, width = own.shape[1:]
    return pl.pallas_call(
        stack_kernel,
        grid=(width // HEAD_DIM,),
        in_specs=[kv_spec(tile)] * 3,
        out_specs=stack_spec(tile),
        out_shape=jax.ShapeDtypeStruct((3, 2, tile, width), BF16),
        compiler_params=params("arbitrary"),
        name="stack",
    )(up, own, down)


def proj_kernel(steps, last, info, w, gate, ot, *refs):
    pieces, rest = refs[: len(steps)], refs[len(steps) :]
    if last:
        acc_in, gate_in, dot_out, delta_out, gate_out = rest
    else:
        acc_out, gate_out = rest
    heads_x, heads_y = info[16], info[17]
    acc = acc_in[...] if last else None
    if last:
        gate_out[...] = gate_in[...]
    else:
        gate_out[...] = jnp.zeros(gate_out.shape, F32)
    tile = ot.shape[1]
    for piece, (flip, dx) in zip(pieces, steps):
        y = info[18] if not flip else heads_y - 1 - info[18]
        x = lax.rem(info[19] + dx + heads_x, heads_x)
        block = y * heads_x + x
        cols = piece.shape[1]
        at = pl.multiple_of(block * cols, 128)
        g = piece[...].astype(F32)
        scaled = (g * gate[:, pl.ds(at, cols)]).astype(BF16)
        wp = w[:, pl.ds(at, cols)]
        part = dot_nt(wp, scaled)
        acc = part if acc is None else acc + part
        terms = dot_nn(ot[...], piece[...]) * wp.astype(F32)
        row = jnp.sum(terms, axis=0, keepdims=True)
        for i in range(cols // 128):
            gate_out[pl.ds(block * (cols // 128) + i, 1), :] = row[:, i * 128 : (i + 1) * 128]
    if not last:
        acc_out[...] = acc
    else:
        rounded = acc.astype(BF16)
        dot_out[...] = rounded
        prod = rounded.astype(F32) * ot[...].astype(F32)
        for h in range(ot.shape[0] // HEAD_DIM):
            d = jnp.sum(prod[h * HEAD_DIM : (h + 1) * HEAD_DIM, :], axis=0, keepdims=True)
            delta_out[8 * h : 8 * h + 8, :] = jnp.broadcast_to(d, (8, tile))


def proj_call(steps, info, w, gate, ot, pieces, carried=None):
    width, tile = ot.shape
    heads = width // HEAD_DIM
    cols = pieces[0].shape[1]
    rows = w.shape[1] // 128
    last = carried is not None
    acc = jax.ShapeDtypeStruct((width, tile), F32)
    gates = jax.ShapeDtypeStruct((rows, 128), F32)
    if last:
        out_shape = [
            jax.ShapeDtypeStruct((width, tile), BF16),
            jax.ShapeDtypeStruct((8 * heads, tile), F32),
            gates,
        ]
    else:
        out_shape = [acc, gates]
    operands = (info, w, gate, ot, *pieces) + (tuple(carried) if last else ())
    return pl.pallas_call(
        functools.partial(proj_kernel, steps, last),
        in_specs=[smem()] + [pl.BlockSpec(memory_space=pltpu.VMEM)] * (len(operands) - 1),
        out_specs=[pl.BlockSpec(memory_space=pltpu.VMEM)] * len(out_shape),
        out_shape=out_shape,
        compiler_params=params(),
        cost_estimate=pl.CostEstimate(
            flops=4 * tile * width * cols * len(pieces),
            bytes_accessed=2 * tile * cols * len(pieces) + 2 * w.size,
            transcendentals=0,
        ),
        name="proj",
    )(*operands)


def bwd_math(keys, values, q, dot, lse, delta, dq, extra):
    s = dot_nt(keys, q[...]) * C1
    if extra is not None:
        s = s + extra
    p = jnp.exp2(s - lse[0:1, :])
    dp = dot_nn(values, dot[...])
    ds = (p * (dp - delta[0:1, :])).astype(BF16)
    dv = dot_nt(p.astype(BF16), dot[...])
    dk = dot_nn(ds, q[...]) * SCALE
    dq[...] += dot_tn(keys, ds)
    return dk, dv


def bwd_block(info, h, a, b, block, out, q, dot, lse, delta, dq):
    def run():
        dk, dv = bwd_math(block[0], block[1], q, dot, lse, delta, dq, None)
        out[0] = dk.astype(out.dtype)
        out[1] = dv.astype(out.dtype)

    if (a, b) == (0, 0):
        run()
    else:
        ok = open_block(info, h, a, b)
        pl.when(ok)(run)

        @pl.when(jnp.logical_not(ok))
        def _():
            out[...] = jnp.zeros(out.shape, out.dtype)


def bwd_side_kernel(
    info, q, dot, lse, delta, tk, tv, bias, left, right, left_out, right_out, text_out, dq_out
):
    h = pl.program_id(0)
    dq_out[...] = jnp.zeros(dq_out.shape, F32)
    dk, dv = bwd_math(tk[...], tv[...], q, dot, lse, delta, dq_out, bias[...])
    text_out[0] = dk.astype(BF16)
    text_out[1] = dv.astype(BF16)
    for b, ref, out in ((-1, left, left_out), (1, right, right_out)):
        for a in (-1, 0, 1):
            bwd_block(
                info, h, a, b, ref.at[a + 1], out.at[a + 1], q, dot, lse, delta, dq_out
            )


def bwd_near_kernel(
    info, q, dot, lse, delta, dq_in, cos, sin, up, own, down, up_out, own_out, down_out, gq_out, dq
):
    h = pl.program_id(0)
    dq[...] = dq_in[...]
    for a, ref, out in ((-1, up, up_out), (1, down, down_out), (0, own, own_out)):
        bwd_block(info, h, a, 0, ref, out, q, dot, lse, delta, dq)
    x = jnp.transpose(dq[...]) * SCALE
    lane = lax.broadcasted_iota(jnp.int32, x.shape, 1)
    gq_out[...] = (x * cos[...] - partner(x, lane) * sin[...]).astype(BF16)


def bwd_specs(tile):
    return [
        smem(),
        pl.BlockSpec((tile, HEAD_DIM), lambda h: (0, h)),
        pl.BlockSpec((HEAD_DIM, tile), lambda h: (h, 0)),
        pl.BlockSpec((8, tile), lambda h: (h, 0)),
        pl.BlockSpec((8, tile), lambda h: (h, 0)),
    ]


def bwd_cost(tile, keys, width):
    return pl.CostEstimate(
        flops=10 * tile * keys * width, bytes_accessed=8 * keys * width, transcendentals=0
    )


def bwd_side_call(common, text_keys, text_values, bias, left, right):
    info, q, dot, lse, delta = common
    tile, width = q.shape
    txt = text_keys.shape[0]
    stack = jax.ShapeDtypeStruct((3, 2, tile, width), BF16)
    return pl.pallas_call(
        bwd_side_kernel,
        grid=(width // HEAD_DIM,),
        in_specs=bwd_specs(tile)
        + [half_spec(txt), half_spec(txt), whole((txt, 1))]
        + [stack_spec(tile)] * 2,
        out_specs=[stack_spec(tile)] * 2 + [kv_spec(txt), row_spec(HEAD_DIM, tile)],
        out_shape=[
            stack,
            stack,
            jax.ShapeDtypeStruct((2, txt, width), BF16),
            jax.ShapeDtypeStruct((width, tile), F32),
        ],
        compiler_params=params("arbitrary"),
        cost_estimate=bwd_cost(tile, 6 * tile + txt, width),
        name="bwd_side",
    )(info, q, dot, lse, delta, text_keys, text_values, bias, left, right)


def bwd_near_call(common, dq, cos, sin, up, own, down):
    info, q, dot, lse, delta = common
    tile, width = q.shape
    table = whole((tile, HEAD_DIM))
    part = jax.ShapeDtypeStruct((2, tile, width), F32)
    return pl.pallas_call(
        bwd_near_kernel,
        grid=(width // HEAD_DIM,),
        in_specs=bwd_specs(tile)
        + [row_spec(HEAD_DIM, tile), table, table]
        + [kv_spec(tile)] * 3,
        out_specs=[kv_spec(tile)] * 3 + [half_spec(tile)],
        out_shape=[part, part, part, jax.ShapeDtypeStruct((tile, width), BF16)],
        scratch_shapes=[pltpu.VMEM((HEAD_DIM, tile), F32)],
        compiler_params=params("arbitrary"),
        cost_estimate=bwd_cost(tile, 3 * tile, width),
        name="bwd_near",
    )(info, q, dot, lse, delta, dq, cos, sin, up, own, down)


def pair_sum_kernel(up, down, left, right, up_out, down_out):
    for i, part, out in ((0, up, up_out), (2, down, down_out)):
        out[...] = (part[...] + left[i].astype(F32) + right[i].astype(F32)).astype(BF16)


def pair_sum_call(up, down, left, right):
    tile, width = up.shape[1:]
    shape = jax.ShapeDtypeStruct((2, tile, width), BF16)
    return pl.pallas_call(
        pair_sum_kernel,
        grid=(width // HEAD_DIM,),
        in_specs=[kv_spec(tile)] * 2 + [stack_spec(tile)] * 2,
        out_specs=[kv_spec(tile)] * 2,
        out_shape=[shape] * 2,
        compiler_params=params("arbitrary"),
        name="pair_sum",
    )(up, down, left, right)


def finish_kernel(own, left, right, up, down, cos, sin, gk_out, gv_out):
    total = own[...]
    for other in (left[0], right[0], up[...], down[...]):
        total = total + other.astype(F32)
    x = total[0]
    lane = lax.broadcasted_iota(jnp.int32, x.shape, 1)
    gk_out[...] = (x * cos[...] - partner(x, lane) * sin[...]).astype(BF16)
    gv_out[...] = total[1].astype(BF16)


def finish_call(own, left, right, up, down, cos, sin):
    tile, width = own.shape[1:]
    table = whole((tile, HEAD_DIM))
    middle = pl.BlockSpec((1, 2, tile, HEAD_DIM), lambda h: (1, 0, 0, h))
    shape = jax.ShapeDtypeStruct((tile, width), BF16)
    return pl.pallas_call(
        finish_kernel,
        grid=(width // HEAD_DIM,),
        in_specs=[kv_spec(tile), middle, middle, kv_spec(tile), kv_spec(tile), table, table],
        out_specs=[half_spec(tile)] * 2,
        out_shape=[shape, shape],
        compiler_params=params("arbitrary"),
        name="finish",
    )(own, left, right, up, down, cos, sin)


def chunk_sum_kernel(got, gate, out):
    groups, rows, width = got.shape
    text = jnp.sum(got[...].astype(F32), axis=0).astype(BF16)
    out[:, :, :width] = jnp.broadcast_to(text[None], (groups, rows, width))
    for i in range(gate.shape[0] // rows):
        part = gate[i * rows : (i + 1) * rows, :].astype(BF16)
        at = width + 128 * i
        out[:, :, at : at + 128] = jnp.broadcast_to(part[None], (groups, rows, 128))


def chunk_sum_call(got, gate):
    groups, rows, width = got.shape
    lanes = width + 128 * (gate.shape[0] // rows)
    return pl.pallas_call(
        chunk_sum_kernel,
        in_specs=[pl.BlockSpec(memory_space=pltpu.VMEM)] * 2,
        out_specs=pl.BlockSpec(memory_space=pltpu.VMEM),
        out_shape=jax.ShapeDtypeStruct((groups, rows, lanes), BF16),
        compiler_params=params(),
        name="chunk_sum",
    )(got, gate)


def unpack_kernel(got, keys_out, values_out, gate_out):
    groups, rows, _ = got.shape
    width = keys_out.shape[1]
    half = groups // 2
    keys_out[...] = got[:half, :, :width].reshape(half * rows, width)
    values_out[...] = got[half:, :, :width].reshape(half * rows, width)
    for i in range(gate_out.shape[0] // rows):
        at = width + 128 * i
        gate_out[i * rows : (i + 1) * rows, :] = jnp.sum(
            got[:, :, at : at + 128].astype(F32), axis=0
        )


def unpack_call(got, width, gate_rows):
    groups, rows, _ = got.shape
    text = jax.ShapeDtypeStruct((groups // 2 * rows, width), BF16)
    return pl.pallas_call(
        unpack_kernel,
        in_specs=[pl.BlockSpec(memory_space=pltpu.VMEM)],
        out_specs=[pl.BlockSpec(memory_space=pltpu.VMEM)] * 3,
        out_shape=[text, text, jax.ShapeDtypeStruct((gate_rows, 128), F32)],
        compiler_params=params(),
        name="unpack",
    )(got)


def shift(array, axis, by, wrap=False):
    length = lax.axis_size(axis)
    pairs = [(i, (i + by) % length) for i in range(length) if wrap or 0 <= i + by < length]
    return lax.ppermute(array, axis, pairs)


def swap(array, axis, bit):
    length = lax.axis_size(axis)
    return lax.ppermute(array, axis, [(i, i ^ bit) for i in range(length)])


def in_hbm(*arrays):
    return [pltpu.with_memory_space_constraint(a, pltpu.HBM) for a in arrays]


def on_device(
    query_in,
    key_in,
    value_in,
    text_keys,
    text_values,
    text_mask,
    window_reach,
    tile_map,
    out_weight,
    gate_scale,
    grad_out,
):
    _, width = query_in.shape
    seq_count = lax.axis_size(SEQ)
    row, col = lax.axis_index("z"), lax.axis_index(COL)
    coords = lax.dynamic_slice(tile_map, (lax.axis_index(SEQ), 0), (1, 3))[0]
    counts = jnp.array(
        [lax.axis_size("z"), lax.axis_size(COL)], jnp.int32
    )
    info = jnp.concatenate(
        [
            jnp.stack([row, col]).astype(jnp.int32),
            counts,
            coords,
            jnp.zeros((1,), jnp.int32),
            window_reach.reshape(-1),
            jnp.zeros((8 - window_reach.size,), jnp.int32),
            jnp.array([lax.axis_size("x"), lax.axis_size("yhi")], jnp.int32),
            jnp.stack([lax.axis_index("yhi"), lax.axis_index("x")]).astype(jnp.int32),
        ]
    )
    bias = jnp.where(text_mask == 1, 0.0, NEG).astype(F32)[:, None]

    query_in, key_in, value_in = in_hbm(query_in, key_in, value_in)
    text_keys, text_values = in_hbm(text_keys, text_values)

    g_y = swap(grad_out, "yhi", 1)
    g_r = shift(grad_out, "x", 1, True)
    g_l = shift(grad_out, "x", -1, True)

    q, kv, cos, sin = rotate_call(info, query_in, key_in, value_in)

    kv_up, kv_down = shift(kv, "z", 1), shift(kv, "z", -1)
    g_far = shift(g_l, "x", -1, True)
    gy_r = shift(g_y, "x", 1, True)
    gy_l = shift(g_y, "x", -1, True)
    stack = stack_call(kv_up, kv, kv_down)
    kv_left, kv_right = shift(stack, COL, 1), shift(stack, COL, -1)
    gy_far = shift(gy_r, "x", 1, True)

    partial = fwd_near_call(info, q, kv, kv_up, kv_down, text_keys, text_values, bias)
    ot, lse = fwd_side_call(info, q, kv_left, kv_right, *partial)

    gate = gate_scale.reshape(1, -1)
    steps = ((False, 0), (False, -1), (False, 1), (False, 2))
    carried = proj_call(steps, info, out_weight, gate, ot, [grad_out, g_r, g_l, g_far])
    steps = ((True, 0), (True, -1), (True, 1), (True, 2))
    dot, delta, gate_terms = proj_call(
        steps, info, out_weight, gate, ot, [g_y, gy_r, gy_l, gy_far], carried
    )

    common = (info, q, dot, lse, delta)
    left, right, text_part, dq = bwd_side_call(
        common, text_keys, text_values, bias, kv_left, kv_right
    )
    back_left = shift(left, COL, -1)
    back_right = shift(right, COL, 1)
    got = lax.all_to_all(
        text_part.reshape(seq_count, -1, width), SEQ, 0, 0, tiled=True
    )
    up, own, down, grad_query = bwd_near_call(common, dq, cos, sin, kv_up, kv, kv_down)
    for axis in ("x", "yhi"):
        bit = 1
        while bit < lax.axis_size(axis):
            gate_terms = gate_terms + swap(gate_terms, axis, bit)
            bit *= 2

    up, down = pair_sum_call(up, down, back_left, back_right)
    up = shift(up, "z", -1)
    down = shift(down, "z", 1)

    chunk = chunk_sum_call(got, gate_terms)
    summed = lax.all_to_all(chunk, SEQ, 0, 0, tiled=True)
    grad_text_keys, grad_text_values, grad_gate = unpack_call(
        summed, width, out_weight.shape[1] // 128
    )
    grad_key, grad_value = finish_call(own, back_left, back_right, up, down, cos, sin)
    return (
        grad_query,
        grad_key,
        grad_value,
        grad_text_keys,
        grad_text_values,
        grad_gate.reshape(-1),
    )


def solution(mesh):
    fine = Mesh(mesh.devices.reshape(SIZES), (*SEQ, *HEAD))
    head = P(SEQ, HEAD)
    placed = (
        head,
        head,
        head,
        P(None, HEAD),
        P(None, HEAD),
        P(),
        P(HEAD, None),
        P(),
        P(HEAD, None),
        P(),
        head,
    )

    return jax.shard_map(
        on_device,
        mesh=fine,
        in_specs=placed,
        out_specs=(head, head, head, P(None, HEAD), P(None, HEAD), P()),
        check_vma=False,
    )


SIZES = (8, 4, 2, 2, 4)
```

profile of v0, /device:TPU:1, one launch (start us, length us, event | category | flops | bytes accessed | tf_op | source)
XLA Modules:
  0.0 193.1 jit_solution(16441192242589585773)
XLA Ops:
  0.6 0.0 copy-start
  0.7 0.8 reshape.24
  1.4 0.2 dynamic-slice_reduce_fusion
  1.6 1.3 concatenate.3.info
  2.9 2.6 %rot.1 = (bf16[384,256]{1,0:T(8,128)(2,1)}, bf16[2,384,256]{2,1,0:T(8,128)(2,1)}, f32[384,128]{1,0:T(8,128)}, f32[384,128]{1,0:T(8,128)}) custom-call(s32[20]{0:T(128)} %concatenate.3.info, f32[8,128]{1,0:T(8,128)} %constant.46.clone.freq, bf16[384,256]{1,0:T(8,128)(2,1)} %q.1, bf16[384,256]{1,0:T(8,128)(2,1)} %k.1, bf16[384,256]{1,0:T(8,128)(2,1)} %v.1), custom_call_target="tpu_custom_call" | custom-call | tf_op jit(solution)/shard_map/rot/pallas_call | solution.py:118
  5.4 5.0 %collective-permute-start = (bf16[2,384,256]{2,1,0:T(8,128)(2,1)}, bf16[2,384,256]{2,1,0:T(8,128)(2,1)S(1)}, u32[]{:S(2)}, u32[]{:S(2)}) collective-permute-start(bf16[2,384,256]{2,1,0:T(8,128)(2,1)} %get-tuple-element.36.own), channel_id=1, source_target_pairs={{0,64},{64,128},{128,192},{192,256},{256,320},{320,384},{384,448},... | collective-permute-start | bytes 1179656 | tf_op jit(solution)/shard_map/ppermute | solution.py:564
  10.4 1.3 collective-permute-start.1
  11.7 4.4 %collective-permute-done.up = bf16[2,384,256]{2,1,0:T(8,128)(2,1)S(1)} collective-permute-done((bf16[2,384,256]{2,1,0:T(8,128)(2,1)}, bf16[2,384,256]{2,1,0:T(8,128)(2,1)S(1)}, u32[]{:S(2)}, u32[]{:S(2)}) %collective-permute-start) | collective-permute-done | bytes 393248 | tf_op jit(solution)/shard_map/ppermute | solution.py:564
  16.1 5.0 %collective-permute-done.1.down = bf16[2,384,256]{2,1,0:T(8,128)(2,1)S(1)} collective-permute-done((bf16[2,384,256]{2,1,0:T(8,128)(2,1)}, bf16[2,384,256]{2,1,0:T(8,128)(2,1)S(1)}, u32[]{:S(2)}, u32[]{:S(2)}) %collective-permute-start.1) | collective-permute-done | bytes 393248 | tf_op jit(solution)/shard_map/ppermute | solution.py:564
  21.1 0.8 copy-done.4
  21.9 2.2 %stack.17 = bf16[3,2,384,256]{3,2,1,0:T(8,128)(2,1)} custom-call(bf16[2,384,256]{2,1,0:T(8,128)(2,1)} %copy-done.3, bf16[2,384,256]{2,1,0:T(8,128)(2,1)} %get-tuple-element.36.own, bf16[2,384,256]{2,1,0:T(8,128)(2,1)} %copy-done.4), custom_call_target="tpu_custom_call" | custom-call | tf_op jit(solution)/shard_map/stack/pallas_call | solution.py:268
  24.1 6.6 %collective-permute-start.2 = (bf16[3,2,384,256]{3,2,1,0:T(8,128)(2,1)}, bf16[3,2,384,256]{3,2,1,0:T(8,128)(2,1)S(1)}, u32[]{:S(2)}, u32[]{:S(2)}) collective-permute-start(bf16[3,2,384,256]{3,2,1,0:T(8,128)(2,1)} %stack.17), channel_id=1, source_target_pairs={{0,8},{8,16},{16,24},{24,32},{32,40},{40,48},{48,56},{1,9},{9,17},... | collective-permute-start | bytes 3538952 | tf_op jit(solution)/shard_map/ppermute | solution.py:564
  30.7 1.9 collective-permute-start.3
  32.7 6.6 %collective-permute-start.4 = (bf16[384,384]{1,0:T(8,128)(2,1)}, bf16[384,384]{1,0:T(8,128)(2,1)}, u32[]{:S(2)}, u32[]{:S(2)}) collective-permute-start(bf16[384,384]{1,0:T(8,128)(2,1)} %refs_0_.1), channel_id=1, source_target_pairs={{0,4},{4,0},{1,5},{5,1},{2,6},{6,2},{3,7},{7,3},{8,12},{12,8},{9,1... | collective-permute-start | bytes 884744 | tf_op jit(solution)/shard_map/ppermute | solution.py:569
  39.2 4.4 %collective-permute-start.9 = (bf16[384,384]{1,0:T(8,128)(2,1)}, bf16[384,384]{1,0:T(8,128)(2,1)S(1)}, u32[]{:S(2)}, u32[]{:S(2)}) collective-permute-start(bf16[384,384]{1,0:T(8,128)(2,1)} %refs_0_.1), channel_id=1, source_target_pairs={{0,3},{1,0},{2,1},{3,2},{4,7},{5,4},{6,5},{7,6},{8,11},{9,8},{10,9... | collective-permute-start | bytes 884744 | tf_op jit(solution)/shard_map/ppermute | solution.py:564
  43.6 15.2 %collective-permute-done.4.refs_0_ = bf16[384,384]{1,0:T(8,128)(2,1)} collective-permute-done((bf16[384,384]{1,0:T(8,128)(2,1)}, bf16[384,384]{1,0:T(8,128)(2,1)}, u32[]{:S(2)}, u32[]{:S(2)}) %collective-permute-start.4) | collective-permute-done | bytes 294944 | tf_op jit(solution)/shard_map/ppermute | solution.py:569
  58.8 3.1 %collective-permute-start.5 = (bf16[384,384]{1,0:T(8,128)(2,1)}, bf16[384,384]{1,0:T(8,128)(2,1)}, u32[]{:S(2)}, u32[]{:S(2)}) collective-permute-start(bf16[384,384]{1,0:T(8,128)(2,1)} %collective-permute-done.4.refs_0_), channel_id=1, source_target_pairs={{0,1},{1,2},{2,3},{3,0},{4,5},{5,6},{6,7},{7,4},{8,9},{9,10},{10,1... | collective-permute-start | bytes 884744 | tf_op jit(solution)/shard_map/ppermute | solution.py:564
  62.0 3.1 %collective-permute-start.8 = (bf16[384,384]{1,0:T(8,128)(2,1)}, bf16[384,384]{1,0:T(8,128)(2,1)S(1)}, u32[]{:S(2)}, u32[]{:S(2)}) collective-permute-start(bf16[384,384]{1,0:T(8,128)(2,1)} %refs_0_.1), channel_id=1, source_target_pairs={{0,1},{1,2},{2,3},{3,0},{4,5},{5,6},{6,7},{7,4},{8,9},{9,10},{10,1... | collective-permute-start | bytes 884744 | tf_op jit(solution)/shard_map/ppermute | solution.py:564
  65.1 0.0 collective-permute-done.9.refs_2_
  65.1 3.4 %collective-permute-start.6 = (bf16[384,384]{1,0:T(8,128)(2,1)}, bf16[384,384]{1,0:T(8,128)(2,1)}, u32[]{:S(2)}, u32[]{:S(2)}) collective-permute-start(bf16[384,384]{1,0:T(8,128)(2,1)} %collective-permute-done.4.refs_0_), channel_id=1, source_target_pairs={{0,3},{1,0},{2,1},{3,2},{4,7},{5,4},{6,5},{7,6},{8,11},{9,8},{10,9... | collective-permute-start | bytes 884744 | tf_op jit(solution)/shard_map/ppermute | solution.py:564
  68.5 0.0 collective-permute-done.5.refs_1_
  68.5 4.3 %collective-permute-start.10 = (bf16[384,384]{1,0:T(8,128)(2,1)S(1)}, bf16[384,384]{1,0:T(8,128)(2,1)S(1)}, u32[]{:S(2)}, u32[]{:S(2)}) collective-permute-start(bf16[384,384]{1,0:T(8,128)(2,1)S(1)} %collective-permute-done.9.refs_2_), channel_id=1, source_target_pairs={{0,3},{1,0},{2,1},{3,2},{4,7},{5,4},{6,5},{7,6},{8,11},{9,8},{10,9... | collective-permute-start | bytes 884744 | tf_op jit(solution)/shard_map/ppermute | solution.py:564
  72.8 0.0 collective-permute-done.2.left
  72.8 1.0 copy-done.10
  73.8 1.9 collective-permute-start.7
  75.7 0.8 copy.20.bias
  76.5 4.5 %fwd_near.1 = (f32[256,384]{1,0:T(8,128)}, f32[16,384]{1,0:T(8,128)}, f32[16,384]{1,0:T(8,128)}) custom-call(s32[20]{0:T(128)} %concatenate.3.info, bf16[384,256]{1,0:T(8,128)(2,1)} %get-tuple-element.35.q, bf16[2,384,256]{2,1,0:T(8,128)(2,1)} %get-tuple-element.36.own, bf16[2,384,256]{2,1,0:T(8,128)(2,1)} %copy-done.3, bf16[2,384,256]{2,1,0:T(8,128)(2,1)} %copy-done.4, ...), custom_call_target="tpu_custom_call" | custom-call | flops 553648128 | bytes 1441792 | tf_op jit(solution)/shard_map/fwd_near/pallas_call | solution.py:210
  81.0 0.0 collective-permute-done.3.right
  81.0 3.7 %fwd_side.1 = (bf16[256,384]{1,0:T(8,128)(2,1)}, f32[16,384]{1,0:T(8,128)}) custom-call(s32[20]{0:T(128)} %concatenate.3.info, bf16[384,256]{1,0:T(8,128)(2,1)} %get-tuple-element.35.q, bf16[3,2,384,256]{3,2,1,0:T(8,128)(2,1)} %copy-done.10, bf16[3,2,384,256]{3,2,1,0:T(8,128)(2,1)} %collective-permute-done.3.right, f32[256,384]{1,0:T(8,128)} %get-tuple-element.37.acc_in, ...), custom_call_target="tpu_custom_call" | custom-call | flops 905969664 | bytes 2359296 | tf_op jit(solution)/shard_map/fwd_side/pallas_call | solution.py:230
  84.8 0.0 collective-permute-done.8.refs_1_
  84.8 0.0 collective-permute-done.10.refs_3_
  84.8 0.7 copy-done.6
  85.5 0.1 copy-done.7
  85.6 3.6 %proj.2 = (f32[256,384]{1,0:T(8,128)}, f32[24,128]{1,0:T(8,128)}) custom-call(s32[20]{0:T(128)} %concatenate.3.info, bf16[256,3072]{1,0:T(8,128)(2,1)} %w.3, f32[1,3072]{1,0:T(1,128)} %bitcast.9, bf16[256,384]{1,0:T(8,128)(2,1)} %get-tuple-element.40.ot, bf16[384,384]{1,0:T(8,128)(2,1)} %refs_0_.1, bf16[384,384]{1,0:T(8,128)(2,1)} %copy-done.6, ...), custom_call_target="tpu_custom_call" | custom-call | flops 603979776 | bytes 2752512 | tf_op jit(solution)/shard_map/proj/pallas_call | solution.py:335
  89.2 0.0 collective-permute-done.6.refs_2_
  89.2 0.0 collective-permute-done.7.refs_3_
  89.2 3.7 %proj.3 = (bf16[256,384]{1,0:T(8,128)(2,1)}, f32[16,384]{1,0:T(8,128)}, f32[24,128]{1,0:T(8,128)}) custom-call(s32[20]{0:T(128)} %concatenate.3.info, bf16[256,3072]{1,0:T(8,128)(2,1)} %w.3, f32[1,3072]{1,0:T(1,128)} %bitcast.10, bf16[256,384]{1,0:T(8,128)(2,1)} %get-tuple-element.40.ot, bf16[384,384]{1,0:T(8,128)(2,1)} %collective-permute-done.4.refs_0_, ...), custom_call_target="tpu_custom_call" | custom-call | flops 603979776 | bytes 2752512 | tf_op jit(solution)/shard_map/proj/pallas_call | solution.py:335
  93.0 5.2 %bwd_side.1 = (bf16[3,2,384,256]{3,2,1,0:T(8,128)(2,1)}, bf16[3,2,384,256]{3,2,1,0:T(8,128)(2,1)}, bf16[2,256,256]{2,1,0:T(8,128)(2,1)}, f32[256,384]{1,0:T(8,128)}) custom-call(s32[20]{0:T(128)} %concatenate.3.info, bf16[384,256]{1,0:T(8,128)(2,1)} %get-tuple-element.35.q, bf16[256,384]{1,0:T(8,128)(2,1)} %get-tuple-element.43.dot, ...), custom_call_target="tpu_custom_call" | custom-call | flops 2516582400 | bytes 5242880 | tf_op jit(solution)/shard_map/bwd_side/pallas_call | solution.py:428
  98.2 20.7 %all-to-all-start = ((bf16[64,8,256]{2,1,0:T(8,128)(2,1)}), bf16[64,8,256]{2,1,0:T(8,128)(2,1)S(1)}, u32[]{:S(2)}, u32[]{:S(2)}) async-start(bf16[64,8,256]{2,1,0:T(8,128)(2,1)} %bitcast.8), calls=%async_computation | async-start | bytes 524288 | tf_op jit(solution)/shard_map/all_to_all | solution.py:644
  118.8 2.4 %collective-permute-start.11 = (bf16[3,2,384,256]{3,2,1,0:T(8,128)(2,1)}, bf16[3,2,384,256]{3,2,1,0:T(8,128)(2,1)}, u32[]{:S(2)}, u32[]{:S(2)}) collective-permute-start(bf16[3,2,384,256]{3,2,1,0:T(8,128)(2,1)} %get-tuple-element.51), channel_id=1, source_target_pairs={{8,0},{16,8},{24,16},{32,24},{40,32},{48,40},{56,48},{9,1},{17,9},... | collective-permute-start | bytes 3538952 | tf_op jit(solution)/shard_map/ppermute | solution.py:564
  121.2 3.2 %collective-permute-start.12 = (bf16[3,2,384,256]{3,2,1,0:T(8,128)(2,1)}, bf16[3,2,384,256]{3,2,1,0:T(8,128)(2,1)}, u32[]{:S(2)}, u32[]{:S(2)}) collective-permute-start(bf16[3,2,384,256]{3,2,1,0:T(8,128)(2,1)} %get-tuple-element.52), channel_id=1, source_target_pairs={{0,8},{8,16},{16,24},{24,32},{32,40},{40,48},{48,56},{1,9},{9,17},... | collective-permute-start | bytes 3538952 | tf_op jit(solution)/shard_map/ppermute | solution.py:564
  124.4 5.6 %collective-permute-start.15 = (f32[24,128]{1,0:T(8,128)S(1)}, f32[24,128]{1,0:T(8,128)S(1)}, u32[]{:S(2)}, u32[]{:S(2)}) collective-permute-start(f32[24,128]{1,0:T(8,128)S(1)} %copy-done.8), channel_id=1, source_target_pairs={{0,1},{1,0},{2,3},{3,2},{4,5},{5,4},{6,7},{7,6},{8,9},{9,8},{10,11... | collective-permute-start | bytes 36872 | tf_op jit(solution)/shard_map/ppermute | solution.py:569
  130.0 1.4 collective-permute-done.15
  131.4 5.5 %collective-permute-start.16 = (f32[24,128]{1,0:T(8,128)S(1)}, f32[24,128]{1,0:T(8,128)S(1)}, u32[]{:S(2)}, u32[]{:S(2)}) collective-permute-start(f32[24,128]{1,0:T(8,128)S(1)} %add.22), channel_id=1, source_target_pairs={{0,2},{1,3},{2,0},{3,1},{4,6},{5,7},{6,4},{7,5},{8,10},{9,11},{10,... | collective-permute-start | bytes 36872 | tf_op jit(solution)/shard_map/ppermute | solution.py:569
  136.9 1.1 collective-permute-done.16
  137.9 1.9 collective-permute-start.17
  139.8 6.4 %collective-permute-done.17 = f32[24,128]{1,0:T(8,128)S(1)} collective-permute-done((f32[24,128]{1,0:T(8,128)S(1)}, f32[24,128]{1,0:T(8,128)S(1)}, u32[]{:S(2)}, u32[]{:S(2)}) %collective-permute-start.17) | collective-permute-done | bytes 12320 | tf_op jit(solution)/shard_map/ppermute | solution.py:569
  146.3 0.6 add.24.gate
  146.9 0.0 all-to-all-done.got
  146.9 0.7 copy-done.2
  147.6 1.9 %chunk_sum.1 = bf16[64,8,640]{2,1,0:T(8,128)(2,1)} custom-call(bf16[64,8,256]{2,1,0:T(8,128)(2,1)} %copy-done.2, f32[24,128]{1,0:T(8,128)} %add.24.gate), custom_call_target="tpu_custom_call" | custom-call | tf_op jit(solution)/shard_map/chunk_sum/pallas_call | solution.py:525
  149.5 13.3 %all-to-all-start.1 = ((bf16[64,8,640]{2,1,0:T(8,128)(2,1)}), bf16[64,8,640]{2,1,0:T(8,128)(2,1)S(1)}, u32[]{:S(2)}, u32[]{:S(2)}) async-start(bf16[64,8,640]{2,1,0:T(8,128)(2,1)} %chunk_sum.1), calls=%async_computation.1 | async-start | bytes 1310720 | tf_op jit(solution)/shard_map/all_to_all | solution.py:659
  162.8 4.8 %bwd_near.1 = (f32[2,384,256]{2,1,0:T(8,128)}, f32[2,384,256]{2,1,0:T(8,128)}, f32[2,384,256]{2,1,0:T(8,128)}, bf16[384,256]{1,0:T(8,128)(2,1)}) custom-call(s32[20]{0:T(128)} %concatenate.3.info, bf16[384,256]{1,0:T(8,128)(2,1)} %get-tuple-element.35.q, bf16[256,384]{1,0:T(8,128)(2,1)} %get-tuple-element.43.dot, f32[16,384]{1,0:T(8,128)} %get-tuple-element.44.lse, ...), custom_call_target="tpu_custom_call" | custom-call | flops 1132462080 | bytes 2359296 | tf_op jit(solution)/shard_map/bwd_near/pallas_call | solution.py:452
  167.6 0.0 collective-permute-done.11.left
  167.6 0.0 collective-permute-done.12.right
  167.6 2.9 %pair_sum.1 = (bf16[2,384,256]{2,1,0:T(8,128)(2,1)}, bf16[2,384,256]{2,1,0:T(8,128)(2,1)}) custom-call(f32[2,384,256]{2,1,0:T(8,128)} %get-tuple-element.53.up, f32[2,384,256]{2,1,0:T(8,128)} %get-tuple-element.54.down, bf16[3,2,384,256]{3,2,1,0:T(8,128)(2,1)} %collective-permute-done.11.left, bf16[3,2,384,256]{3,2,1,0:T(8,128)(2,1)} %collective-permute-done.12.right), custom_call_target="tpu_custom_call" | custom-call | tf_op jit(solution)/shard_map/pair_sum/pallas_call | solution.py:475
  170.5 1.3 collective-permute-start.13
  171.8 5.2 %collective-permute-start.14 = (bf16[2,384,256]{2,1,0:T(8,128)(2,1)}, bf16[2,384,256]{2,1,0:T(8,128)(2,1)}, u32[]{:S(2)}, u32[]{:S(2)}) collective-permute-start(bf16[2,384,256]{2,1,0:T(8,128)(2,1)} %get-tuple-element.56), channel_id=1, source_target_pairs={{0,64},{64,128},{128,192},{192,256},{256,320},{320,384},{384,448},... | collective-permute-start | bytes 1179656 | tf_op jit(solution)/shard_map/ppermute | solution.py:564
  177.0 10.4 %collective-permute-done.13.up = bf16[2,384,256]{2,1,0:T(8,128)(2,1)} collective-permute-done((bf16[2,384,256]{2,1,0:T(8,128)(2,1)}, bf16[2,384,256]{2,1,0:T(8,128)(2,1)}, u32[]{:S(2)}, u32[]{:S(2)}) %collective-permute-start.13) | collective-permute-done | bytes 393248 | tf_op jit(solution)/shard_map/ppermute | solution.py:564
  187.4 0.0 collective-permute-done.14.down
  187.4 3.0 %finish.1 = (bf16[384,256]{1,0:T(8,128)(2,1)}, bf16[384,256]{1,0:T(8,128)(2,1)}) custom-call(f32[2,384,256]{2,1,0:T(8,128)} %get-tuple-element.50.own, bf16[3,2,384,256]{3,2,1,0:T(8,128)(2,1)} %collective-permute-done.11.left, bf16[3,2,384,256]{3,2,1,0:T(8,128)(2,1)} %collective-permute-done.12.right, bf16[2,384,256]{2,1,0:T(8,128)(2,1)} %collective-permute-done.13.up, ...), custom_call_target="tpu_custom_call" | custom-call | tf_op jit(solution)/shard_map/finish/pallas_call | solution.py:501
  190.4 0.0 all-to-all-done.1.got
  190.4 0.8 copy-done.1
  191.3 1.8 unpack.1
  (20 shorter events, 0.0 us)
Async XLA Ops:
  0.6 0.8 copy-start
  5.4 70.3 %copy-start.9 = (s32[256]{0:T(256)S(1)}, s32[256]{0:T(256)}, u32[]{:S(2)}) copy-start(s32[256]{0:T(256)} %param.19) | copy-start | bytes 3076
  5.4 10.7 %collective-permute-start = (bf16[2,384,256]{2,1,0:T(8,128)(2,1)}, bf16[2,384,256]{2,1,0:T(8,128)(2,1)S(1)}, u32[]{:S(2)}, u32[]{:S(2)}) collective-permute-start(bf16[2,384,256]{2,1,0:T(8,128)(2,1)} %get-tuple-element.36.own), channel_id=1, source_target_pairs={{0,64},{64,128},{128,192},{192,256},{256,320},{320,384},{384,448},... | collective-permute-start | bytes 1179656 | tf_op jit(solution)/shard_map/ppermute | solution.py:564
  10.4 10.7 %collective-permute-start.1 = (bf16[2,384,256]{2,1,0:T(8,128)(2,1)}, bf16[2,384,256]{2,1,0:T(8,128)(2,1)S(1)}, u32[]{:S(2)}, u32[]{:S(2)}) collective-permute-start(bf16[2,384,256]{2,1,0:T(8,128)(2,1)} %get-tuple-element.36.own), channel_id=1, source_target_pairs={{64,0},{128,64},{192,128},{256,192},{320,256},{384,320},{448,384},... | collective-permute-start | bytes 1179656 | tf_op jit(solution)/shard_map/ppermute | solution.py:564
  16.1 5.0 %copy-start.3 = (bf16[2,384,256]{2,1,0:T(8,128)(2,1)}, bf16[2,384,256]{2,1,0:T(8,128)(2,1)S(1)}, u32[]{:S(2)}) copy-start(bf16[2,384,256]{2,1,0:T(8,128)(2,1)S(1)} %collective-permute-done.up) | copy-start | bytes 1179652
  21.1 0.8 copy-start.4
  24.1 48.7 %collective-permute-start.2 = (bf16[3,2,384,256]{3,2,1,0:T(8,128)(2,1)}, bf16[3,2,384,256]{3,2,1,0:T(8,128)(2,1)S(1)}, u32[]{:S(2)}, u32[]{:S(2)}) collective-permute-start(bf16[3,2,384,256]{3,2,1,0:T(8,128)(2,1)} %stack.17), channel_id=1, source_target_pairs={{0,8},{8,16},{16,24},{24,32},{32,40},{40,48},{48,56},{1,9},{9,17},... | collective-permute-start | bytes 3538952 | tf_op jit(solution)/shard_map/ppermute | solution.py:564
  30.7 50.3 %collective-permute-start.3 = (bf16[3,2,384,256]{3,2,1,0:T(8,128)(2,1)}, bf16[3,2,384,256]{3,2,1,0:T(8,128)(2,1)}, u32[]{:S(2)}, u32[]{:S(2)}) collective-permute-start(bf16[3,2,384,256]{3,2,1,0:T(8,128)(2,1)} %stack.17), channel_id=1, source_target_pairs={{8,0},{16,8},{24,16},{32,24},{40,32},{48,40},{56,48},{9,1},{17,9},... | collective-permute-start | bytes 3538952 | tf_op jit(solution)/shard_map/ppermute | solution.py:564
  32.7 26.2 %collective-permute-start.4 = (bf16[384,384]{1,0:T(8,128)(2,1)}, bf16[384,384]{1,0:T(8,128)(2,1)}, u32[]{:S(2)}, u32[]{:S(2)}) collective-permute-start(bf16[384,384]{1,0:T(8,128)(2,1)} %refs_0_.1), channel_id=1, source_target_pairs={{0,4},{4,0},{1,5},{5,1},{2,6},{6,2},{3,7},{7,3},{8,12},{12,8},{9,1... | collective-permute-start | bytes 884744 | tf_op jit(solution)/shard_map/ppermute | solution.py:569
  39.2 25.9 %collective-permute-start.9 = (bf16[384,384]{1,0:T(8,128)(2,1)}, bf16[384,384]{1,0:T(8,128)(2,1)S(1)}, u32[]{:S(2)}, u32[]{:S(2)}) collective-permute-start(bf16[384,384]{1,0:T(8,128)(2,1)} %refs_0_.1), channel_id=1, source_target_pairs={{0,3},{1,0},{2,1},{3,2},{4,7},{5,4},{6,5},{7,6},{8,11},{9,8},{10,9... | collective-permute-start | bytes 884744 | tf_op jit(solution)/shard_map/ppermute | solution.py:564
  58.8 9.7 %collective-permute-start.5 = (bf16[384,384]{1,0:T(8,128)(2,1)}, bf16[384,384]{1,0:T(8,128)(2,1)}, u32[]{:S(2)}, u32[]{:S(2)}) collective-permute-start(bf16[384,384]{1,0:T(8,128)(2,1)} %collective-permute-done.4.refs_0_), channel_id=1, source_target_pairs={{0,1},{1,2},{2,3},{3,0},{4,5},{5,6},{6,7},{7,4},{8,9},{9,10},{10,1... | collective-permute-start | bytes 884744 | tf_op jit(solution)/shard_map/ppermute | solution.py:564
  62.0 22.8 %collective-permute-start.8 = (bf16[384,384]{1,0:T(8,128)(2,1)}, bf16[384,384]{1,0:T(8,128)(2,1)S(1)}, u32[]{:S(2)}, u32[]{:S(2)}) collective-permute-start(bf16[384,384]{1,0:T(8,128)(2,1)} %refs_0_.1), channel_id=1, source_target_pairs={{0,1},{1,2},{2,3},{3,0},{4,5},{5,6},{6,7},{7,4},{8,9},{9,10},{10,1... | collective-permute-start | bytes 884744 | tf_op jit(solution)/shard_map/ppermute | solution.py:564
  65.1 19.7 %copy-start.5 = (bf16[384,384]{1,0:T(8,128)(2,1)}, bf16[384,384]{1,0:T(8,128)(2,1)S(1)}, u32[]{:S(2)}) copy-start(bf16[384,384]{1,0:T(8,128)(2,1)S(1)} %collective-permute-done.9.refs_2_) | copy-start | bytes 884740
  65.1 24.1 %collective-permute-start.6 = (bf16[384,384]{1,0:T(8,128)(2,1)}, bf16[384,384]{1,0:T(8,128)(2,1)}, u32[]{:S(2)}, u32[]{:S(2)}) collective-permute-start(bf16[384,384]{1,0:T(8,128)(2,1)} %collective-permute-done.4.refs_0_), channel_id=1, source_target_pairs={{0,3},{1,0},{2,1},{3,2},{4,7},{5,4},{6,5},{7,6},{8,11},{9,8},{10,9... | collective-permute-start | bytes 884744 | tf_op jit(solution)/shard_map/ppermute | solution.py:564
  68.5 16.3 %collective-permute-start.10 = (bf16[384,384]{1,0:T(8,128)(2,1)S(1)}, bf16[384,384]{1,0:T(8,128)(2,1)S(1)}, u32[]{:S(2)}, u32[]{:S(2)}) collective-permute-start(bf16[384,384]{1,0:T(8,128)(2,1)S(1)} %collective-permute-done.9.refs_2_), channel_id=1, source_target_pairs={{0,3},{1,0},{2,1},{3,2},{4,7},{5,4},{6,5},{7,6},{8,11},{9,8},{10,9... | collective-permute-start | bytes 884744 | tf_op jit(solution)/shard_map/ppermute | solution.py:564
  72.8 1.0 copy-start.10
  73.8 15.4 %collective-permute-start.7 = (bf16[384,384]{1,0:T(8,128)(2,1)}, bf16[384,384]{1,0:T(8,128)(2,1)}, u32[]{:S(2)}, u32[]{:S(2)}) collective-permute-start(bf16[384,384]{1,0:T(8,128)(2,1)} %collective-permute-done.5.refs_1_), channel_id=1, source_target_pairs={{0,1},{1,2},{2,3},{3,0},{4,5},{5,6},{6,7},{7,4},{8,9},{9,10},{10,1... | collective-permute-start | bytes 884744 | tf_op jit(solution)/shard_map/ppermute | solution.py:564
  84.8 0.7 copy-start.6
  84.8 0.8 copy-start.7
  93.0 31.5 %copy-start.8 = (f32[24,128]{1,0:T(8,128)S(1)}, f32[24,128]{1,0:T(8,128)}, u32[]{:S(2)}) copy-start(f32[24,128]{1,0:T(8,128)} %get-tuple-element.60) | copy-start | bytes 36868
  98.2 48.7 %all-to-all-start = ((bf16[64,8,256]{2,1,0:T(8,128)(2,1)}), bf16[64,8,256]{2,1,0:T(8,128)(2,1)S(1)}, u32[]{:S(2)}, u32[]{:S(2)}) async-start(bf16[64,8,256]{2,1,0:T(8,128)(2,1)} %bitcast.8), calls=%async_computation | async-start | bytes 524288 | tf_op jit(solution)/shard_map/all_to_all | solution.py:644
  118.8 48.8 %collective-permute-start.11 = (bf16[3,2,384,256]{3,2,1,0:T(8,128)(2,1)}, bf16[3,2,384,256]{3,2,1,0:T(8,128)(2,1)}, u32[]{:S(2)}, u32[]{:S(2)}) collective-permute-start(bf16[3,2,384,256]{3,2,1,0:T(8,128)(2,1)} %get-tuple-element.51), channel_id=1, source_target_pairs={{8,0},{16,8},{24,16},{32,24},{40,32},{48,40},{56,48},{9,1},{17,9},... | collective-permute-start | bytes 3538952 | tf_op jit(solution)/shard_map/ppermute | solution.py:564
  121.2 46.4 %collective-permute-start.12 = (bf16[3,2,384,256]{3,2,1,0:T(8,128)(2,1)}, bf16[3,2,384,256]{3,2,1,0:T(8,128)(2,1)}, u32[]{:S(2)}, u32[]{:S(2)}) collective-permute-start(bf16[3,2,384,256]{3,2,1,0:T(8,128)(2,1)} %get-tuple-element.52), channel_id=1, source_target_pairs={{0,8},{8,16},{16,24},{24,32},{32,40},{40,48},{48,56},{1,9},{9,17},... | collective-permute-start | bytes 3538952 | tf_op jit(solution)/shard_map/ppermute | solution.py:564
  124.4 7.0 %collective-permute-start.15 = (f32[24,128]{1,0:T(8,128)S(1)}, f32[24,128]{1,0:T(8,128)S(1)}, u32[]{:S(2)}, u32[]{:S(2)}) collective-permute-start(f32[24,128]{1,0:T(8,128)S(1)} %copy-done.8), channel_id=1, source_target_pairs={{0,1},{1,0},{2,3},{3,2},{4,5},{5,4},{6,7},{7,6},{8,9},{9,8},{10,11... | collective-permute-start | bytes 36872 | tf_op jit(solution)/shard_map/ppermute | solution.py:569
  131.4 6.5 %collective-permute-start.16 = (f32[24,128]{1,0:T(8,128)S(1)}, f32[24,128]{1,0:T(8,128)S(1)}, u32[]{:S(2)}, u32[]{:S(2)}) collective-permute-start(f32[24,128]{1,0:T(8,128)S(1)} %add.22), channel_id=1, source_target_pairs={{0,2},{1,3},{2,0},{3,1},{4,6},{5,7},{6,4},{7,5},{8,10},{9,11},{10,... | collective-permute-start | bytes 36872 | tf_op jit(solution)/shard_map/ppermute | solution.py:569
  137.9 8.3 %collective-permute-start.17 = (f32[24,128]{1,0:T(8,128)S(1)}, f32[24,128]{1,0:T(8,128)S(1)}, u32[]{:S(2)}, u32[]{:S(2)}) collective-permute-start(f32[24,128]{1,0:T(8,128)S(1)} %add.23), channel_id=1, source_target_pairs={{0,4},{4,0},{1,5},{5,1},{2,6},{6,2},{3,7},{7,3},{8,12},{12,8},{9,1... | collective-permute-start | bytes 36872 | tf_op jit(solution)/shard_map/ppermute | solution.py:569
  146.9 0.7 copy-start.2
  149.5 40.9 %all-to-all-start.1 = ((bf16[64,8,640]{2,1,0:T(8,128)(2,1)}), bf16[64,8,640]{2,1,0:T(8,128)(2,1)S(1)}, u32[]{:S(2)}, u32[]{:S(2)}) async-start(bf16[64,8,640]{2,1,0:T(8,128)(2,1)} %chunk_sum.1), calls=%async_computation.1 | async-start | bytes 1310720 | tf_op jit(solution)/shard_map/all_to_all | solution.py:659
  170.5 16.8 %collective-permute-start.13 = (bf16[2,384,256]{2,1,0:T(8,128)(2,1)}, bf16[2,384,256]{2,1,0:T(8,128)(2,1)}, u32[]{:S(2)}, u32[]{:S(2)}) collective-permute-start(bf16[2,384,256]{2,1,0:T(8,128)(2,1)} %get-tuple-element.55), channel_id=1, source_target_pairs={{64,0},{128,64},{192,128},{256,192},{320,256},{384,320},{448,384},... | collective-permute-start | bytes 1179656 | tf_op jit(solution)/shard_map/ppermute | solution.py:564
  171.8 15.5 %collective-permute-start.14 = (bf16[2,384,256]{2,1,0:T(8,128)(2,1)}, bf16[2,384,256]{2,1,0:T(8,128)(2,1)}, u32[]{:S(2)}, u32[]{:S(2)}) collective-permute-start(bf16[2,384,256]{2,1,0:T(8,128)(2,1)} %get-tuple-element.56), channel_id=1, source_target_pairs={{0,64},{64,128},{128,192},{192,256},{256,320},{320,384},{384,448},... | collective-permute-start | bytes 1179656 | tf_op jit(solution)/shard_map/ppermute | solution.py:564
  190.4 0.9 copy-start.1
where the time goes:
time: 194 us; the launch traced here: 193 us
  starting transfers between devices  100 us (52%)
  waiting for transfers between devices  43.9 us (23%)
  Pallas kernels  40 us (21%)
  local copies, waits for them, and re-layouts  7.18 us (4%)
    ppermute x14, starting transfers between devices, shift(): return lax.ppermute(array, axis, pairs)  47 us
    ppermute x4, waiting for transfers between devices, swap(): return lax.ppermute(array, axis, [(i, i ^ bit) for i in range(length)])  24.1 us
    all_to_all x1, starting transfers between devices, on_device(): lax.all_to_all(text_part.reshape(seq_count, -1, width), SEQ, 0, 0, tiled=...  20.7 us
    ppermute x14, waiting for transfers between devices, shift(): return lax.ppermute(array, axis, pairs)  19.8 us
    ppermute x4, starting transfers between devices, swap(): return lax.ppermute(array, axis, [(i, i ^ bit) for i in range(length)])  19.5 us
    all_to_all x1, starting transfers between devices, on_device(): summed = lax.all_to_all(chunk, SEQ, 0, 0, tiled=True)  13.3 us
    pallas_call x2, Pallas kernels, proj_call(): pl.pallas_call(functools.partial(proj_kernel, steps, last), in_specs=[sme...  7.35 us
    pallas_call x1, Pallas kernels, bwd_side_call(): pl.pallas_call(bwd_side_kernel, grid=(width // HEAD_DIM,), in_specs=bwd_s...  5.19 us
  transfers between devices with their start and end apart: 20, of which 7 were waited for; matrix products, arithmetic and copies ran while one was open for 1% of the time, Pallas kernels for 13%

commit v1 on v0

--- a/solution.py
+++ b/solution.py
@@ -26,6 +26,7 @@
 BF16 = jnp.bfloat16
 NEG = -1e30
 VMEM_LIMIT = 66_000_000
+SMALL = 16_000_000
 
 
 def dot_nn(a, b):
@@ -40,9 +41,9 @@
     return lax.dot_general(a, b, (((0,), (0,)), ((), ())), preferred_element_type=F32)
 
 
-def params(*semantics):
+def params(*semantics, limit=VMEM_LIMIT):
     return pltpu.CompilerParams(
-        dimension_semantics=semantics or None, vmem_limit_bytes=VMEM_LIMIT
+        dimension_semantics=semantics or None, vmem_limit_bytes=limit
     )
 
 
@@ -73,11 +74,23 @@
     return pl.BlockSpec(memory_space=pltpu.SMEM)
 
 
-def rot_kernel(info, freq, q, k, v, q_out, kv_out, cos_out, sin_out):
+def rot_kernel(sizes, reach, tiles, freq, q, k, v, q_out, kv_out, cos_out, sin_out, info):
     tile = q.shape[0]
 
     @pl.when(pl.program_id(0) == 0)
     def _():
+        rows, ys, cores, _, _ = sizes
+        row = lax.axis_index("z")
+        col = lax.axis_index("y") * cores + lax.axis_index("core")
+        info[0] = row
+        info[1] = col
+        info[2] = rows
+        info[3] = ys * cores
+        info[4] = lax.axis_index("yhi")
+        for h in range(reach.shape[0]):
+            info[8 + 2 * h] = reach[h, 0]
+            info[9 + 2 * h] = reach[h, 1]
+        own = row * (ys * cores) + col
         frames = tile // (TILE_H * TILE_W)
         step = lax.broadcasted_iota(jnp.int32, (8, HEAD_DIM), 0)
         lane = lax.broadcasted_iota(jnp.int32, (8, HEAD_DIM), 1)
@@ -91,9 +104,9 @@
             s = jnp.sin(angle)
             return jnp.cos(angle), jnp.where(first, -s, s)
 
-        cf, sf = table(info[4] * frames)
-        cr, sr = table(info[5] * TILE_H)
-        cc, sc = table(info[6] * TILE_W)
+        cf, sf = table(tiles[0, own] * frames)
+        cr, sr = table(tiles[1, own] * TILE_H)
+        cc, sc = table(tiles[2, own] * TILE_W)
         for r in range(TILE_H):
             crr = jnp.where(lane < 72, cr[r : r + 1, :], cc)
             srr = jnp.where(lane < 72, sr[r : r + 1, :], sc)
@@ -110,25 +123,26 @@
     kv_out[1] = v[...]
 
 
-def rotate_call(info, q_in, k_in, v_in):
+def rotate_call(sizes, reach, tile_map, q_in, k_in, v_in):
     tile, width = q_in.shape
     heads = width // HEAD_DIM
     half = pl.BlockSpec((tile, HEAD_DIM), lambda h: (0, h))
     table = whole((tile, HEAD_DIM))
     return pl.pallas_call(
-        rot_kernel,
+        functools.partial(rot_kernel, sizes),
         grid=(heads,),
-        in_specs=[smem(), whole((8, HEAD_DIM)), half, half, half],
-        out_specs=[half, pl.BlockSpec((2, tile, HEAD_DIM), lambda h: (0, 0, h)), table, table],
+        in_specs=[smem(), smem(), whole((8, HEAD_DIM)), half, half, half],
+        out_specs=[half, kv_spec(tile), table, table, smem()],
         out_shape=[
             jax.ShapeDtypeStruct((tile, width), BF16),
             jax.ShapeDtypeStruct((2, tile, width), BF16),
             jax.ShapeDtypeStruct((tile, HEAD_DIM), F32),
             jax.ShapeDtypeStruct((tile, HEAD_DIM), F32),
+            jax.ShapeDtypeStruct((24,), jnp.int32),
         ],
         compiler_params=params("arbitrary"),
         name="rot",
-    )(info, jnp.asarray(lane_freqs()), q_in, k_in, v_in)
+    )(reach, tile_map.T, jnp.asarray(lane_freqs()), q_in, k_in, v_in)
 
 
 def open_block(info, h, a, b):
@@ -140,6 +154,11 @@
         col = info[1] + b
         ok = ok & (col >= 0) & (col < info[3])
     return ok
+
+
+def mask_column(mask):
+    closed = jnp.where(mask[...] == 1, 0.0, NEG).astype(F32)
+    return jnp.transpose(jnp.broadcast_to(closed, (8, closed.shape[1])))[:, 0:1]
 
 
 def fwd_block(keys, values, extra, q, m, l, acc):
@@ -155,13 +174,13 @@
     acc[...] = acc[...] * alpha + dot_tn(values, p.astype(BF16))
 
 
-def fwd_near_kernel(info, q, own, up, down, tk, tv, bias, acc, m, l):
+def fwd_near_kernel(info, q, own, up, down, tk, tv, mask, acc, m, l):
     h = pl.program_id(0)
     m[...] = jnp.full(m.shape, NEG, F32)
     l[...] = jnp.zeros(l.shape, F32)
     acc[...] = jnp.zeros(acc.shape, F32)
     fwd_block(own[0], own[1], None, q, m, l, acc)
-    fwd_block(tk[...], tv[...], bias[...], q, m, l, acc)
+    fwd_block(tk[...], tv[...], mask_column(mask), q, m, l, acc)
     for a, ref in ((-1, up), (1, down)):
 
         @pl.when(open_block(info, h, a, 0))
@@ -201,7 +220,7 @@
     return pl.BlockSpec((rows, tile), lambda h: (h, 0))
 
 
-def fwd_near_call(info, q, own, up, down, text_keys, text_values, bias):
+def fwd_near_call(info, q, own, up, down, text_keys, text_values, mask):
     tile, width = q.shape
     heads = width // HEAD_DIM
     txt = text_keys.shape[0]
@@ -212,7 +231,7 @@
         grid=(heads,),
         in_specs=[smem(), half_spec(tile)]
         + [kv_spec(tile)] * 3
-        + [half_spec(txt), half_spec(txt), whole((txt, 1))],
+        + [half_spec(txt), half_spec(txt), whole((1, txt))],
         out_specs=[row_spec(HEAD_DIM, tile), row_spec(8, tile), row_spec(8, tile)],
         out_shape=[jax.ShapeDtypeStruct((width, tile), F32), stats, stats],
         compiler_params=params("arbitrary"),
@@ -220,7 +239,7 @@
             flops=4 * tile * keys * width, bytes_accessed=4 * keys * width, transcendentals=0
         ),
         name="fwd_near",
-    )(info, q, own, up, down, text_keys, text_values, bias)
+    )(info, q, own, up, down, text_keys, text_values, mask)
 
 
 def fwd_side_call(info, q, left, right, acc, m, l):
@@ -271,80 +290,99 @@
         in_specs=[kv_spec(tile)] * 3,
         out_specs=stack_spec(tile),
         out_shape=jax.ShapeDtypeStruct((3, 2, tile, width), BF16),
-        compiler_params=params("arbitrary"),
+        compiler_params=params("arbitrary", limit=SMALL),
         name="stack",
     )(up, own, down)
 
 
-def proj_kernel(steps, last, info, w, gate, ot, *refs):
-    pieces, rest = refs[: len(steps)], refs[len(steps) :]
-    if last:
-        acc_in, gate_in, dot_out, delta_out, gate_out = rest
+def piece_block(info, flip, ys, xs, x):
+    y = ys - 1 - info[4] if flip else info[4]
+    return y * xs + x
+
+
+def proj_kernel(flip, ys, xs, info, w, gate, ot, piece, *refs):
+    if flip:
+        acc_in, gate_in, dot_out, delta_out, gate_out, acc, gates = refs
     else:
-        acc_out, gate_out = rest
-    heads_x, heads_y = info[16], info[17]
-    acc = acc_in[...] if last else None
-    if last:
-        gate_out[...] = gate_in[...]
-    else:
-        gate_out[...] = jnp.zeros(gate_out.shape, F32)
-    tile = ot.shape[1]
-    for piece, (flip, dx) in zip(pieces, steps):
-        y = info[18] if not flip else heads_y - 1 - info[18]
-        x = lax.rem(info[19] + dx + heads_x, heads_x)
-        block = y * heads_x + x
-        cols = piece.shape[1]
-        at = pl.multiple_of(block * cols, 128)
-        g = piece[...].astype(F32)
-        scaled = (g * gate[:, pl.ds(at, cols)]).astype(BF16)
-        wp = w[:, pl.ds(at, cols)]
-        part = dot_nt(wp, scaled)
-        acc = part if acc is None else acc + part
-        terms = dot_nn(ot[...], piece[...]) * wp.astype(F32)
-        row = jnp.sum(terms, axis=0, keepdims=True)
-        for i in range(cols // 128):
-            gate_out[pl.ds(block * (cols // 128) + i, 1), :] = row[:, i * 128 : (i + 1) * 128]
-    if not last:
-        acc_out[...] = acc
-    else:
-        rounded = acc.astype(BF16)
+        acc, gates = refs
+    x = pl.program_id(0)
+
+    @pl.when(x == 0)
+    def _():
+        acc[...] = acc_in[...] if flip else jnp.zeros(acc.shape, F32)
+        gates[...] = gate_in[...] if flip else jnp.zeros(gates.shape, F32)
+
+    g = piece[0]
+    scaled = (g.astype(F32) * gate[...]).astype(BF16)
+    acc[...] += dot_nt(w[...], scaled)
+    terms = dot_nn(ot[...], g) * w[...].astype(F32)
+    row = jnp.sum(terms, axis=0, keepdims=True)
+    count = g.shape[1] // 128
+    block = piece_block(info, flip, ys, xs, x)
+    for i in range(count):
+        gates[pl.ds(block * count + i, 1), :] = row[:, i * 128 : (i + 1) * 128]
+    if not flip:
+        return
+
+    @pl.when(x == xs - 1)
+    def _():
+        tile = ot.shape[1]
+        rounded = acc[...].astype(BF16)
         dot_out[...] = rounded
         prod = rounded.astype(F32) * ot[...].astype(F32)
         for h in range(ot.shape[0] // HEAD_DIM):
             d = jnp.sum(prod[h * HEAD_DIM : (h + 1) * HEAD_DIM, :], axis=0, keepdims=True)
             delta_out[8 * h : 8 * h + 8, :] = jnp.broadcast_to(d, (8, tile))
-
-
-def proj_call(steps, info, w, gate, ot, pieces, carried=None):
+        for i in range(gate_out.shape[0]):
+            gate_out[i] = gates[...]
+
+
+def proj_call(flip, sizes, info, w, gate, ot, pieces, carried=()):
+    ys, xs = sizes[3:]
     width, tile = ot.shape
     heads = width // HEAD_DIM
-    cols = pieces[0].shape[1]
+    cols = pieces.shape[2]
     rows = w.shape[1] // 128
-    last = carried is not None
     acc = jax.ShapeDtypeStruct((width, tile), F32)
     gates = jax.ShapeDtypeStruct((rows, 128), F32)
-    if last:
+    if flip:
         out_shape = [
             jax.ShapeDtypeStruct((width, tile), BF16),
             jax.ShapeDtypeStruct((8 * heads, tile), F32),
-            gates,
+            jax.ShapeDtypeStruct((ys * xs, rows, 128), F32),
         ]
+        scratch = [pltpu.VMEM((width, tile), F32), pltpu.VMEM((rows, 128), F32)]
     else:
         out_shape = [acc, gates]
-    operands = (info, w, gate, ot, *pieces) + (tuple(carried) if last else ())
-    return pl.pallas_call(
-        functools.partial(proj_kernel, steps, last),
-        in_specs=[smem()] + [pl.BlockSpec(memory_space=pltpu.VMEM)] * (len(operands) - 1),
-        out_specs=[pl.BlockSpec(memory_space=pltpu.VMEM)] * len(out_shape),
+        scratch = []
+
+    def column(x, info_ref):
+        return (0, piece_block(info_ref, flip, ys, xs, x))
+
+    return pl.pallas_call(
+        functools.partial(proj_kernel, flip, ys, xs),
+        grid_spec=pltpu.PrefetchScalarGridSpec(
+            num_scalar_prefetch=1,
+            grid=(xs,),
+            in_specs=[
+                pl.BlockSpec((width, cols), column),
+                pl.BlockSpec((1, cols), column),
+                whole((width, tile)),
+                pl.BlockSpec((1, tile, cols), lambda x, _: (x, 0, 0)),
+            ]
+            + [whole(c.shape) for c in carried],
+            out_specs=[whole(o.shape) for o in out_shape],
+            scratch_shapes=scratch,
+        ),
         out_shape=out_shape,
-        compiler_params=params(),
+        compiler_params=params("arbitrary"),
         cost_estimate=pl.CostEstimate(
-            flops=4 * tile * width * cols * len(pieces),
-            bytes_accessed=2 * tile * cols * len(pieces) + 2 * w.size,
+            flops=4 * tile * width * cols * xs,
+            bytes_accessed=2 * (tile + width) * cols * xs,
             transcendentals=0,
         ),
         name="proj",
-    )(*operands)
+    )(info, w, gate, ot, pieces, *carried)
 
 
 def bwd_math(keys, values, q, dot, lse, delta, dq, extra):
@@ -378,11 +416,11 @@
 
 
 def bwd_side_kernel(
-    info, q, dot, lse, delta, tk, tv, bias, left, right, left_out, right_out, text_out, dq_out
+    info, q, dot, lse, delta, tk, tv, mask, left, right, left_out, right_out, text_out, dq_out
 ):
     h = pl.program_id(0)
     dq_out[...] = jnp.zeros(dq_out.shape, F32)
-    dk, dv = bwd_math(tk[...], tv[...], q, dot, lse, delta, dq_out, bias[...])
+    dk, dv = bwd_math(tk[...], tv[...], q, dot, lse, delta, dq_out, mask_column(mask))
     text_out[0] = dk.astype(BF16)
     text_out[1] = dv.astype(BF16)
     for b, ref, out in ((-1, left, left_out), (1, right, right_out)):
@@ -420,7 +458,7 @@
     )
 
 
-def bwd_side_call(common, text_keys, text_values, bias, left, right):
+def bwd_side_call(common, text_keys, text_values, mask, left, right):
     info, q, dot, lse, delta = common
     tile, width = q.shape
     txt = text_keys.shape[0]
@@ -429,7 +467,7 @@
         bwd_side_kernel,
         grid=(width // HEAD_DIM,),
         in_specs=bwd_specs(tile)
-        + [half_spec(txt), half_spec(txt), whole((txt, 1))]
+        + [half_spec(txt), half_spec(txt), whole((1, txt))]
         + [stack_spec(tile)] * 2,
         out_specs=[stack_spec(tile)] * 2 + [kv_spec(txt), row_spec(HEAD_DIM, tile)],
         out_shape=[
@@ -441,7 +479,7 @@
         compiler_params=params("arbitrary"),
         cost_estimate=bwd_cost(tile, 6 * tile + txt, width),
         name="bwd_side",
-    )(info, q, dot, lse, delta, text_keys, text_values, bias, left, right)
+    )(info, q, dot, lse, delta, text_keys, text_values, mask, left, right)
 
 
 def bwd_near_call(common, dq, cos, sin, up, own, down):
@@ -504,32 +542,61 @@
         in_specs=[kv_spec(tile), middle, middle, kv_spec(tile), kv_spec(tile), table, table],
         out_specs=[half_spec(tile)] * 2,
         out_shape=[shape, shape],
-        compiler_params=params("arbitrary"),
+        compiler_params=params("arbitrary", limit=SMALL),
         name="finish",
     )(own, left, right, up, down, cos, sin)
 
 
-def chunk_sum_kernel(got, gate, out):
-    groups, rows, width = got.shape
-    text = jnp.sum(got[...].astype(F32), axis=0).astype(BF16)
-    out[:, :, :width] = jnp.broadcast_to(text[None], (groups, rows, width))
-    for i in range(gate.shape[0] // rows):
-        part = gate[i * rows : (i + 1) * rows, :].astype(BF16)
-        at = width + 128 * i
-        out[:, :, at : at + 128] = jnp.broadcast_to(part[None], (groups, rows, 128))
-
-
-def chunk_sum_call(got, gate):
-    groups, rows, width = got.shape
-    lanes = width + 128 * (gate.shape[0] // rows)
-    return pl.pallas_call(
-        chunk_sum_kernel,
+def split_pair(values):
+    hi = values.astype(BF16)
+    return hi, (values - hi.astype(F32)).astype(BF16)
+
+
+def pack_kernel(text, gate, out):
+    groups, rows, _ = out.shape
+    width = text.shape[1]
+    out[:, :, :width] = text[...].reshape(groups, rows, width)
+    out[:, :, width:] = jnp.zeros((groups, rows, 128), BF16)
+    hi, lo = split_pair(jnp.sum(gate[...], axis=0))
+    for i in range(gate.shape[1]):
+        out[i, 0:1, width:] = hi[i : i + 1, :]
+        out[i, 1:2, width:] = lo[i : i + 1, :]
+
+
+def pack_call(text, gate, groups):
+    rows = text.shape[0] // groups
+    return pl.pallas_call(
+        pack_kernel,
         in_specs=[pl.BlockSpec(memory_space=pltpu.VMEM)] * 2,
         out_specs=pl.BlockSpec(memory_space=pltpu.VMEM),
-        out_shape=jax.ShapeDtypeStruct((groups, rows, lanes), BF16),
-        compiler_params=params(),
+        out_shape=jax.ShapeDtypeStruct((groups, rows, text.shape[1] + 128), BF16),
+        compiler_params=params(limit=SMALL),
+        name="pack",
+    )(text, gate)
+
+
+def chunk_sum_kernel(width, got, out):
+    total = jnp.sum(got[...].astype(F32), axis=0)
+    text = total[:, :width].astype(BF16)
+    hi, lo = split_pair(total[0:1, width:] + total[1:2, width:])
+    row = lax.broadcasted_iota(jnp.int32, (total.shape[0], 128), 0)
+    side = jnp.where(
+        row == 0, hi.astype(F32), jnp.where(row == 1, lo.astype(F32), 0.0)
+    ).astype(BF16)
+    groups = out.shape[0]
+    out[:, :, :width] = jnp.broadcast_to(text[None], (groups, *text.shape))
+    out[:, :, width:] = jnp.broadcast_to(side[None], (groups, *side.shape))
+
+
+def chunk_sum_call(got, width):
+    return pl.pallas_call(
+        functools.partial(chunk_sum_kernel, width),
+        in_specs=[pl.BlockSpec(memory_space=pltpu.VMEM)],
+        out_specs=pl.BlockSpec(memory_space=pltpu.VMEM),
+        out_shape=jax.ShapeDtypeStruct(got.shape, BF16),
+        compiler_params=params(limit=SMALL),
         name="chunk_sum",
-    )(got, gate)
+    )(got)
 
 
 def unpack_kernel(got, keys_out, values_out, gate_out):
@@ -538,11 +605,9 @@
     half = groups // 2
     keys_out[...] = got[:half, :, :width].reshape(half * rows, width)
     values_out[...] = got[half:, :, :width].reshape(half * rows, width)
-    for i in range(gate_out.shape[0] // rows):
-        at = width + 128 * i
-        gate_out[i * rows : (i + 1) * rows, :] = jnp.sum(
-            got[:, :, at : at + 128].astype(F32), axis=0
-        )
+    for i in range(gate_out.shape[0]):
+        pair = got[i, :, width:].astype(F32)
+        gate_out[i : i + 1, :] = pair[0:1, :] + pair[1:2, :]
 
 
 def unpack_call(got, width, gate_rows):
@@ -553,7 +618,7 @@
         in_specs=[pl.BlockSpec(memory_space=pltpu.VMEM)],
         out_specs=[pl.BlockSpec(memory_space=pltpu.VMEM)] * 3,
         out_shape=[text, text, jax.ShapeDtypeStruct((gate_rows, 128), F32)],
-        compiler_params=params(),
+        compiler_params=params(limit=SMALL),
         name="unpack",
     )(got)
 
@@ -569,8 +634,9 @@
     return lax.ppermute(array, axis, [(i, i ^ bit) for i in range(length)])
 
 
-def in_hbm(*arrays):
-    return [pltpu.with_memory_space_constraint(a, pltpu.HBM) for a in arrays]
+def spread(array, axis):
+    copies = jnp.broadcast_to(array[None], (lax.axis_size(axis), *array.shape))
+    return lax.all_to_all(copies, axis, 0, 0, tiled=True)
 
 
 def on_device(
@@ -588,74 +654,44 @@
 ):
     _, width = query_in.shape
     seq_count = lax.axis_size(SEQ)
-    row, col = lax.axis_index("z"), lax.axis_index(COL)
-    coords = lax.dynamic_slice(tile_map, (lax.axis_index(SEQ), 0), (1, 3))[0]
-    counts = jnp.array(
-        [lax.axis_size("z"), lax.axis_size(COL)], jnp.int32
-    )
-    info = jnp.concatenate(
-        [
-            jnp.stack([row, col]).astype(jnp.int32),
-            counts,
-            coords,
-            jnp.zeros((1,), jnp.int32),
-            window_reach.reshape(-1),
-            jnp.zeros((8 - window_reach.size,), jnp.int32),
-            jnp.array([lax.axis_size("x"), lax.axis_size("yhi")], jnp.int32),
-            jnp.stack([lax.axis_index("yhi"), lax.axis_index("x")]).astype(jnp.int32),
-        ]
-    )
-    bias = jnp.where(text_mask == 1, 0.0, NEG).astype(F32)[:, None]
-
-    query_in, key_in, value_in = in_hbm(query_in, key_in, value_in)
-    text_keys, text_values = in_hbm(text_keys, text_values)
+    sizes = tuple(lax.axis_size(axis) for axis in (*SEQ, *HEAD))
+    mask = text_mask.reshape(1, -1)
 
     g_y = swap(grad_out, "yhi", 1)
-    g_r = shift(grad_out, "x", 1, True)
-    g_l = shift(grad_out, "x", -1, True)
-
-    q, kv, cos, sin = rotate_call(info, query_in, key_in, value_in)
+    g_x = spread(grad_out, "x")
+
+    q, kv, cos, sin, info = rotate_call(sizes, window_reach, tile_map, query_in, key_in, value_in)
 
     kv_up, kv_down = shift(kv, "z", 1), shift(kv, "z", -1)
-    g_far = shift(g_l, "x", -1, True)
-    gy_r = shift(g_y, "x", 1, True)
-    gy_l = shift(g_y, "x", -1, True)
     stack = stack_call(kv_up, kv, kv_down)
     kv_left, kv_right = shift(stack, COL, 1), shift(stack, COL, -1)
-    gy_far = shift(gy_r, "x", 1, True)
-
-    partial = fwd_near_call(info, q, kv, kv_up, kv_down, text_keys, text_values, bias)
+    gy_x = spread(g_y, "x")
+
+    partial = fwd_near_call(info, q, kv, kv_up, kv_down, text_keys, text_values, mask)
     ot, lse = fwd_side_call(info, q, kv_left, kv_right, *partial)
 
     gate = gate_scale.reshape(1, -1)
-    steps = ((False, 0), (False, -1), (False, 1), (False, 2))
-    carried = proj_call(steps, info, out_weight, gate, ot, [grad_out, g_r, g_l, g_far])
-    steps = ((True, 0), (True, -1), (True, 1), (True, 2))
+    carried = proj_call(False, sizes, info, out_weight, gate, ot, g_x)
     dot, delta, gate_terms = proj_call(
-        steps, info, out_weight, gate, ot, [g_y, gy_r, gy_l, gy_far], carried
+        True, sizes, info, out_weight, gate, ot, gy_x, carried
     )
+    gate_terms = lax.all_to_all(gate_terms, HEAD, 0, 0, tiled=True)
 
     common = (info, q, dot, lse, delta)
     left, right, text_part, dq = bwd_side_call(
-        common, text_keys, text_values, bias, kv_left, kv_right
+        common, text_keys, text_values, mask, kv_left, kv_right
     )
     back_left = shift(left, COL, -1)
     back_right = shift(right, COL, 1)
-    got = lax.all_to_all(
-        text_part.reshape(seq_count, -1, width), SEQ, 0, 0, tiled=True
-    )
+    packed = pack_call(text_part.reshape(-1, width), gate_terms, seq_count)
+    got = lax.all_to_all(packed, SEQ, 0, 0, tiled=True)
     up, own, down, grad_query = bwd_near_call(common, dq, cos, sin, kv_up, kv, kv_down)
-    for axis in ("x", "yhi"):
-        bit = 1
-        while bit < lax.axis_size(axis):
-            gate_terms = gate_terms + swap(gate_terms, axis, bit)
-            bit *= 2
 
     up, down = pair_sum_call(up, down, back_left, back_right)
     up = shift(up, "z", -1)
     down = shift(down, "z", 1)
 
-    chunk = chunk_sum_call(got, gate_terms)
+    chunk = chunk_sum_call(got, width)
     summed = lax.all_to_all(chunk, SEQ, 0, 0, tiled=True)
     grad_text_keys, grad_text_values, grad_gate = unpack_call(
         summed, width, out_weight.shape[1] // 128

time: 194 us -> 179 us (0.923)
  the two profiles are of different devices: /device:TPU:1 before, /device:TPU:68 now
where the time goes in v1:
time: 179 us; the launch traced here: 178 us
  starting transfers between devices  67.7 us (38%)
  Pallas kernels  42.2 us (24%)
  blocking collectives  32.9 us (18%)
  waiting for transfers between devices  27.8 us (16%)
  local copies, waits for them, and re-layouts  6.34 us (4%)
    all_to_all x1, blocking collectives, on_device(): got = lax.all_to_all(packed, SEQ, 0, 0, tiled=True)  32.9 us
    ppermute x8, starting transfers between devices, shift(): return lax.ppermute(array, axis, pairs)  31.5 us
    ppermute x8, waiting for transfers between devices, shift(): return lax.ppermute(array, axis, pairs)  18.4 us
    pallas_call x2, Pallas kernels, proj_call(): pl.pallas_call(functools.partial(proj_kernel, flip, ys, xs), grid_spec=pl...  10.3 us
    all_to_all x1, starting transfers between devices, on_device(): gate_terms = lax.all_to_all(gate_terms, HEAD, 0, 0, tiled=True)  9.78 us
    all_to_all x2, starting transfers between devices, spread(): return lax.all_to_all(copies, axis, 0, 0, tiled=True)  9.59 us
    ppermute x1, waiting for transfers between devices, swap(): return lax.ppermute(array, axis, [(i, i ^ bit) for i in range(length)])  9.39 us
    all_to_all x1, starting transfers between devices, on_device(): summed = lax.all_to_all(chunk, SEQ, 0, 0, tiled=True)  9.02 us
  transfers between devices with their start and end apart: 13, of which 5 were waited for; matrix products, arithmetic and copies ran while one was open for 1% of the time, Pallas kernels for 20%

profile of v1, /device:TPU:68, one launch (start us, length us, event | category | flops | bytes accessed | tf_op | source)
XLA Modules:
  0.0 177.7 jit_solution(6059785370218811350)
XLA Ops:
  0.6 2.1 %broadcast_in_dim.5 = bf16[4,384,384]{2,1,0:T(8,128)(2,1)} broadcast(bf16[384,384]{1,0:T(8,128)(2,1)} %param.22), dimensions={1,2} | broadcast | bytes 1474560 | tf_op jit(solution)/shard_map/broadcast_in_dim | solution.py:638
  2.7 4.8 %all-to-all-start.1 = ((bf16[4,384,384]{2,1,0:T(8,128)(2,1)}), bf16[4,384,384]{2,1,0:T(8,128)(2,1)}, u32[]{:S(2)}, u32[]{:S(2)}) async-start(bf16[4,384,384]{2,1,0:T(8,128)(2,1)} %broadcast_in_dim.5), calls=%async_computation.1 | async-start | bytes 2359296 | tf_op jit(solution)/shard_map/all_to_all | solution.py:639
  7.5 0.0 copy-start.7
  7.5 2.5 %rot.1 = (bf16[384,256]{1,0:T(8,128)(2,1)}, bf16[2,384,256]{2,1,0:T(8,128)(2,1)}, f32[384,128]{1,0:T(8,128)}, f32[384,128]{1,0:T(8,128)}, s32[24]{0:T(128)}) custom-call(s32[2,2]{1,0:T(2,128)} %reach.1, s32[3,64]{1,0:T(4,128)} %bitcast.8, f32[8,128]{1,0:T(8,128)} %constant.2.clone.freq, bf16[384,256]{1,0:T(8,128)(2,1)} %q.1, bf16[384,256]{1,0:T(8,128)(2,1)} %k.1, ...), custom_call_target="tpu_custom_call" | custom-call | tf_op jit(solution)/shard_map/rot/pallas_call | solution.py:131
  10.0 4.3 %collective-permute-start = (bf16[2,384,256]{2,1,0:T(8,128)(2,1)}, bf16[2,384,256]{2,1,0:T(8,128)(2,1)S(1)}, u32[]{:S(2)}, u32[]{:S(2)}) collective-permute-start(bf16[2,384,256]{2,1,0:T(8,128)(2,1)} %get-tuple-element.38.own), channel_id=1, source_target_pairs={{0,64},{64,128},{128,192},{192,256},{256,320},{320,384},{384,448},... | collective-permute-start | bytes 1179656 | tf_op jit(solution)/shard_map/ppermute | solution.py:629
  14.3 3.9 %collective-permute-start.1 = (bf16[2,384,256]{2,1,0:T(8,128)(2,1)}, bf16[2,384,256]{2,1,0:T(8,128)(2,1)S(1)}, u32[]{:S(2)}, u32[]{:S(2)}) collective-permute-start(bf16[2,384,256]{2,1,0:T(8,128)(2,1)} %get-tuple-element.38.own), channel_id=1, source_target_pairs={{64,0},{128,64},{192,128},{256,192},{320,256},{384,320},{448,384},... | collective-permute-start | bytes 1179656 | tf_op jit(solution)/shard_map/ppermute | solution.py:629
  18.2 4.4 %collective-permute-done.up = bf16[2,384,256]{2,1,0:T(8,128)(2,1)S(1)} collective-permute-done((bf16[2,384,256]{2,1,0:T(8,128)(2,1)}, bf16[2,384,256]{2,1,0:T(8,128)(2,1)S(1)}, u32[]{:S(2)}, u32[]{:S(2)}) %collective-permute-start) | collective-permute-done | bytes 393248 | tf_op jit(solution)/shard_map/ppermute | solution.py:629
  22.7 0.0 copy-start.2
  22.7 4.6 %collective-permute-done.1.down = bf16[2,384,256]{2,1,0:T(8,128)(2,1)S(1)} collective-permute-done((bf16[2,384,256]{2,1,0:T(8,128)(2,1)}, bf16[2,384,256]{2,1,0:T(8,128)(2,1)S(1)}, u32[]{:S(2)}, u32[]{:S(2)}) %collective-permute-start.1) | collective-permute-done | bytes 393248 | tf_op jit(solution)/shard_map/ppermute | solution.py:629
  27.3 0.0 copy-start.1
  27.3 1.0 copy-done.1
  28.3 0.0 copy-start.3
  28.3 1.3 stack.1
  29.6 2.3 %collective-permute-start.2 = (bf16[3,2,384,256]{3,2,1,0:T(8,128)(2,1)}, bf16[3,2,384,256]{3,2,1,0:T(8,128)(2,1)}, u32[]{:S(2)}, u32[]{:S(2)}) collective-permute-start(bf16[3,2,384,256]{3,2,1,0:T(8,128)(2,1)} %stack.1), channel_id=1, source_target_pairs={{0,8},{8,16},{16,24},{24,32},{32,40},{40,48},{48,56},{1,9},{9,17},... | collective-permute-start | bytes 3538952 | tf_op jit(solution)/shard_map/ppermute | solution.py:629
  31.9 1.3 collective-permute-start.3
  33.2 0.0 copy-done.7
  33.2 7.7 %collective-permute-start.4 = (bf16[384,384]{1,0:T(8,128)(2,1)S(1)}, bf16[384,384]{1,0:T(8,128)(2,1)S(1)}, u32[]{:S(2)}, u32[]{:S(2)}) collective-permute-start(bf16[384,384]{1,0:T(8,128)(2,1)S(1)} %copy-done.7), channel_id=1, source_target_pairs={{0,4},{4,0},{1,5},{5,1},{2,6},{6,2},{3,7},{7,3},{8,12},{12,8},{9,1... | collective-permute-start | bytes 884744 | tf_op jit(solution)/shard_map/ppermute | solution.py:634
  41.0 9.4 %collective-permute-done.4 = bf16[384,384]{1,0:T(8,128)(2,1)S(1)} collective-permute-done((bf16[384,384]{1,0:T(8,128)(2,1)S(1)}, bf16[384,384]{1,0:T(8,128)(2,1)S(1)}, u32[]{:S(2)}, u32[]{:S(2)}) %collective-permute-start.4) | collective-permute-done | bytes 294944 | tf_op jit(solution)/shard_map/ppermute | solution.py:634
  50.4 0.0 all-to-all-done.1.piece
  50.4 1.2 broadcast_in_dim.4
  51.5 0.0 copy-done.2
  51.5 0.0 copy-done.3
  51.5 4.8 %all-to-all-start = ((bf16[4,384,384]{2,1,0:T(8,128)(2,1)}), bf16[4,384,384]{2,1,0:T(8,128)(2,1)}, u32[]{:S(2)}, u32[]{:S(2)}) async-start(bf16[4,384,384]{2,1,0:T(8,128)(2,1)} %broadcast_in_dim.4), calls=%async_computation | async-start | bytes 2359296 | tf_op jit(solution)/shard_map/all_to_all | solution.py:639
  56.3 4.9 %fwd_near.1 = (f32[256,384]{1,0:T(8,128)}, f32[16,384]{1,0:T(8,128)}, f32[16,384]{1,0:T(8,128)}) custom-call(s32[24]{0:T(128)} %get-tuple-element.36.info, bf16[384,256]{1,0:T(8,128)(2,1)} %get-tuple-element.37.q, bf16[2,384,256]{2,1,0:T(8,128)(2,1)} %get-tuple-element.38.own, bf16[2,384,256]{2,1,0:T(8,128)(2,1)} %copy-done.2, ...), custom_call_target="tpu_custom_call" | custom-call | flops 553648128 | bytes 1441792 | tf_op jit(solution)/shard_map/fwd_near/pallas_call | solution.py:229
  61.2 0.0 collective-permute-done.2.left
  61.2 0.0 collective-permute-done.3.right
  61.2 4.5 %fwd_side.1 = (bf16[256,384]{1,0:T(8,128)(2,1)}, f32[16,384]{1,0:T(8,128)}) custom-call(s32[24]{0:T(128)} %get-tuple-element.36.info, bf16[384,256]{1,0:T(8,128)(2,1)} %get-tuple-element.37.q, bf16[3,2,384,256]{3,2,1,0:T(8,128)(2,1)} %collective-permute-done.2.left, bf16[3,2,384,256]{3,2,1,0:T(8,128)(2,1)} %collective-permute-done.3.right, ...), custom_call_target="tpu_custom_call" | custom-call | flops 905969664 | bytes 2359296 | tf_op jit(solution)/shard_map/fwd_side/pallas_call | solution.py:249
  65.7 5.0 %proj.2 = (f32[256,384]{1,0:T(8,128)}, f32[24,128]{1,0:T(8,128)}) custom-call(s32[24]{0:T(128)} %get-tuple-element.36.info, bf16[256,3072]{1,0:T(8,128)(2,1)} %w.3, f32[1,3072]{1,0:T(1,128)} %bitcast.6, bf16[256,384]{1,0:T(8,128)(2,1)} %get-tuple-element.42.ot, bf16[4,384,384]{2,1,0:T(8,128)(2,1)} %all-to-all-done.1.piece), custom_call_target="tpu_custom_call" | custom-call | flops 603979776 | bytes 1966080 | tf_op jit(solution)/shard_map/proj/pallas_call | solution.py:362
  70.7 0.0 all-to-all-done.piece
  70.7 5.3 %proj.3 = (bf16[256,384]{1,0:T(8,128)(2,1)}, f32[16,384]{1,0:T(8,128)}, f32[8,24,128]{2,1,0:T(8,128)}) custom-call(s32[24]{0:T(128)} %get-tuple-element.36.info, bf16[256,3072]{1,0:T(8,128)(2,1)} %w.3, f32[1,3072]{1,0:T(1,128)} %bitcast.7, bf16[256,384]{1,0:T(8,128)(2,1)} %get-tuple-element.42.ot, bf16[4,384,384]{2,1,0:T(8,128)(2,1)} %all-to-all-done.piece, ...), custom_call_target="tpu_custom_call" | custom-call | flops 603979776 | bytes 1966080 | tf_op jit(solution)/shard_map/proj/pallas_call | solution.py:362
  76.0 9.8 %all-to-all-start.2 = ((f32[8,24,128]{2,1,0:T(8,128)}), f32[8,24,128]{2,1,0:T(8,128)S(1)}, u32[]{:S(2)}, u32[]{:S(2)}) async-start(f32[8,24,128]{2,1,0:T(8,128)} %get-tuple-element.62), calls=%async_computation.2 | async-start | bytes 196608 | tf_op jit(solution)/shard_map/all_to_all | solution.py:678
  85.8 6.3 %bwd_side.1 = (bf16[3,2,384,256]{3,2,1,0:T(8,128)(2,1)}, bf16[3,2,384,256]{3,2,1,0:T(8,128)(2,1)}, bf16[2,256,256]{2,1,0:T(8,128)(2,1)}, f32[256,384]{1,0:T(8,128)}) custom-call(s32[24]{0:T(128)} %get-tuple-element.36.info, bf16[384,256]{1,0:T(8,128)(2,1)} %get-tuple-element.37.q, bf16[256,384]{1,0:T(8,128)(2,1)} %get-tuple-element.45.dot, ...), custom_call_target="tpu_custom_call" | custom-call | flops 2516582400 | bytes 5242880 | tf_op jit(solution)/shard_map/bwd_side/pallas_call | solution.py:466
  92.1 1.3 collective-permute-start.5
  93.4 12.6 %collective-permute-start.6 = (bf16[3,2,384,256]{3,2,1,0:T(8,128)(2,1)}, bf16[3,2,384,256]{3,2,1,0:T(8,128)(2,1)}, u32[]{:S(2)}, u32[]{:S(2)}) collective-permute-start(bf16[3,2,384,256]{3,2,1,0:T(8,128)(2,1)} %get-tuple-element.54), channel_id=1, source_target_pairs={{0,8},{8,16},{16,24},{24,32},{32,40},{40,48},{48,56},{1,9},{9,17},... | collective-permute-start | bytes 3538952 | tf_op jit(solution)/shard_map/ppermute | solution.py:629
  106.0 0.0 all-to-all-done.2.gate
  106.0 0.0 copy-start.4
  106.0 0.9 copy-done.4
  107.0 0.1 pack.1
  107.0 32.9 %all_to_all.25.got = bf16[64,8,384]{2,1,0:T(8,128)(2,1)S(1)} all-to-all(bf16[64,8,384]{2,1,0:T(8,128)(2,1)S(1)} %pack.1), channel_id=1, replica_groups=mesh['z'=8,'y'=4,'core'=2,'yhi'=2,'x'=4] {'z','y','core'}, dimensions={0} | all-to-all | bytes 786432 | tf_op jit(solution)/shard_map/all_to_all | solution.py:687
  140.0 0.9 chunk_sum.1
  140.8 9.0 %all-to-all-start.4 = ((bf16[64,8,384]{2,1,0:T(8,128)(2,1)}), bf16[64,8,384]{2,1,0:T(8,128)(2,1)S(1)}, u32[]{:S(2)}, u32[]{:S(2)}) async-start(bf16[64,8,384]{2,1,0:T(8,128)(2,1)} %chunk_sum.1), calls=%async_computation.4 | async-start | bytes 786432 | tf_op jit(solution)/shard_map/all_to_all | solution.py:695
  149.9 5.3 %bwd_near.1 = (f32[2,384,256]{2,1,0:T(8,128)}, f32[2,384,256]{2,1,0:T(8,128)}, f32[2,384,256]{2,1,0:T(8,128)}, bf16[384,256]{1,0:T(8,128)(2,1)}) custom-call(s32[24]{0:T(128)} %get-tuple-element.36.info, bf16[384,256]{1,0:T(8,128)(2,1)} %get-tuple-element.37.q, bf16[256,384]{1,0:T(8,128)(2,1)} %get-tuple-element.45.dot, f32[16,384]{1,0:T(8,128)} %get-tuple-element.46.lse, ...), custom_call_target="tpu_custom_call" | custom-call | flops 1132462080 | bytes 2359296 | tf_op jit(solution)/shard_map/bwd_near/pallas_call | solution.py:490
  155.2 0.0 collective-permute-done.5.left
  155.2 0.0 collective-permute-done.6.right
  155.2 0.0 copy-start.5
  155.2 0.0 copy-start.6
  155.2 3.0 %pair_sum.1 = (bf16[2,384,256]{2,1,0:T(8,128)(2,1)}, bf16[2,384,256]{2,1,0:T(8,128)(2,1)}) custom-call(f32[2,384,256]{2,1,0:T(8,128)} %get-tuple-element.55.up, f32[2,384,256]{2,1,0:T(8,128)} %get-tuple-element.56.down, bf16[3,2,384,256]{3,2,1,0:T(8,128)(2,1)} %collective-permute-done.5.left, bf16[3,2,384,256]{3,2,1,0:T(8,128)(2,1)} %collective-permute-done.6.right), custom_call_target="tpu_custom_call" | custom-call | tf_op jit(solution)/shard_map/pair_sum/pallas_call | solution.py:513
  158.2 1.9 %collective-permute-start.7 = (bf16[2,384,256]{2,1,0:T(8,128)(2,1)}, bf16[2,384,256]{2,1,0:T(8,128)(2,1)S(1)}, u32[]{:S(2)}, u32[]{:S(2)}) collective-permute-start(bf16[2,384,256]{2,1,0:T(8,128)(2,1)} %get-tuple-element.57), channel_id=1, source_target_pairs={{64,0},{128,64},{192,128},{256,192},{320,256},{384,320},{448,384},... | collective-permute-start | bytes 1179656 | tf_op jit(solution)/shard_map/ppermute | solution.py:629
  160.1 3.9 %collective-permute-start.8 = (bf16[2,384,256]{2,1,0:T(8,128)(2,1)}, bf16[2,384,256]{2,1,0:T(8,128)(2,1)S(1)}, u32[]{:S(2)}, u32[]{:S(2)}) collective-permute-start(bf16[2,384,256]{2,1,0:T(8,128)(2,1)} %get-tuple-element.58), channel_id=1, source_target_pairs={{0,64},{64,128},{128,192},{192,256},{256,320},{320,384},{384,448},... | collective-permute-start | bytes 1179656 | tf_op jit(solution)/shard_map/ppermute | solution.py:629
  164.1 7.6 %collective-permute-done.7.up = bf16[2,384,256]{2,1,0:T(8,128)(2,1)S(1)} collective-permute-done((bf16[2,384,256]{2,1,0:T(8,128)(2,1)}, bf16[2,384,256]{2,1,0:T(8,128)(2,1)S(1)}, u32[]{:S(2)}, u32[]{:S(2)}) %collective-permute-start.7) | collective-permute-done | bytes 393248 | tf_op jit(solution)/shard_map/ppermute | solution.py:629
  171.6 1.7 collective-permute-done.8.down
  173.4 0.0 copy-done.5
  173.4 0.0 copy-done.6
  173.4 0.0 copy-start
  173.4 1.1 copy-done
  174.5 2.4 %finish.1 = (bf16[384,256]{1,0:T(8,128)(2,1)}, bf16[384,256]{1,0:T(8,128)(2,1)}) custom-call(f32[2,384,256]{2,1,0:T(8,128)S(1)} %copy-done, bf16[3,2,384,256]{3,2,1,0:T(8,128)(2,1)} %collective-permute-done.5.left, bf16[3,2,384,256]{3,2,1,0:T(8,128)(2,1)} %collective-permute-done.6.right, bf16[2,384,256]{2,1,0:T(8,128)(2,1)S(1)} %collective-permute-done.7.up, ...), custom_call_target="tpu_custom_call" | custom-call | tf_op jit(solution)/shard_map/finish/pallas_call | solution.py:539
  177.0 0.0 all-to-all-done.4.got
  177.0 0.7 unpack.1
Async XLA Ops:
  2.7 47.7 %all-to-all-start.1 = ((bf16[4,384,384]{2,1,0:T(8,128)(2,1)}), bf16[4,384,384]{2,1,0:T(8,128)(2,1)}, u32[]{:S(2)}, u32[]{:S(2)}) async-start(bf16[4,384,384]{2,1,0:T(8,128)(2,1)} %broadcast_in_dim.5), calls=%async_computation.1 | async-start | bytes 2359296 | tf_op jit(solution)/shard_map/all_to_all | solution.py:639
  7.5 25.7 %copy-start.7 = (bf16[384,384]{1,0:T(8,128)(2,1)S(1)}, bf16[384,384]{1,0:T(8,128)(2,1)}, u32[]{:S(2)}) copy-start(bf16[384,384]{1,0:T(8,128)(2,1)} %param.22) | copy-start | bytes 884740
  10.0 12.6 %collective-permute-start = (bf16[2,384,256]{2,1,0:T(8,128)(2,1)}, bf16[2,384,256]{2,1,0:T(8,128)(2,1)S(1)}, u32[]{:S(2)}, u32[]{:S(2)}) collective-permute-start(bf16[2,384,256]{2,1,0:T(8,128)(2,1)} %get-tuple-element.38.own), channel_id=1, source_target_pairs={{0,64},{64,128},{128,192},{192,256},{256,320},{320,384},{384,448},... | collective-permute-start | bytes 1179656 | tf_op jit(solution)/shard_map/ppermute | solution.py:629
  14.3 13.0 %collective-permute-start.1 = (bf16[2,384,256]{2,1,0:T(8,128)(2,1)}, bf16[2,384,256]{2,1,0:T(8,128)(2,1)S(1)}, u32[]{:S(2)}, u32[]{:S(2)}) collective-permute-start(bf16[2,384,256]{2,1,0:T(8,128)(2,1)} %get-tuple-element.38.own), channel_id=1, source_target_pairs={{64,0},{128,64},{192,128},{256,192},{320,256},{384,320},{448,384},... | collective-permute-start | bytes 1179656 | tf_op jit(solution)/shard_map/ppermute | solution.py:629
  22.7 28.9 %copy-start.2 = (bf16[2,384,256]{2,1,0:T(8,128)(2,1)}, bf16[2,384,256]{2,1,0:T(8,128)(2,1)S(1)}, u32[]{:S(2)}) copy-start(bf16[2,384,256]{2,1,0:T(8,128)(2,1)S(1)} %collective-permute-done.up) | copy-start | bytes 1179652
  27.3 1.0 copy-start.1
  28.3 23.2 %copy-start.3 = (bf16[2,384,256]{2,1,0:T(8,128)(2,1)}, bf16[2,384,256]{2,1,0:T(8,128)(2,1)S(1)}, u32[]{:S(2)}) copy-start(bf16[2,384,256]{2,1,0:T(8,128)(2,1)S(1)} %collective-permute-done.1.down) | copy-start | bytes 1179652
  29.6 31.6 %collective-permute-start.2 = (bf16[3,2,384,256]{3,2,1,0:T(8,128)(2,1)}, bf16[3,2,384,256]{3,2,1,0:T(8,128)(2,1)}, u32[]{:S(2)}, u32[]{:S(2)}) collective-permute-start(bf16[3,2,384,256]{3,2,1,0:T(8,128)(2,1)} %stack.1), channel_id=1, source_target_pairs={{0,8},{8,16},{16,24},{24,32},{32,40},{40,48},{48,56},{1,9},{9,17},... | collective-permute-start | bytes 3538952 | tf_op jit(solution)/shard_map/ppermute | solution.py:629
  31.9 29.3 %collective-permute-start.3 = (bf16[3,2,384,256]{3,2,1,0:T(8,128)(2,1)}, bf16[3,2,384,256]{3,2,1,0:T(8,128)(2,1)}, u32[]{:S(2)}, u32[]{:S(2)}) collective-permute-start(bf16[3,2,384,256]{3,2,1,0:T(8,128)(2,1)} %stack.1), channel_id=1, source_target_pairs={{8,0},{16,8},{24,16},{32,24},{40,32},{48,40},{56,48},{9,1},{17,9},... | collective-permute-start | bytes 3538952 | tf_op jit(solution)/shard_map/ppermute | solution.py:629
  33.2 17.1 %collective-permute-start.4 = (bf16[384,384]{1,0:T(8,128)(2,1)S(1)}, bf16[384,384]{1,0:T(8,128)(2,1)S(1)}, u32[]{:S(2)}, u32[]{:S(2)}) collective-permute-start(bf16[384,384]{1,0:T(8,128)(2,1)S(1)} %copy-done.7), channel_id=1, source_target_pairs={{0,4},{4,0},{1,5},{5,1},{2,6},{6,2},{3,7},{7,3},{8,12},{12,8},{9,1... | collective-permute-start | bytes 884744 | tf_op jit(solution)/shard_map/ppermute | solution.py:634
  51.5 19.2 %all-to-all-start = ((bf16[4,384,384]{2,1,0:T(8,128)(2,1)}), bf16[4,384,384]{2,1,0:T(8,128)(2,1)}, u32[]{:S(2)}, u32[]{:S(2)}) async-start(bf16[4,384,384]{2,1,0:T(8,128)(2,1)} %broadcast_in_dim.4), calls=%async_computation | async-start | bytes 2359296 | tf_op jit(solution)/shard_map/all_to_all | solution.py:639
  76.0 30.0 %all-to-all-start.2 = ((f32[8,24,128]{2,1,0:T(8,128)}), f32[8,24,128]{2,1,0:T(8,128)S(1)}, u32[]{:S(2)}, u32[]{:S(2)}) async-start(f32[8,24,128]{2,1,0:T(8,128)} %get-tuple-element.62), calls=%async_computation.2 | async-start | bytes 196608 | tf_op jit(solution)/shard_map/all_to_all | solution.py:678
  92.1 63.0 %collective-permute-start.5 = (bf16[3,2,384,256]{3,2,1,0:T(8,128)(2,1)}, bf16[3,2,384,256]{3,2,1,0:T(8,128)(2,1)}, u32[]{:S(2)}, u32[]{:S(2)}) collective-permute-start(bf16[3,2,384,256]{3,2,1,0:T(8,128)(2,1)} %get-tuple-element.53), channel_id=1, source_target_pairs={{8,0},{16,8},{24,16},{32,24},{40,32},{48,40},{56,48},{9,1},{17,9},... | collective-permute-start | bytes 3538952 | tf_op jit(solution)/shard_map/ppermute | solution.py:629
  93.4 61.8 %collective-permute-start.6 = (bf16[3,2,384,256]{3,2,1,0:T(8,128)(2,1)}, bf16[3,2,384,256]{3,2,1,0:T(8,128)(2,1)}, u32[]{:S(2)}, u32[]{:S(2)}) collective-permute-start(bf16[3,2,384,256]{3,2,1,0:T(8,128)(2,1)} %get-tuple-element.54), channel_id=1, source_target_pairs={{0,8},{8,16},{16,24},{24,32},{32,40},{40,48},{48,56},{1,9},{9,17},... | collective-permute-start | bytes 3538952 | tf_op jit(solution)/shard_map/ppermute | solution.py:629
  106.0 1.0 copy-start.4
  140.8 36.1 %all-to-all-start.4 = ((bf16[64,8,384]{2,1,0:T(8,128)(2,1)}), bf16[64,8,384]{2,1,0:T(8,128)(2,1)S(1)}, u32[]{:S(2)}, u32[]{:S(2)}) async-start(bf16[64,8,384]{2,1,0:T(8,128)(2,1)} %chunk_sum.1), calls=%async_computation.4 | async-start | bytes 786432 | tf_op jit(solution)/shard_map/all_to_all | solution.py:695
  155.2 18.2 %copy-start.5 = (f32[384,128]{1,0:T(8,128)S(1)}, f32[384,128]{1,0:T(8,128)}, u32[]{:S(2)}) copy-start(f32[384,128]{1,0:T(8,128)} %get-tuple-element.49.cos) | copy-start | bytes 589828
  155.2 18.2 %copy-start.6 = (f32[384,128]{1,0:T(8,128)S(1)}, f32[384,128]{1,0:T(8,128)}, u32[]{:S(2)}) copy-start(f32[384,128]{1,0:T(8,128)} %get-tuple-element.50.sin) | copy-start | bytes 589828
  158.2 13.4 %collective-permute-start.7 = (bf16[2,384,256]{2,1,0:T(8,128)(2,1)}, bf16[2,384,256]{2,1,0:T(8,128)(2,1)S(1)}, u32[]{:S(2)}, u32[]{:S(2)}) collective-permute-start(bf16[2,384,256]{2,1,0:T(8,128)(2,1)} %get-tuple-element.57), channel_id=1, source_target_pairs={{64,0},{128,64},{192,128},{256,192},{320,256},{384,320},{448,384},... | collective-permute-start | bytes 1179656 | tf_op jit(solution)/shard_map/ppermute | solution.py:629
  160.1 13.2 %collective-permute-start.8 = (bf16[2,384,256]{2,1,0:T(8,128)(2,1)}, bf16[2,384,256]{2,1,0:T(8,128)(2,1)S(1)}, u32[]{:S(2)}, u32[]{:S(2)}) collective-permute-start(bf16[2,384,256]{2,1,0:T(8,128)(2,1)} %get-tuple-element.58), channel_id=1, source_target_pairs={{0,64},{64,128},{128,192},{192,256},{256,320},{320,384},{384,448},... | collective-permute-start | bytes 1179656 | tf_op jit(solution)/shard_map/ppermute | solution.py:629
  173.4 1.1 copy-start

commit v2 on v1

--- a/solution.py
+++ b/solution.py
@@ -21,6 +21,7 @@
 C1 = SCALE * LOG2E
 SEQ = ("z", "y", "core")
 COL = ("y", "core")
+CHIPS = ("z", "y")
 HEAD = ("yhi", "x")
 F32 = jnp.float32
 BF16 = jnp.bfloat16
@@ -87,6 +88,7 @@
         info[2] = rows
         info[3] = ys * cores
         info[4] = lax.axis_index("yhi")
+        info[5] = lax.axis_index("core")
         for h in range(reach.shape[0]):
             info[8 + 2 * h] = reach[h, 0]
             info[9 + 2 * h] = reach[h, 1]
@@ -188,7 +190,9 @@
             fwd_block(ref[0], ref[1], None, q, m, l, acc)
 
 
-def fwd_side_kernel(info, q, left, right, acc_in, m_in, l_in, ot_out, lse_out, acc, m, l):
+def fwd_side_kernel(
+    info, q, left, right, acc_in, m_in, l_in, dot, ot_out, lse_out, delta_out, acc, m, l
+):
     h = pl.program_id(0)
     acc[...] = acc_in[...]
     m[...] = m_in[...]
@@ -200,7 +204,10 @@
             def _(ref=ref, a=a):
                 fwd_block(ref[a + 1, 0], ref[a + 1, 1], None, q, m, l, acc)
 
-    ot_out[...] = (acc[...] * (1.0 / l[0:1, :])).astype(BF16)
+    ot = (acc[...] * (1.0 / l[0:1, :])).astype(BF16)
+    ot_out[...] = ot
+    delta = jnp.sum(ot.astype(F32) * dot[...].astype(F32), axis=0, keepdims=True)
+    delta_out[...] = jnp.broadcast_to(delta, delta_out.shape)
     lse_out[...] = jnp.broadcast_to(m[0:1, :] + jnp.log2(l[0:1, :]), lse_out.shape)
 
 
@@ -242,7 +249,7 @@
     )(info, q, own, up, down, text_keys, text_values, mask)
 
 
-def fwd_side_call(info, q, left, right, acc, m, l):
+def fwd_side_call(info, q, left, right, acc, m, l, dot):
     tile, width = q.shape
     heads = width // HEAD_DIM
     keys = 6 * tile
@@ -257,10 +264,12 @@
             row_spec(HEAD_DIM, tile),
             row_spec(8, tile),
             row_spec(8, tile),
-        ],
-        out_specs=[row_spec(HEAD_DIM, tile), row_spec(8, tile)],
+            row_spec(HEAD_DIM, tile),
+        ],
+        out_specs=[row_spec(HEAD_DIM, tile), row_spec(8, tile), row_spec(8, tile)],
         out_shape=[
             jax.ShapeDtypeStruct((width, tile), BF16),
+            jax.ShapeDtypeStruct((8 * heads, tile), F32),
             jax.ShapeDtypeStruct((8 * heads, tile), F32),
         ],
         scratch_shapes=[
@@ -273,7 +282,7 @@
             flops=4 * tile * keys * width, bytes_accessed=4 * keys * width, transcendentals=0
         ),
         name="fwd_side",
-    )(info, q, left, right, acc, m, l)
+    )(info, q, left, right, acc, m, l, dot)
 
 
 def stack_kernel(up, own, down, out):
@@ -295,94 +304,112 @@
     )(up, own, down)
 
 
-def piece_block(info, flip, ys, xs, x):
-    y = ys - 1 - info[4] if flip else info[4]
-    return y * xs + x
-
-
-def proj_kernel(flip, ys, xs, info, w, gate, ot, piece, *refs):
-    if flip:
-        acc_in, gate_in, dot_out, delta_out, gate_out, acc, gates = refs
-    else:
-        acc, gates = refs
-    x = pl.program_id(0)
-
-    @pl.when(x == 0)
-    def _():
-        acc[...] = acc_in[...] if flip else jnp.zeros(acc.shape, F32)
-        gates[...] = gate_in[...] if flip else jnp.zeros(gates.shape, F32)
-
-    g = piece[0]
-    scaled = (g.astype(F32) * gate[...]).astype(BF16)
-    acc[...] += dot_nt(w[...], scaled)
-    terms = dot_nn(ot[...], g) * w[...].astype(F32)
-    row = jnp.sum(terms, axis=0, keepdims=True)
-    count = g.shape[1] // 128
-    block = piece_block(info, flip, ys, xs, x)
-    for i in range(count):
-        gates[pl.ds(block * count + i, 1), :] = row[:, i * 128 : (i + 1) * 128]
-    if not flip:
-        return
-
-    @pl.when(x == xs - 1)
-    def _():
-        tile = ot.shape[1]
-        rounded = acc[...].astype(BF16)
-        dot_out[...] = rounded
-        prod = rounded.astype(F32) * ot[...].astype(F32)
-        for h in range(ot.shape[0] // HEAD_DIM):
-            d = jnp.sum(prod[h * HEAD_DIM : (h + 1) * HEAD_DIM, :], axis=0, keepdims=True)
-            delta_out[8 * h : 8 * h + 8, :] = jnp.broadcast_to(d, (8, tile))
-        for i in range(gate_out.shape[0]):
-            gate_out[i] = gates[...]
-
-
-def proj_call(flip, sizes, info, w, gate, ot, pieces, carried=()):
+def first_block(info, flip, ys, xs):
+    return (ys - 1 - info[4] if flip else info[4]) * xs
+
+
+def fetch(w, pieces, w_buf, p_buf, sems, slot, block):
+    cols = p_buf.shape[2]
+    at = pl.multiple_of(block * cols, 128)
+    copies = [
+        pltpu.make_async_copy(pieces, p_buf.at[slot], sems.at[2 * slot]),
+        pltpu.make_async_copy(
+            w.at[:, pl.ds(at, cols)], w_buf.at[slot], sems.at[2 * slot + 1]
+        ),
+    ]
+    for copy in copies:
+        copy.start()
+    return copies
+
+
+def proj_kernel(flip, ys, xs, info, w, gate, pieces, *refs):
+    *acc_in, out, w_buf, p_buf, sems = refs
+    start = first_block(info, flip, ys, xs)
+    copies = [
+        fetch(w, pieces.at[x], w_buf, p_buf, sems, x, start + x) for x in range(xs)
+    ]
+    cols = p_buf.shape[2]
+    acc = acc_in[0][...] if acc_in else None
+    for x in range(xs):
+        for copy in copies[x]:
+            copy.wait()
+        at = pl.multiple_of((start + x) * cols, 128)
+        scaled = (p_buf[x].astype(F32) * gate[:, pl.ds(at, cols)]).astype(BF16)
+        part = dot_nt(w_buf[x], scaled)
+        acc = part if acc is None else acc + part
+    out[...] = acc.astype(out.dtype)
+
+
+def proj_call(flip, sizes, info, w, gate, pieces, *acc):
     ys, xs = sizes[3:]
-    width, tile = ot.shape
-    heads = width // HEAD_DIM
-    cols = pieces.shape[2]
-    rows = w.shape[1] // 128
-    acc = jax.ShapeDtypeStruct((width, tile), F32)
-    gates = jax.ShapeDtypeStruct((rows, 128), F32)
-    if flip:
-        out_shape = [
-            jax.ShapeDtypeStruct((width, tile), BF16),
-            jax.ShapeDtypeStruct((8 * heads, tile), F32),
-            jax.ShapeDtypeStruct((ys * xs, rows, 128), F32),
-        ]
-        scratch = [pltpu.VMEM((width, tile), F32), pltpu.VMEM((rows, 128), F32)]
-    else:
-        out_shape = [acc, gates]
-        scratch = []
-
-    def column(x, info_ref):
-        return (0, piece_block(info_ref, flip, ys, xs, x))
-
+    width = w.shape[0]
+    _, tile, cols = pieces.shape
+    vmem = pl.BlockSpec(memory_space=pltpu.VMEM)
+    hbm = pl.BlockSpec(memory_space=pltpu.HBM)
     return pl.pallas_call(
         functools.partial(proj_kernel, flip, ys, xs),
-        grid_spec=pltpu.PrefetchScalarGridSpec(
-            num_scalar_prefetch=1,
-            grid=(xs,),
-            in_specs=[
-                pl.BlockSpec((width, cols), column),
-                pl.BlockSpec((1, cols), column),
-                whole((width, tile)),
-                pl.BlockSpec((1, tile, cols), lambda x, _: (x, 0, 0)),
-            ]
-            + [whole(c.shape) for c in carried],
-            out_specs=[whole(o.shape) for o in out_shape],
-            scratch_shapes=scratch,
-        ),
-        out_shape=out_shape,
-        compiler_params=params("arbitrary"),
+        in_specs=[smem(), hbm, vmem, hbm] + [vmem] * len(acc),
+        out_specs=vmem,
+        out_shape=jax.ShapeDtypeStruct((width, tile), BF16 if flip else F32),
+        scratch_shapes=[
+            pltpu.VMEM((xs, width, cols), BF16),
+            pltpu.VMEM((xs, tile, cols), BF16),
+            pltpu.SemaphoreType.DMA((2 * xs,)),
+        ],
+        compiler_params=params(),
         cost_estimate=pl.CostEstimate(
-            flops=4 * tile * width * cols * xs,
+            flops=2 * tile * width * cols * xs,
             bytes_accessed=2 * (tile + width) * cols * xs,
             transcendentals=0,
         ),
         name="proj",
-    )(info, w, gate, ot, pieces, *carried)
+    )(info, w, gate, pieces, *acc)
+
+
+def gate_kernel(ys, xs, info, w, ot, near, far, out, w_buf, p_buf, sems, gates):
+    jobs = []
+    for flip, pieces in ((False, near), (True, far)):
+        start = first_block(info, flip, ys, xs)
+        for x in range(xs):
+            slot = len(jobs)
+            copies = fetch(w, pieces.at[x], w_buf, p_buf, sems, slot, start + x)
+            jobs.append((slot, start + x, copies))
+    count = p_buf.shape[2] // 128
+    for slot, block, copies in jobs:
+        for copy in copies:
+            copy.wait()
+        terms = dot_nn(ot[...], p_buf[slot]) * w_buf[slot].astype(F32)
+        row = jnp.sum(terms, axis=0, keepdims=True)
+        for i in range(count):
+            gates[pl.ds(block * count + i, 1), :] = row[:, i * 128 : (i + 1) * 128]
+    for i in range(out.shape[0]):
+        out[i] = gates[...]
+
+
+def gate_call(sizes, info, w, ot, near, far):
+    ys, xs = sizes[3:]
+    width, tile = ot.shape
+    cols = near.shape[2]
+    rows = w.shape[1] // 128
+    vmem = pl.BlockSpec(memory_space=pltpu.VMEM)
+    hbm = pl.BlockSpec(memory_space=pltpu.HBM)
+    return pl.pallas_call(
+        functools.partial(gate_kernel, ys, xs),
+        in_specs=[smem(), hbm, vmem, hbm, hbm],
+        out_specs=vmem,
+        out_shape=jax.ShapeDtypeStruct((sizes[2] * ys * xs, rows, 128), F32),
+        scratch_shapes=[
+            pltpu.VMEM((ys * xs, width, cols), BF16),
+            pltpu.VMEM((ys * xs, tile, cols), BF16),
+            pltpu.SemaphoreType.DMA((2 * ys * xs,)),
+            pltpu.VMEM((rows, 128), F32),
+        ],
+        compiler_params=params(),
+        cost_estimate=pl.CostEstimate(
+            flops=2 * tile * w.size, bytes_accessed=2 * w.size, transcendentals=0
+        ),
+        name="gate_terms",
+    )(info, w, ot, near, far)
 
 
 def bwd_math(keys, values, q, dot, lse, delta, dq, extra):
@@ -416,13 +443,14 @@
 
 
 def bwd_side_kernel(
-    info, q, dot, lse, delta, tk, tv, mask, left, right, left_out, right_out, text_out, dq_out
+    info, q, dot, lse, delta, tk, tv, mask, left, right, left_out, right_out, keep, give, dq_out
 ):
     h = pl.program_id(0)
     dq_out[...] = jnp.zeros(dq_out.shape, F32)
     dk, dv = bwd_math(tk[...], tv[...], q, dot, lse, delta, dq_out, mask_column(mask))
-    text_out[0] = dk.astype(BF16)
-    text_out[1] = dv.astype(BF16)
+    first = info[5] == 0
+    keep[...] = jnp.where(first, dk, dv)
+    give[...] = jnp.where(first, dv, dk).astype(BF16)
     for b, ref, out in ((-1, left, left_out), (1, right, right_out)):
         for a in (-1, 0, 1):
             bwd_block(
@@ -469,11 +497,13 @@
         in_specs=bwd_specs(tile)
         + [half_spec(txt), half_spec(txt), whole((1, txt))]
         + [stack_spec(tile)] * 2,
-        out_specs=[stack_spec(tile)] * 2 + [kv_spec(txt), row_spec(HEAD_DIM, tile)],
+        out_specs=[stack_spec(tile)] * 2
+        + [half_spec(txt), half_spec(txt), row_spec(HEAD_DIM, tile)],
         out_shape=[
             stack,
             stack,
-            jax.ShapeDtypeStruct((2, txt, width), BF16),
+            jax.ShapeDtypeStruct((txt, width), F32),
+            jax.ShapeDtypeStruct((txt, width), BF16),
             jax.ShapeDtypeStruct((width, tile), F32),
         ],
         compiler_params=params("arbitrary"),
@@ -486,7 +516,6 @@
     info, q, dot, lse, delta = common
     tile, width = q.shape
     table = whole((tile, HEAD_DIM))
-    part = jax.ShapeDtypeStruct((2, tile, width), F32)
     return pl.pallas_call(
         bwd_near_kernel,
         grid=(width // HEAD_DIM,),
@@ -494,7 +523,12 @@
         + [row_spec(HEAD_DIM, tile), table, table]
         + [kv_spec(tile)] * 3,
         out_specs=[kv_spec(tile)] * 3 + [half_spec(tile)],
-        out_shape=[part, part, part, jax.ShapeDtypeStruct((tile, width), BF16)],
+        out_shape=[
+            jax.ShapeDtypeStruct((2, tile, width), BF16),
+            jax.ShapeDtypeStruct((2, tile, width), F32),
+            jax.ShapeDtypeStruct((2, tile, width), BF16),
+            jax.ShapeDtypeStruct((tile, width), BF16),
+        ],
         scratch_shapes=[pltpu.VMEM((HEAD_DIM, tile), F32)],
         compiler_params=params("arbitrary"),
         cost_estimate=bwd_cost(tile, 3 * tile, width),
@@ -502,23 +536,29 @@
     )(info, q, dot, lse, delta, dq, cos, sin, up, own, down)
 
 
-def pair_sum_kernel(up, down, left, right, up_out, down_out):
-    for i, part, out in ((0, up, up_out), (2, down, down_out)):
-        out[...] = (part[...] + left[i].astype(F32) + right[i].astype(F32)).astype(BF16)
+def pair_sum_kernel(up, down, up_l, up_r, down_l, down_r, up_out, down_out):
+    for part, left, right, out in (
+        (up, up_l, up_r, up_out),
+        (down, down_l, down_r, down_out),
+    ):
+        total = part[...].astype(F32) + left[0].astype(F32) + right[0].astype(F32)
+        out[...] = total.astype(BF16)
 
 
 def pair_sum_call(up, down, left, right):
     tile, width = up.shape[1:]
     shape = jax.ShapeDtypeStruct((2, tile, width), BF16)
+    top = pl.BlockSpec((1, 2, tile, HEAD_DIM), lambda h: (0, 0, 0, h))
+    bottom = pl.BlockSpec((1, 2, tile, HEAD_DIM), lambda h: (2, 0, 0, h))
     return pl.pallas_call(
         pair_sum_kernel,
         grid=(width // HEAD_DIM,),
-        in_specs=[kv_spec(tile)] * 2 + [stack_spec(tile)] * 2,
+        in_specs=[kv_spec(tile)] * 2 + [top, top, bottom, bottom],
         out_specs=[kv_spec(tile)] * 2,
         out_shape=[shape] * 2,
         compiler_params=params("arbitrary"),
         name="pair_sum",
-    )(up, down, left, right)
+    )(up, down, left, right, left, right)
 
 
 def finish_kernel(own, left, right, up, down, cos, sin, gk_out, gv_out):
@@ -552,10 +592,11 @@
     return hi, (values - hi.astype(F32)).astype(BF16)
 
 
-def pack_kernel(text, gate, out):
+def pack_kernel(keep, got, gate, out):
     groups, rows, _ = out.shape
-    width = text.shape[1]
-    out[:, :, :width] = text[...].reshape(groups, rows, width)
+    width = keep.shape[1]
+    text = (keep[...] + got[...].astype(F32)).astype(BF16)
+    out[:, :, :width] = text.reshape(groups, rows, width)
     out[:, :, width:] = jnp.zeros((groups, rows, 128), BF16)
     hi, lo = split_pair(jnp.sum(gate[...], axis=0))
     for i in range(gate.shape[1]):
@@ -563,16 +604,16 @@
         out[i, 1:2, width:] = lo[i : i + 1, :]
 
 
-def pack_call(text, gate, groups):
-    rows = text.shape[0] // groups
+def pack_call(keep, got, gate, groups):
+    txt, width = keep.shape
     return pl.pallas_call(
         pack_kernel,
-        in_specs=[pl.BlockSpec(memory_space=pltpu.VMEM)] * 2,
+        in_specs=[pl.BlockSpec(memory_space=pltpu.VMEM)] * 3,
         out_specs=pl.BlockSpec(memory_space=pltpu.VMEM),
-        out_shape=jax.ShapeDtypeStruct((groups, rows, text.shape[1] + 128), BF16),
+        out_shape=jax.ShapeDtypeStruct((groups, txt // groups, width + 128), BF16),
         compiler_params=params(limit=SMALL),
         name="pack",
-    )(text, gate)
+    )(keep, got, gate)
 
 
 def chunk_sum_kernel(width, got, out):
@@ -594,17 +635,15 @@
         in_specs=[pl.BlockSpec(memory_space=pltpu.VMEM)],
         out_specs=pl.BlockSpec(memory_space=pltpu.VMEM),
         out_shape=jax.ShapeDtypeStruct(got.shape, BF16),
-        compiler_params=params(limit=SMALL),
+        compiler_params=params(),
         name="chunk_sum",
     )(got)
 
 
-def unpack_kernel(got, keys_out, values_out, gate_out):
+def unpack_kernel(got, text_out, gate_out):
     groups, rows, _ = got.shape
-    width = keys_out.shape[1]
-    half = groups // 2
-    keys_out[...] = got[:half, :, :width].reshape(half * rows, width)
-    values_out[...] = got[half:, :, :width].reshape(half * rows, width)
+    width = text_out.shape[1]
+    text_out[...] = got[:, :, :width].reshape(groups * rows, width)
     for i in range(gate_out.shape[0]):
         pair = got[i, :, width:].astype(F32)
         gate_out[i : i + 1, :] = pair[0:1, :] + pair[1:2, :]
@@ -612,15 +651,37 @@
 
 def unpack_call(got, width, gate_rows):
     groups, rows, _ = got.shape
-    text = jax.ShapeDtypeStruct((groups // 2 * rows, width), BF16)
+    vmem = pl.BlockSpec(memory_space=pltpu.VMEM)
     return pl.pallas_call(
         unpack_kernel,
-        in_specs=[pl.BlockSpec(memory_space=pltpu.VMEM)],
-        out_specs=[pl.BlockSpec(memory_space=pltpu.VMEM)] * 3,
-        out_shape=[text, text, jax.ShapeDtypeStruct((gate_rows, 128), F32)],
+        in_specs=[vmem],
+        out_specs=[vmem, vmem],
+        out_shape=[
+            jax.ShapeDtypeStruct((groups * rows, width), BF16),
+            jax.ShapeDtypeStruct((gate_rows, 128), F32),
+        ],
         compiler_params=params(limit=SMALL),
         name="unpack",
     )(got)
+
+
+def choose_kernel(info, own, other, keys_out, values_out):
+    first = info[5] == 0
+    keys_out[...] = jnp.where(first, own[...], other[...])
+    values_out[...] = jnp.where(first, other[...], own[...])
+
+
+def choose_call(info, own, other):
+    vmem = pl.BlockSpec(memory_space=pltpu.VMEM)
+    shape = jax.ShapeDtypeStruct(own.shape, BF16)
+    return pl.pallas_call(
+        choose_kernel,
+        in_specs=[smem(), vmem, vmem],
+        out_specs=[vmem, vmem],
+        out_shape=[shape, shape],
+        compiler_params=params(limit=SMALL),
+        name="choose",
+    )(info, own, other)
 
 
 def shift(array, axis, by, wrap=False):
@@ -653,38 +714,39 @@
     grad_out,
 ):
     _, width = query_in.shape
-    seq_count = lax.axis_size(SEQ)
     sizes = tuple(lax.axis_size(axis) for axis in (*SEQ, *HEAD))
     mask = text_mask.reshape(1, -1)
+    gate = gate_scale.reshape(1, -1)
 
     g_y = swap(grad_out, "yhi", 1)
     g_x = spread(grad_out, "x")
 
-    q, kv, cos, sin, info = rotate_call(sizes, window_reach, tile_map, query_in, key_in, value_in)
+    q, kv, cos, sin, info = rotate_call(
+        sizes, window_reach, tile_map, query_in, key_in, value_in
+    )
 
     kv_up, kv_down = shift(kv, "z", 1), shift(kv, "z", -1)
+    gy_x = spread(g_y, "x")
     stack = stack_call(kv_up, kv, kv_down)
     kv_left, kv_right = shift(stack, COL, 1), shift(stack, COL, -1)
-    gy_x = spread(g_y, "x")
 
     partial = fwd_near_call(info, q, kv, kv_up, kv_down, text_keys, text_values, mask)
-    ot, lse = fwd_side_call(info, q, kv_left, kv_right, *partial)
-
-    gate = gate_scale.reshape(1, -1)
-    carried = proj_call(False, sizes, info, out_weight, gate, ot, g_x)
-    dot, delta, gate_terms = proj_call(
-        True, sizes, info, out_weight, gate, ot, gy_x, carried
-    )
-    gate_terms = lax.all_to_all(gate_terms, HEAD, 0, 0, tiled=True)
+    acc = proj_call(False, sizes, info, out_weight, gate, g_x)
+    dot = proj_call(True, sizes, info, out_weight, gate, gy_x, acc)
+    ot, lse, delta = fwd_side_call(info, q, kv_left, kv_right, *partial, dot)
+
+    gate_terms = gate_call(sizes, info, out_weight, ot, g_x, gy_x)
+    gate_terms = lax.all_to_all(gate_terms, ("core", *HEAD), 0, 0, tiled=True)
 
     common = (info, q, dot, lse, delta)
-    left, right, text_part, dq = bwd_side_call(
+    left, right, keep, give, dq = bwd_side_call(
         common, text_keys, text_values, mask, kv_left, kv_right
     )
+    taken = swap(give, "core", 1)
     back_left = shift(left, COL, -1)
     back_right = shift(right, COL, 1)
-    packed = pack_call(text_part.reshape(-1, width), gate_terms, seq_count)
-    got = lax.all_to_all(packed, SEQ, 0, 0, tiled=True)
+    packed = pack_call(keep, taken, gate_terms, lax.axis_size(CHIPS))
+    got = lax.all_to_all(packed, CHIPS, 0, 0, tiled=True)
     up, own, down, grad_query = bwd_near_call(common, dq, cos, sin, kv_up, kv, kv_down)
 
     up, down = pair_sum_call(up, down, back_left, back_right)
@@ -692,11 +754,11 @@
     down = shift(down, "z", 1)
 
     chunk = chunk_sum_call(got, width)
-    summed = lax.all_to_all(chunk, SEQ, 0, 0, tiled=True)
-    grad_text_keys, grad_text_values, grad_gate = unpack_call(
-        summed, width, out_weight.shape[1] // 128
-    )
+    summed = lax.all_to_all(chunk, CHIPS, 0, 0, tiled=True)
+    own_text, grad_gate = unpack_call(summed, width, out_weight.shape[1] // 128)
+    other_text = swap(own_text, "core", 1)
     grad_key, grad_value = finish_call(own, back_left, back_right, up, down, cos, sin)
+    grad_text_keys, grad_text_values = choose_call(info, own_text, other_text)
     return (
         grad_query,
         grad_key,

time: 179 us -> 159 us (0.89)
  the two profiles are of different devices: /device:TPU:68 before, /device:TPU:64 now
where the time goes in v2:
time: 159 us; the launch traced here: 158 us
  starting transfers between devices  58.8 us (37%)
  Pallas kernels  43.8 us (28%)
  blocking collectives  25.3 us (16%)
  waiting for transfers between devices  23.3 us (15%)
  local copies, waits for them, and re-layouts  6.12 us (4%)
    ppermute x8, starting transfers between devices, shift(): return lax.ppermute(array, axis, pairs)  25.4 us
    all_to_all x1, blocking collectives, on_device(): got = lax.all_to_all(packed, CHIPS, 0, 0, tiled=True)  25.3 us
    all_to_all x1, starting transfers between devices, on_device(): gate_terms = lax.all_to_all(gate_terms, ('core', *HEAD), 0, 0, tiled=True)  10.4 us
    ppermute x3, starting transfers between devices, swap(): return lax.ppermute(array, axis, [(i, i ^ bit) for i in range(length)])  9.34 us
    all_to_all x2, starting transfers between devices, spread(): return lax.all_to_all(copies, axis, 0, 0, tiled=True)  8.88 us
    pallas_call x2, Pallas kernels, proj_call(): pl.pallas_call(functools.partial(proj_kernel, flip, ys, xs), in_specs=[sm...  7.87 us
    all_to_all x1, waiting for transfers between devices, on_device(): gate_terms = lax.all_to_all(gate_terms, ('core', *HEAD), 0, 0, tiled=True)  7.76 us
    ppermute x8, waiting for transfers between devices, shift(): return lax.ppermute(array, axis, pairs)  5.9 us
  transfers between devices with their start and end apart: 15, of which 8 were waited for; matrix products, arithmetic and copies ran while one was open for 1% of the time, Pallas kernels for 21%

profile of v2, /device:TPU:64, one launch (start us, length us, event | category | flops | bytes accessed | tf_op | source)
XLA Modules:
  0.0 158.2 jit_solution(3040231743371841028)
XLA Ops:
  0.6 2.1 %broadcast_in_dim.5 = bf16[4,384,384]{2,1,0:T(8,128)(2,1)} broadcast(bf16[384,384]{1,0:T(8,128)(2,1)} %param.22), dimensions={1,2} | broadcast | bytes 1474560 | tf_op jit(solution)/shard_map/broadcast_in_dim | solution.py:699
  2.7 0.0 copy-start.8
  2.7 4.4 %all-to-all-start.1 = ((bf16[4,384,384]{2,1,0:T(8,128)(2,1)}), bf16[4,384,384]{2,1,0:T(8,128)(2,1)}, u32[]{:S(2)}, u32[]{:S(2)}) async-start(bf16[4,384,384]{2,1,0:T(8,128)(2,1)} %broadcast_in_dim.5), calls=%async_computation.1 | async-start | bytes 2359296 | tf_op jit(solution)/shard_map/all_to_all | solution.py:700
  7.1 2.5 %rot.1 = (bf16[384,256]{1,0:T(8,128)(2,1)}, bf16[2,384,256]{2,1,0:T(8,128)(2,1)}, f32[384,128]{1,0:T(8,128)}, f32[384,128]{1,0:T(8,128)}, s32[24]{0:T(128)}) custom-call(s32[2,2]{1,0:T(2,128)} %reach.1, s32[3,64]{1,0:T(4,128)} %bitcast.6, f32[8,128]{1,0:T(8,128)} %constant.2.clone.freq, bf16[384,256]{1,0:T(8,128)(2,1)} %q.1, bf16[384,256]{1,0:T(8,128)(2,1)} %k.1, ...), custom_call_target="tpu_custom_call" | custom-call | tf_op jit(solution)/shard_map/rot/pallas_call | solution.py:133
  9.6 6.9 %collective-permute-start.2 = (bf16[2,384,256]{2,1,0:T(8,128)(2,1)}, bf16[2,384,256]{2,1,0:T(8,128)(2,1)S(1)}, u32[]{:S(2)}, u32[]{:S(2)}) collective-permute-start(bf16[2,384,256]{2,1,0:T(8,128)(2,1)} %get-tuple-element.36.own), channel_id=1, source_target_pairs={{64,0},{128,64},{192,128},{256,192},{320,256},{384,320},{448,384},... | collective-permute-start | bytes 1179656 | tf_op jit(solution)/shard_map/ppermute | solution.py:690
  16.5 1.9 %collective-permute-start.1 = (bf16[2,384,256]{2,1,0:T(8,128)(2,1)}, bf16[2,384,256]{2,1,0:T(8,128)(2,1)S(1)}, u32[]{:S(2)}, u32[]{:S(2)}) collective-permute-start(bf16[2,384,256]{2,1,0:T(8,128)(2,1)} %get-tuple-element.36.own), channel_id=1, source_target_pairs={{0,64},{64,128},{128,192},{192,256},{256,320},{320,384},{384,448},... | collective-permute-start | bytes 1179656 | tf_op jit(solution)/shard_map/ppermute | solution.py:690
  18.5 0.0 copy-done.8
  18.5 5.1 %collective-permute-start = (bf16[384,384]{1,0:T(8,128)(2,1)S(1)}, bf16[384,384]{1,0:T(8,128)(2,1)S(1)}, u32[]{:S(2)}, u32[]{:S(2)}) collective-permute-start(bf16[384,384]{1,0:T(8,128)(2,1)S(1)} %copy-done.8), channel_id=1, source_target_pairs={{0,4},{4,0},{1,5},{5,1},{2,6},{6,2},{3,7},{7,3},{8,12},{12,8},{9,1... | collective-permute-start | bytes 884744 | tf_op jit(solution)/shard_map/ppermute | solution.py:695
  23.6 0.0 collective-permute-done.2.down
  23.6 0.0 copy-start.2
  23.6 2.8 %collective-permute-done.1.up = bf16[2,384,256]{2,1,0:T(8,128)(2,1)S(1)} collective-permute-done((bf16[2,384,256]{2,1,0:T(8,128)(2,1)}, bf16[2,384,256]{2,1,0:T(8,128)(2,1)S(1)}, u32[]{:S(2)}, u32[]{:S(2)}) %collective-permute-start.1) | collective-permute-done | bytes 393248 | tf_op jit(solution)/shard_map/ppermute | solution.py:690
  26.4 0.0 copy-start.1
  26.4 1.0 copy-done.1
  27.4 0.0 copy-start.3
  27.4 1.3 stack.1
  28.8 1.3 collective-permute-start.4
  30.0 4.1 %collective-permute-start.3 = (bf16[3,2,384,256]{3,2,1,0:T(8,128)(2,1)}, bf16[3,2,384,256]{3,2,1,0:T(8,128)(2,1)}, u32[]{:S(2)}, u32[]{:S(2)}) collective-permute-start(bf16[3,2,384,256]{3,2,1,0:T(8,128)(2,1)} %stack.1), channel_id=1, source_target_pairs={{0,8},{8,16},{16,24},{24,32},{32,40},{40,48},{48,56},{1,9},{9,17},... | collective-permute-start | bytes 3538952 | tf_op jit(solution)/shard_map/ppermute | solution.py:690
  34.1 1.8 %collective-permute-done = bf16[384,384]{1,0:T(8,128)(2,1)S(1)} collective-permute-done((bf16[384,384]{1,0:T(8,128)(2,1)S(1)}, bf16[384,384]{1,0:T(8,128)(2,1)S(1)}, u32[]{:S(2)}, u32[]{:S(2)}) %collective-permute-start) | collective-permute-done | bytes 294944 | tf_op jit(solution)/shard_map/ppermute | solution.py:695
  36.0 0.0 all-to-all-done.1.pieces.near
  36.0 1.2 broadcast_in_dim.4
  37.1 0.0 copy-done.2
  37.1 0.0 copy-done.3
  37.1 4.5 %all-to-all-start = ((bf16[4,384,384]{2,1,0:T(8,128)(2,1)}), bf16[4,384,384]{2,1,0:T(8,128)(2,1)}, u32[]{:S(2)}, u32[]{:S(2)}) async-start(bf16[4,384,384]{2,1,0:T(8,128)(2,1)} %broadcast_in_dim.4), calls=%async_computation | async-start | bytes 2359296 | tf_op jit(solution)/shard_map/all_to_all | solution.py:700
  41.6 4.9 %fwd_near.1 = (f32[256,384]{1,0:T(8,128)}, f32[16,384]{1,0:T(8,128)}, f32[16,384]{1,0:T(8,128)}) custom-call(s32[24]{0:T(128)} %get-tuple-element.34.info, bf16[384,256]{1,0:T(8,128)(2,1)} %get-tuple-element.35.q, bf16[2,384,256]{2,1,0:T(8,128)(2,1)} %get-tuple-element.36.own, bf16[2,384,256]{2,1,0:T(8,128)(2,1)} %copy-done.3, ...), custom_call_target="tpu_custom_call" | custom-call | flops 553648128 | bytes 1441792 | tf_op jit(solution)/shard_map/fwd_near/pallas_call | solution.py:236
  46.5 3.8 %proj.2.refs_0_ = f32[256,384]{1,0:T(8,128)} custom-call(s32[24]{0:T(128)} %get-tuple-element.34.info, bf16[256,3072]{1,0:T(8,128)(2,1)} %w.5, f32[1,3072]{1,0:T(1,128)} %bitcast.4, bf16[4,384,384]{2,1,0:T(8,128)(2,1)} %all-to-all-done.1.pieces.near), custom_call_target="tpu_custom_call" | custom-call | flops 301989888 | bytes 1966080 | tf_op jit(solution)/shard_map/proj/pallas_call | solution.py:349
  50.3 5.5 %all-to-all-done.pieces.far = bf16[4,384,384]{2,1,0:T(8,128)(2,1)} async-done(((bf16[4,384,384]{2,1,0:T(8,128)(2,1)}), bf16[4,384,384]{2,1,0:T(8,128)(2,1)}, u32[]{:S(2)}, u32[]{:S(2)}) %all-to-all-start) | async-done | bytes 1179680 | tf_op jit(solution)/shard_map/all_to_all | solution.py:700
  55.8 4.1 %proj.3.dot = bf16[256,384]{1,0:T(8,128)(2,1)} custom-call(s32[24]{0:T(128)} %get-tuple-element.34.info, bf16[256,3072]{1,0:T(8,128)(2,1)} %w.5, f32[1,3072]{1,0:T(1,128)} %bitcast.5, bf16[4,384,384]{2,1,0:T(8,128)(2,1)} %all-to-all-done.pieces.far, f32[256,384]{1,0:T(8,128)} %proj.2.refs_0_), custom_call_target="tpu_custom_call" | custom-call | flops 301989888 | bytes 1966080 | tf_op jit(solution)/shard_map/proj/pallas_call | solution.py:349
  59.9 0.0 collective-permute-done.4.right
  59.9 0.0 collective-permute-done.3.left
  59.9 3.2 %fwd_side.1 = (bf16[256,384]{1,0:T(8,128)(2,1)}, f32[16,384]{1,0:T(8,128)}, f32[16,384]{1,0:T(8,128)}) custom-call(s32[24]{0:T(128)} %get-tuple-element.34.info, bf16[384,256]{1,0:T(8,128)(2,1)} %get-tuple-element.35.q, bf16[3,2,384,256]{3,2,1,0:T(8,128)(2,1)} %collective-permute-done.3.left, bf16[3,2,384,256]{3,2,1,0:T(8,128)(2,1)} %collective-permute-done.4.right, ...), custom_call_target="tpu_custom_call" | custom-call | flops 905969664 | bytes 2359296 | tf_op jit(solution)/shard_map/fwd_side/pallas_call | solution.py:256
  63.1 4.8 %bwd_side.1 = (bf16[3,2,384,256]{3,2,1,0:T(8,128)(2,1)}, bf16[3,2,384,256]{3,2,1,0:T(8,128)(2,1)}, f32[256,256]{1,0:T(8,128)}, bf16[256,256]{1,0:T(8,128)(2,1)}, f32[256,384]{1,0:T(8,128)}) custom-call(s32[24]{0:T(128)} %get-tuple-element.34.info, bf16[384,256]{1,0:T(8,128)(2,1)} %get-tuple-element.35.q, bf16[256,384]{1,0:T(8,128)(2,1)} %proj.3.dot, ...), custom_call_target="tpu_custom_call" | custom-call | flops 2516582400 | bytes 5242880 | tf_op jit(solution)/shard_map/bwd_side/pallas_call | solution.py:494
  67.9 1.3 collective-permute-start.5
  69.2 4.1 %collective-permute-start.6 = (bf16[3,2,384,256]{3,2,1,0:T(8,128)(2,1)}, bf16[3,2,384,256]{3,2,1,0:T(8,128)(2,1)}, u32[]{:S(2)}, u32[]{:S(2)}) collective-permute-start(bf16[3,2,384,256]{3,2,1,0:T(8,128)(2,1)} %get-tuple-element.48), channel_id=1, source_target_pairs={{0,8},{8,16},{16,24},{24,32},{32,40},{40,48},{48,56},{1,9},{9,17},... | collective-permute-start | bytes 3538952 | tf_op jit(solution)/shard_map/ppermute | solution.py:690
  73.3 5.2 %gate_terms.1 = f32[16,24,128]{2,1,0:T(8,128)} custom-call(s32[24]{0:T(128)} %get-tuple-element.34.info, bf16[256,3072]{1,0:T(8,128)(2,1)} %w.5, bf16[256,384]{1,0:T(8,128)(2,1)} %get-tuple-element.57.ot, bf16[4,384,384]{2,1,0:T(8,128)(2,1)} %all-to-all-done.1.pieces.near, bf16[4,384,384]{2,1,0:T(8,128)(2,1)} %all-to-all-done.pieces.far), custom_call_target="tpu_custom_call" | custom-call | flops 603979776 | bytes 1572864 | tf_op jit(solution)/shard_map/gate_terms/pallas_call | solution.py:396
  78.5 10.4 %all-to-all-start.2 = ((f32[16,24,128]{2,1,0:T(8,128)}), f32[16,24,128]{2,1,0:T(8,128)S(1)}, u32[]{:S(2)}, u32[]{:S(2)}) async-start(f32[16,24,128]{2,1,0:T(8,128)} %gate_terms.1), calls=%async_computation.2 | async-start | bytes 393216 | tf_op jit(solution)/shard_map/all_to_all | solution.py:739
  89.0 0.0 copy-done.9
  89.0 2.3 %collective-permute-start.9 = (bf16[256,256]{1,0:T(8,128)(2,1)S(1)}, bf16[256,256]{1,0:T(8,128)(2,1)S(1)}, u32[]{:S(2)}, u32[]{:S(2)}) collective-permute-start(bf16[256,256]{1,0:T(8,128)(2,1)S(1)} %copy-done.9), channel_id=1, source_target_pairs={{0,8},{8,0},{1,9},{9,1},{2,10},{10,2},{3,11},{11,3},{4,12},{12,4},... | collective-permute-start | bytes 393224 | tf_op jit(solution)/shard_map/ppermute | solution.py:695
  91.3 1.0 collective-permute-done.9.got
  92.3 7.8 %all-to-all-done.2.gate = f32[16,24,128]{2,1,0:T(8,128)S(1)} async-done(((f32[16,24,128]{2,1,0:T(8,128)}), f32[16,24,128]{2,1,0:T(8,128)S(1)}, u32[]{:S(2)}, u32[]{:S(2)}) %all-to-all-start.2) | async-done | bytes 196640 | tf_op jit(solution)/shard_map/all_to_all | solution.py:739
  100.0 0.0 copy-done.4
  100.0 0.1 pack.1
  100.1 25.3 %all_to_all.25.got = bf16[32,8,384]{2,1,0:T(8,128)(2,1)} all-to-all(bf16[32,8,384]{2,1,0:T(8,128)(2,1)S(1)} %pack.1), channel_id=1, replica_groups=mesh['z'=8,'y'=4,'core'=2,'yhi'=2,'x'=4] {'z','y'}, dimensions={0} | all-to-all | bytes 393216 | tf_op jit(solution)/shard_map/all_to_all | solution.py:749
  125.5 1.7 %chunk_sum.1 = bf16[32,8,384]{2,1,0:T(8,128)(2,1)} custom-call(bf16[32,8,384]{2,1,0:T(8,128)(2,1)} %all_to_all.25.got), custom_call_target="tpu_custom_call" | custom-call | tf_op jit(solution)/shard_map/chunk_sum/pallas_call | solution.py:633
  127.1 4.8 %all-to-all-start.4 = ((bf16[32,8,384]{2,1,0:T(8,128)(2,1)}), bf16[32,8,384]{2,1,0:T(8,128)(2,1)S(1)}, u32[]{:S(2)}, u32[]{:S(2)}) async-start(bf16[32,8,384]{2,1,0:T(8,128)(2,1)} %chunk_sum.1), calls=%async_computation.4 | async-start | bytes 393216 | tf_op jit(solution)/shard_map/all_to_all | solution.py:757
  131.9 5.3 %bwd_near.1 = (bf16[2,384,256]{2,1,0:T(8,128)(2,1)}, f32[2,384,256]{2,1,0:T(8,128)}, bf16[2,384,256]{2,1,0:T(8,128)(2,1)}, bf16[384,256]{1,0:T(8,128)(2,1)}) custom-call(s32[24]{0:T(128)} %get-tuple-element.34.info, bf16[384,256]{1,0:T(8,128)(2,1)} %get-tuple-element.35.q, bf16[256,384]{1,0:T(8,128)(2,1)} %proj.3.dot, f32[16,384]{1,0:T(8,128)} %get-tuple-element.40.lse, ...), custom_call_target="tpu_custom_call" | custom-call | flops 1132462080 | bytes 2359296 | tf_op jit(solution)/shard_map/bwd_near/pallas_call | solution.py:519
  137.2 0.0 collective-permute-done.5.up_l.down_l.left
  137.2 0.0 collective-permute-done.6.up_r.down_r.right
  137.2 0.0 copy-start.7
  137.2 0.0 copy-start
  137.2 2.7 %pair_sum.1 = (bf16[2,384,256]{2,1,0:T(8,128)(2,1)}, bf16[2,384,256]{2,1,0:T(8,128)(2,1)}) custom-call(bf16[2,384,256]{2,1,0:T(8,128)(2,1)} %get-tuple-element.49.up, bf16[2,384,256]{2,1,0:T(8,128)(2,1)} %get-tuple-element.50.down, bf16[3,2,384,256]{3,2,1,0:T(8,128)(2,1)} %collective-permute-done.5.up_l.down_l.left, ...), custom_call_target="tpu_custom_call" | custom-call | tf_op jit(solution)/shard_map/pair_sum/pallas_call | solution.py:553
  139.9 1.9 %collective-permute-start.7 = (bf16[2,384,256]{2,1,0:T(8,128)(2,1)}, bf16[2,384,256]{2,1,0:T(8,128)(2,1)S(1)}, u32[]{:S(2)}, u32[]{:S(2)}) collective-permute-start(bf16[2,384,256]{2,1,0:T(8,128)(2,1)} %get-tuple-element.51), channel_id=1, source_target_pairs={{64,0},{128,64},{192,128},{256,192},{320,256},{384,320},{448,384},... | collective-permute-start | bytes 1179656 | tf_op jit(solution)/shard_map/ppermute | solution.py:690
  141.8 3.9 %collective-permute-start.8 = (bf16[2,384,256]{2,1,0:T(8,128)(2,1)}, bf16[2,384,256]{2,1,0:T(8,128)(2,1)S(1)}, u32[]{:S(2)}, u32[]{:S(2)}) collective-permute-start(bf16[2,384,256]{2,1,0:T(8,128)(2,1)} %get-tuple-element.52), channel_id=1, source_target_pairs={{0,64},{64,128},{128,192},{192,256},{256,320},{320,384},{384,448},... | collective-permute-start | bytes 1179656 | tf_op jit(solution)/shard_map/ppermute | solution.py:690
  145.7 0.0 all-to-all-done.4.got
  145.7 0.6 unpack.1
  146.4 1.9 %collective-permute-start.10 = (bf16[256,256]{1,0:T(8,128)(2,1)S(1)}, bf16[256,256]{1,0:T(8,128)(2,1)S(1)}, u32[]{:S(2)}, u32[]{:S(2)}) collective-permute-start(bf16[256,256]{1,0:T(8,128)(2,1)S(1)} %get-tuple-element.58.own), channel_id=1, source_target_pairs={{0,8},{8,0},{1,9},{9,1},{2,10},{10,2},{3,11},{11,3},{4,12},{12,4},... | collective-permute-start | bytes 393224 | tf_op jit(solution)/shard_map/ppermute | solution.py:695
  148.3 1.3 collective-permute-done.10.other
  149.6 0.0 copy-done.7
  149.6 1.3 choose.1
  150.9 1.2 collective-permute-done.7.up
  152.0 1.9 %collective-permute-done.8.down = bf16[2,384,256]{2,1,0:T(8,128)(2,1)S(1)} collective-permute-done((bf16[2,384,256]{2,1,0:T(8,128)(2,1)}, bf16[2,384,256]{2,1,0:T(8,128)(2,1)S(1)}, u32[]{:S(2)}, u32[]{:S(2)}) %collective-permute-start.8) | collective-permute-done | bytes 393248 | tf_op jit(solution)/shard_map/ppermute | solution.py:690
  153.9 0.0 copy-done
  153.9 0.9 copy-done.5
  154.9 0.9 copy-done.6
  155.8 2.4 %finish.1 = (bf16[384,256]{1,0:T(8,128)(2,1)}, bf16[384,256]{1,0:T(8,128)(2,1)}) custom-call(f32[2,384,256]{2,1,0:T(8,128)S(1)} %copy-done, bf16[3,2,384,256]{3,2,1,0:T(8,128)(2,1)} %collective-permute-done.5.up_l.down_l.left, bf16[3,2,384,256]{3,2,1,0:T(8,128)(2,1)} %collective-permute-done.6.up_r.down_r.right, ...), custom_call_target="tpu_custom_call" | custom-call | tf_op jit(solution)/shard_map/finish/pallas_call | solution.py:579
  (4 shorter events, 0.0 us)
Async XLA Ops:
  2.7 15.8 %copy-start.8 = (bf16[384,384]{1,0:T(8,128)(2,1)S(1)}, bf16[384,384]{1,0:T(8,128)(2,1)}, u32[]{:S(2)}) copy-start(bf16[384,384]{1,0:T(8,128)(2,1)} %param.22) | copy-start | bytes 884740
  2.7 33.2 %all-to-all-start.1 = ((bf16[4,384,384]{2,1,0:T(8,128)(2,1)}), bf16[4,384,384]{2,1,0:T(8,128)(2,1)}, u32[]{:S(2)}, u32[]{:S(2)}) async-start(bf16[4,384,384]{2,1,0:T(8,128)(2,1)} %broadcast_in_dim.5), calls=%async_computation.1 | async-start | bytes 2359296 | tf_op jit(solution)/shard_map/all_to_all | solution.py:700
  9.6 14.0 %collective-permute-start.2 = (bf16[2,384,256]{2,1,0:T(8,128)(2,1)}, bf16[2,384,256]{2,1,0:T(8,128)(2,1)S(1)}, u32[]{:S(2)}, u32[]{:S(2)}) collective-permute-start(bf16[2,384,256]{2,1,0:T(8,128)(2,1)} %get-tuple-element.36.own), channel_id=1, source_target_pairs={{64,0},{128,64},{192,128},{256,192},{320,256},{384,320},{448,384},... | collective-permute-start | bytes 1179656 | tf_op jit(solution)/shard_map/ppermute | solution.py:690
  16.5 9.9 %collective-permute-start.1 = (bf16[2,384,256]{2,1,0:T(8,128)(2,1)}, bf16[2,384,256]{2,1,0:T(8,128)(2,1)S(1)}, u32[]{:S(2)}, u32[]{:S(2)}) collective-permute-start(bf16[2,384,256]{2,1,0:T(8,128)(2,1)} %get-tuple-element.36.own), channel_id=1, source_target_pairs={{0,64},{64,128},{128,192},{192,256},{256,320},{320,384},{384,448},... | collective-permute-start | bytes 1179656 | tf_op jit(solution)/shard_map/ppermute | solution.py:690
  18.5 17.5 %collective-permute-start = (bf16[384,384]{1,0:T(8,128)(2,1)S(1)}, bf16[384,384]{1,0:T(8,128)(2,1)S(1)}, u32[]{:S(2)}, u32[]{:S(2)}) collective-permute-start(bf16[384,384]{1,0:T(8,128)(2,1)S(1)} %copy-done.8), channel_id=1, source_target_pairs={{0,4},{4,0},{1,5},{5,1},{2,6},{6,2},{3,7},{7,3},{8,12},{12,8},{9,1... | collective-permute-start | bytes 884744 | tf_op jit(solution)/shard_map/ppermute | solution.py:695
  23.6 13.5 %copy-start.2 = (bf16[2,384,256]{2,1,0:T(8,128)(2,1)}, bf16[2,384,256]{2,1,0:T(8,128)(2,1)S(1)}, u32[]{:S(2)}) copy-start(bf16[2,384,256]{2,1,0:T(8,128)(2,1)S(1)} %collective-permute-done.2.down) | copy-start | bytes 1179652
  26.4 1.0 copy-start.1
  27.4 9.7 %copy-start.3 = (bf16[2,384,256]{2,1,0:T(8,128)(2,1)}, bf16[2,384,256]{2,1,0:T(8,128)(2,1)S(1)}, u32[]{:S(2)}) copy-start(bf16[2,384,256]{2,1,0:T(8,128)(2,1)S(1)} %collective-permute-done.1.up) | copy-start | bytes 1179652
  28.8 31.1 %collective-permute-start.4 = (bf16[3,2,384,256]{3,2,1,0:T(8,128)(2,1)}, bf16[3,2,384,256]{3,2,1,0:T(8,128)(2,1)}, u32[]{:S(2)}, u32[]{:S(2)}) collective-permute-start(bf16[3,2,384,256]{3,2,1,0:T(8,128)(2,1)} %stack.1), channel_id=1, source_target_pairs={{8,0},{16,8},{24,16},{32,24},{40,32},{48,40},{56,48},{9,1},{17,9},... | collective-permute-start | bytes 3538952 | tf_op jit(solution)/shard_map/ppermute | solution.py:690
  30.0 29.8 %collective-permute-start.3 = (bf16[3,2,384,256]{3,2,1,0:T(8,128)(2,1)}, bf16[3,2,384,256]{3,2,1,0:T(8,128)(2,1)}, u32[]{:S(2)}, u32[]{:S(2)}) collective-permute-start(bf16[3,2,384,256]{3,2,1,0:T(8,128)(2,1)} %stack.1), channel_id=1, source_target_pairs={{0,8},{8,16},{16,24},{24,32},{32,40},{40,48},{48,56},{1,9},{9,17},... | collective-permute-start | bytes 3538952 | tf_op jit(solution)/shard_map/ppermute | solution.py:690
  37.1 18.7 %all-to-all-start = ((bf16[4,384,384]{2,1,0:T(8,128)(2,1)}), bf16[4,384,384]{2,1,0:T(8,128)(2,1)}, u32[]{:S(2)}, u32[]{:S(2)}) async-start(bf16[4,384,384]{2,1,0:T(8,128)(2,1)} %broadcast_in_dim.4), calls=%async_computation | async-start | bytes 2359296 | tf_op jit(solution)/shard_map/all_to_all | solution.py:700
  67.9 69.3 %collective-permute-start.5 = (bf16[3,2,384,256]{3,2,1,0:T(8,128)(2,1)}, bf16[3,2,384,256]{3,2,1,0:T(8,128)(2,1)}, u32[]{:S(2)}, u32[]{:S(2)}) collective-permute-start(bf16[3,2,384,256]{3,2,1,0:T(8,128)(2,1)} %get-tuple-element.47), channel_id=1, source_target_pairs={{8,0},{16,8},{24,16},{32,24},{40,32},{48,40},{56,48},{9,1},{17,9},... | collective-permute-start | bytes 3538952 | tf_op jit(solution)/shard_map/ppermute | solution.py:690
  69.2 68.0 %collective-permute-start.6 = (bf16[3,2,384,256]{3,2,1,0:T(8,128)(2,1)}, bf16[3,2,384,256]{3,2,1,0:T(8,128)(2,1)}, u32[]{:S(2)}, u32[]{:S(2)}) collective-permute-start(bf16[3,2,384,256]{3,2,1,0:T(8,128)(2,1)} %get-tuple-element.48), channel_id=1, source_target_pairs={{0,8},{8,16},{16,24},{24,32},{32,40},{40,48},{48,56},{1,9},{9,17},... | collective-permute-start | bytes 3538952 | tf_op jit(solution)/shard_map/ppermute | solution.py:690
  73.3 15.7 %copy-start.9 = (bf16[256,256]{1,0:T(8,128)(2,1)S(1)}, bf16[256,256]{1,0:T(8,128)(2,1)}, u32[]{:S(2)}) copy-start(bf16[256,256]{1,0:T(8,128)(2,1)} %get-tuple-element.56) | copy-start | bytes 393220
  73.3 26.8 %copy-start.4 = (f32[256,256]{1,0:T(8,128)S(1)}, f32[256,256]{1,0:T(8,128)}, u32[]{:S(2)}) copy-start(f32[256,256]{1,0:T(8,128)} %get-tuple-element.55.keep) | copy-start | bytes 786436
  78.5 21.5 %all-to-all-start.2 = ((f32[16,24,128]{2,1,0:T(8,128)}), f32[16,24,128]{2,1,0:T(8,128)S(1)}, u32[]{:S(2)}, u32[]{:S(2)}) async-start(f32[16,24,128]{2,1,0:T(8,128)} %gate_terms.1), calls=%async_computation.2 | async-start | bytes 393216 | tf_op jit(solution)/shard_map/all_to_all | solution.py:739
  89.0 3.3 %collective-permute-start.9 = (bf16[256,256]{1,0:T(8,128)(2,1)S(1)}, bf16[256,256]{1,0:T(8,128)(2,1)S(1)}, u32[]{:S(2)}, u32[]{:S(2)}) collective-permute-start(bf16[256,256]{1,0:T(8,128)(2,1)S(1)} %copy-done.9), channel_id=1, source_target_pairs={{0,8},{8,0},{1,9},{9,1},{2,10},{10,2},{3,11},{11,3},{4,12},{12,4},... | collective-permute-start | bytes 393224 | tf_op jit(solution)/shard_map/ppermute | solution.py:695
  127.1 18.6 %all-to-all-start.4 = ((bf16[32,8,384]{2,1,0:T(8,128)(2,1)}), bf16[32,8,384]{2,1,0:T(8,128)(2,1)S(1)}, u32[]{:S(2)}, u32[]{:S(2)}) async-start(bf16[32,8,384]{2,1,0:T(8,128)(2,1)} %chunk_sum.1), calls=%async_computation.4 | async-start | bytes 393216 | tf_op jit(solution)/shard_map/all_to_all | solution.py:757
  137.2 12.4 %copy-start.7 = (s32[24]{0:T(128)S(1)}, s32[24]{0:T(128)}, u32[]{:S(2)}) copy-start(s32[24]{0:T(128)} %get-tuple-element.34.info) | copy-start | bytes 292
  137.2 16.7 %copy-start = (f32[2,384,256]{2,1,0:T(8,128)S(1)}, f32[2,384,256]{2,1,0:T(8,128)}, u32[]{:S(2)}) copy-start(f32[2,384,256]{2,1,0:T(8,128)} %get-tuple-element.46.own) | copy-start | bytes 2359300
  139.9 12.1 %collective-permute-start.7 = (bf16[2,384,256]{2,1,0:T(8,128)(2,1)}, bf16[2,384,256]{2,1,0:T(8,128)(2,1)S(1)}, u32[]{:S(2)}, u32[]{:S(2)}) collective-permute-start(bf16[2,384,256]{2,1,0:T(8,128)(2,1)} %get-tuple-element.51), channel_id=1, source_target_pairs={{64,0},{128,64},{192,128},{256,192},{320,256},{384,320},{448,384},... | collective-permute-start | bytes 1179656 | tf_op jit(solution)/shard_map/ppermute | solution.py:690
  141.8 12.1 %collective-permute-start.8 = (bf16[2,384,256]{2,1,0:T(8,128)(2,1)}, bf16[2,384,256]{2,1,0:T(8,128)(2,1)S(1)}, u32[]{:S(2)}, u32[]{:S(2)}) collective-permute-start(bf16[2,384,256]{2,1,0:T(8,128)(2,1)} %get-tuple-element.52), channel_id=1, source_target_pairs={{0,64},{64,128},{128,192},{192,256},{256,320},{320,384},{384,448},... | collective-permute-start | bytes 1179656 | tf_op jit(solution)/shard_map/ppermute | solution.py:690
  146.4 3.2 %collective-permute-start.10 = (bf16[256,256]{1,0:T(8,128)(2,1)S(1)}, bf16[256,256]{1,0:T(8,128)(2,1)S(1)}, u32[]{:S(2)}, u32[]{:S(2)}) collective-permute-start(bf16[256,256]{1,0:T(8,128)(2,1)S(1)} %get-tuple-element.58.own), channel_id=1, source_target_pairs={{0,8},{8,0},{1,9},{9,1},{2,10},{10,2},{3,11},{11,3},{4,12},{12,4},... | collective-permute-start | bytes 393224 | tf_op jit(solution)/shard_map/ppermute | solution.py:695
  153.9 0.9 copy-start.5
  154.9 0.9 copy-start.6

commit v3 on v2

--- a/solution.py
+++ b/solution.py
@@ -176,39 +176,24 @@
     acc[...] = acc[...] * alpha + dot_tn(values, p.astype(BF16))
 
 
-def fwd_near_kernel(info, q, own, up, down, tk, tv, mask, acc, m, l):
-    h = pl.program_id(0)
+def fwd_own_kernel(q, own, tk, tv, mask, acc, m, l):
     m[...] = jnp.full(m.shape, NEG, F32)
     l[...] = jnp.zeros(l.shape, F32)
     acc[...] = jnp.zeros(acc.shape, F32)
     fwd_block(own[0], own[1], None, q, m, l, acc)
     fwd_block(tk[...], tv[...], mask_column(mask), q, m, l, acc)
-    for a, ref in ((-1, up), (1, down)):
-
-        @pl.when(open_block(info, h, a, 0))
-        def _(ref=ref):
-            fwd_block(ref[0], ref[1], None, q, m, l, acc)
-
-
-def fwd_side_kernel(
-    info, q, left, right, acc_in, m_in, l_in, dot, ot_out, lse_out, delta_out, acc, m, l
-):
+
+
+def fwd_rows_kernel(info, q, up, down, acc_in, m_in, l_in, acc, m, l):
     h = pl.program_id(0)
     acc[...] = acc_in[...]
     m[...] = m_in[...]
     l[...] = l_in[...]
-    for b, ref in ((-1, left), (1, right)):
-        for a in (-1, 0, 1):
-
-            @pl.when(open_block(info, h, a, b))
-            def _(ref=ref, a=a):
-                fwd_block(ref[a + 1, 0], ref[a + 1, 1], None, q, m, l, acc)
-
-    ot = (acc[...] * (1.0 / l[0:1, :])).astype(BF16)
-    ot_out[...] = ot
-    delta = jnp.sum(ot.astype(F32) * dot[...].astype(F32), axis=0, keepdims=True)
-    delta_out[...] = jnp.broadcast_to(delta, delta_out.shape)
-    lse_out[...] = jnp.broadcast_to(m[0:1, :] + jnp.log2(l[0:1, :]), lse_out.shape)
+    for a, ref in ((-1, up), (1, down)):
+
+        @pl.when(open_block(info, h, a, 0))
+        def _(ref=ref):
+            fwd_block(ref[0], ref[1], None, q, m, l, acc)
 
 
 def kv_spec(tile):
@@ -227,62 +212,48 @@
     return pl.BlockSpec((rows, tile), lambda h: (h, 0))
 
 
-def fwd_near_call(info, q, own, up, down, text_keys, text_values, mask):
+def fwd_own_call(q, own, text_keys, text_values, mask):
     tile, width = q.shape
     heads = width // HEAD_DIM
     txt = text_keys.shape[0]
-    keys = 3 * tile + txt
+    keys = tile + txt
     stats = jax.ShapeDtypeStruct((8 * heads, tile), F32)
     return pl.pallas_call(
-        fwd_near_kernel,
+        fwd_own_kernel,
         grid=(heads,),
-        in_specs=[smem(), half_spec(tile)]
-        + [kv_spec(tile)] * 3
-        + [half_spec(txt), half_spec(txt), whole((1, txt))],
+        in_specs=[
+            half_spec(tile),
+            kv_spec(tile),
+            half_spec(txt),
+            half_spec(txt),
+            whole((1, txt)),
+        ],
         out_specs=[row_spec(HEAD_DIM, tile), row_spec(8, tile), row_spec(8, tile)],
         out_shape=[jax.ShapeDtypeStruct((width, tile), F32), stats, stats],
         compiler_params=params("arbitrary"),
         cost_estimate=pl.CostEstimate(
             flops=4 * tile * keys * width, bytes_accessed=4 * keys * width, transcendentals=0
         ),
-        name="fwd_near",
-    )(info, q, own, up, down, text_keys, text_values, mask)
-
-
-def fwd_side_call(info, q, left, right, acc, m, l, dot):
+        name="fwd_own",
+    )(q, own, text_keys, text_values, mask)
+
+
+def fwd_rows_call(info, q, up, down, acc, m, l):
     tile, width = q.shape
-    heads = width // HEAD_DIM
-    keys = 6 * tile
-    return pl.pallas_call(
-        fwd_side_kernel,
-        grid=(heads,),
-        in_specs=[
-            smem(),
-            half_spec(tile),
-            stack_spec(tile),
-            stack_spec(tile),
-            row_spec(HEAD_DIM, tile),
-            row_spec(8, tile),
-            row_spec(8, tile),
-            row_spec(HEAD_DIM, tile),
-        ],
-        out_specs=[row_spec(HEAD_DIM, tile), row_spec(8, tile), row_spec(8, tile)],
-        out_shape=[
-            jax.ShapeDtypeStruct((width, tile), BF16),
-            jax.ShapeDtypeStruct((8 * heads, tile), F32),
-            jax.ShapeDtypeStruct((8 * heads, tile), F32),
-        ],
-        scratch_shapes=[
-            pltpu.VMEM((HEAD_DIM, tile), F32),
-            pltpu.VMEM((8, tile), F32),
-            pltpu.VMEM((8, tile), F32),
-        ],
+    state_specs = [row_spec(HEAD_DIM, tile), row_spec(8, tile), row_spec(8, tile)]
+    keys = 2 * tile
+    return pl.pallas_call(
+        fwd_rows_kernel,
+        grid=(width // HEAD_DIM,),
+        in_specs=[smem(), half_spec(tile), kv_spec(tile), kv_spec(tile)] + state_specs,
+        out_specs=state_specs,
+        out_shape=[jax.ShapeDtypeStruct(x.shape, F32) for x in (acc, m, l)],
         compiler_params=params("arbitrary"),
         cost_estimate=pl.CostEstimate(
             flops=4 * tile * keys * width, bytes_accessed=4 * keys * width, transcendentals=0
         ),
-        name="fwd_side",
-    )(info, q, left, right, acc, m, l, dot)
+        name="fwd_rows",
+    )(info, q, up, down, acc, m, l)
 
 
 def stack_kernel(up, own, down, out):
@@ -322,35 +293,38 @@
     return copies
 
 
-def proj_kernel(flip, ys, xs, info, w, gate, pieces, *refs):
-    *acc_in, out, w_buf, p_buf, sems = refs
-    start = first_block(info, flip, ys, xs)
+def proj_piece(gate, w_buf, p_buf, slot, block):
+    cols = p_buf.shape[2]
+    at = pl.multiple_of(block * cols, 128)
+    scaled = (p_buf[slot].astype(F32) * gate[:, pl.ds(at, cols)]).astype(BF16)
+    return dot_nt(w_buf[slot], scaled)
+
+
+def proj_kernel(ys, xs, info, w, gate, pieces, out, w_buf, p_buf, sems):
+    start = first_block(info, False, ys, xs)
     copies = [
         fetch(w, pieces.at[x], w_buf, p_buf, sems, x, start + x) for x in range(xs)
     ]
-    cols = p_buf.shape[2]
-    acc = acc_in[0][...] if acc_in else None
+    acc = None
     for x in range(xs):
         for copy in copies[x]:
             copy.wait()
-        at = pl.multiple_of((start + x) * cols, 128)
-        scaled = (p_buf[x].astype(F32) * gate[:, pl.ds(at, cols)]).astype(BF16)
-        part = dot_nt(w_buf[x], scaled)
+        part = proj_piece(gate, w_buf, p_buf, x, start + x)
         acc = part if acc is None else acc + part
-    out[...] = acc.astype(out.dtype)
-
-
-def proj_call(flip, sizes, info, w, gate, pieces, *acc):
+    out[...] = acc
+
+
+def proj_call(sizes, info, w, gate, pieces):
     ys, xs = sizes[3:]
     width = w.shape[0]
     _, tile, cols = pieces.shape
     vmem = pl.BlockSpec(memory_space=pltpu.VMEM)
     hbm = pl.BlockSpec(memory_space=pltpu.HBM)
     return pl.pallas_call(
-        functools.partial(proj_kernel, flip, ys, xs),
-        in_specs=[smem(), hbm, vmem, hbm] + [vmem] * len(acc),
+        functools.partial(proj_kernel, ys, xs),
+        in_specs=[smem(), hbm, vmem, hbm],
         out_specs=vmem,
-        out_shape=jax.ShapeDtypeStruct((width, tile), BF16 if flip else F32),
+        out_shape=jax.ShapeDtypeStruct((width, tile), F32),
         scratch_shapes=[
             pltpu.VMEM((xs, width, cols), BF16),
             pltpu.VMEM((xs, tile, cols), BF16),
@@ -363,53 +337,118 @@
             transcendentals=0,
         ),
         name="proj",
-    )(info, w, gate, pieces, *acc)
-
-
-def gate_kernel(ys, xs, info, w, ot, near, far, out, w_buf, p_buf, sems, gates):
+    )(info, w, gate, pieces)
+
+
+def middle_kernel(ys, xs, *refs):
+    info, w, near, far, left, right, gate, q, acc_proj, acc_in, m_in, l_in = refs[:12]
+    dot_out, ot_out, lse_out, delta_out, gate_out = refs[12:17]
+    w_buf, p_buf, side_buf, sems, kv_sems, acc, m, l, gates = refs[17:]
     jobs = []
-    for flip, pieces in ((False, near), (True, far)):
+    kv_copies = []
+    for flip, pieces in ((True, far), (False, near)):
         start = first_block(info, flip, ys, xs)
         for x in range(xs):
             slot = len(jobs)
             copies = fetch(w, pieces.at[x], w_buf, p_buf, sems, slot, start + x)
             jobs.append((slot, start + x, copies))
-    count = p_buf.shape[2] // 128
-    for slot, block, copies in jobs:
+        if flip:
+            for i, source in enumerate((left, right)):
+                copy = pltpu.make_async_copy(source, side_buf.at[i], kv_sems.at[i])
+                copy.start()
+                kv_copies.append(copy)
+
+    acc[...] = acc_in[...]
+    m[...] = m_in[...]
+    l[...] = l_in[...]
+    total = acc_proj[...]
+    for slot, block, copies in jobs[:xs]:
         for copy in copies:
             copy.wait()
-        terms = dot_nn(ot[...], p_buf[slot]) * w_buf[slot].astype(F32)
+        total = total + proj_piece(gate, w_buf, p_buf, slot, block)
+    dot_out[...] = total.astype(BF16)
+
+    for copy in kv_copies:
+        copy.wait()
+    width, tile = acc.shape
+    for h in range(width // HEAD_DIM):
+        lanes = slice(h * HEAD_DIM, (h + 1) * HEAD_DIM)
+        stats = slice(8 * h, 8 * h + 8)
+        state = (q.at[:, lanes], m.at[stats], l.at[stats], acc.at[lanes])
+        for b, i in ((-1, 0), (1, 1)):
+            for a in (-1, 0, 1):
+
+                @pl.when(open_block(info, h, a, b))
+                def _(i=i, a=a, lanes=lanes, state=state):
+                    fwd_block(
+                        side_buf[i, a + 1, 0, :, lanes],
+                        side_buf[i, a + 1, 1, :, lanes],
+                        None,
+                        *state,
+                    )
+
+        norm = l[8 * h : 8 * h + 1, :]
+        ot = (acc[lanes, :] * (1.0 / norm)).astype(BF16)
+        ot_out[lanes, :] = ot
+        lse = m[8 * h : 8 * h + 1, :] + jnp.log2(norm)
+        lse_out[stats, :] = jnp.broadcast_to(lse, (8, tile))
+        delta = jnp.sum(
+            ot.astype(F32) * dot_out[lanes, :].astype(F32), axis=0, keepdims=True
+        )
+        delta_out[stats, :] = jnp.broadcast_to(delta, (8, tile))
+
+    count = p_buf.shape[2] // 128
+    for n, (slot, block, copies) in enumerate(jobs):
+        if n >= xs:
+            for copy in copies:
+                copy.wait()
+        terms = dot_nn(ot_out[...], p_buf[slot]) * w_buf[slot].astype(F32)
         row = jnp.sum(terms, axis=0, keepdims=True)
         for i in range(count):
             gates[pl.ds(block * count + i, 1), :] = row[:, i * 128 : (i + 1) * 128]
-    for i in range(out.shape[0]):
-        out[i] = gates[...]
-
-
-def gate_call(sizes, info, w, ot, near, far):
+    for i in range(gate_out.shape[0]):
+        gate_out[i] = gates[...]
+
+
+def middle_call(sizes, info, w, near, far, left, right, gate, q, acc_proj, partial):
     ys, xs = sizes[3:]
-    width, tile = ot.shape
+    tile, width = q.shape
+    heads = width // HEAD_DIM
     cols = near.shape[2]
     rows = w.shape[1] // 128
     vmem = pl.BlockSpec(memory_space=pltpu.VMEM)
     hbm = pl.BlockSpec(memory_space=pltpu.HBM)
-    return pl.pallas_call(
-        functools.partial(gate_kernel, ys, xs),
-        in_specs=[smem(), hbm, vmem, hbm, hbm],
-        out_specs=vmem,
-        out_shape=jax.ShapeDtypeStruct((sizes[2] * ys * xs, rows, 128), F32),
+    stats = jax.ShapeDtypeStruct((8 * heads, tile), F32)
+    plane = jax.ShapeDtypeStruct((width, tile), BF16)
+    keys = 6 * tile
+    return pl.pallas_call(
+        functools.partial(middle_kernel, ys, xs),
+        in_specs=[smem()] + [hbm] * 5 + [vmem] * 6,
+        out_specs=[vmem] * 5,
+        out_shape=[
+            plane,
+            plane,
+            stats,
+            stats,
+            jax.ShapeDtypeStruct((sizes[2] * ys * xs, rows, 128), F32),
+        ],
         scratch_shapes=[
             pltpu.VMEM((ys * xs, width, cols), BF16),
             pltpu.VMEM((ys * xs, tile, cols), BF16),
+            pltpu.VMEM((2, 3, 2, tile, width), BF16),
             pltpu.SemaphoreType.DMA((2 * ys * xs,)),
+            pltpu.SemaphoreType.DMA((2,)),
+            pltpu.VMEM((width, tile), F32),
+            pltpu.VMEM((8 * heads, tile), F32),
+            pltpu.VMEM((8 * heads, tile), F32),
             pltpu.VMEM((rows, 128), F32),
         ],
         compiler_params=params(),
         cost_estimate=pl.CostEstimate(
-            flops=2 * tile * w.size, bytes_accessed=2 * w.size, transcendentals=0
+            flops=4 * tile * keys * width, bytes_accessed=8 * keys * width, transcendentals=0
         ),
-        name="gate_terms",
-    )(info, w, ot, near, far)
+        name="middle",
+    )(info, w, near, far, left, right, gate, q, acc_proj, *partial)
 
 
 def bwd_math(keys, values, q, dot, lse, delta, dq, extra):
@@ -459,12 +498,30 @@
 
 
 def bwd_near_kernel(
-    info, q, dot, lse, delta, dq_in, cos, sin, up, own, down, up_out, own_out, down_out, gq_out, dq
+    info, q, dot, lse, delta, dq_in, cos, sin, up, own, down, left, right, *refs
 ):
+    up_out, own_out, down_out, gq_out, dq = refs
     h = pl.program_id(0)
     dq[...] = dq_in[...]
     for a, ref, out in ((-1, up, up_out), (1, down, down_out), (0, own, own_out)):
-        bwd_block(info, h, a, 0, ref, out, q, dot, lse, delta, dq)
+        came = [left[a + 1, i].astype(F32) + right[a + 1, i].astype(F32) for i in (0, 1)]
+
+        def run(ref=ref, out=out, came=came):
+            dk, dv = bwd_math(ref[0], ref[1], q, dot, lse, delta, dq, None)
+            out[0] = (dk + came[0]).astype(out.dtype)
+            out[1] = (dv + came[1]).astype(out.dtype)
+
+        if a == 0:
+            run()
+            continue
+        ok = open_block(info, h, a, 0)
+        pl.when(ok)(run)
+
+        @pl.when(jnp.logical_not(ok))
+        def _(out=out, came=came):
+            out[0] = came[0].astype(out.dtype)
+            out[1] = came[1].astype(out.dtype)
+
     x = jnp.transpose(dq[...]) * SCALE
     lane = lax.broadcasted_iota(jnp.int32, x.shape, 1)
     gq_out[...] = (x * cos[...] - partner(x, lane) * sin[...]).astype(BF16)
@@ -512,7 +569,7 @@
     )(info, q, dot, lse, delta, text_keys, text_values, mask, left, right)
 
 
-def bwd_near_call(common, dq, cos, sin, up, own, down):
+def bwd_near_call(common, dq, cos, sin, up, own, down, left, right):
     info, q, dot, lse, delta = common
     tile, width = q.shape
     table = whole((tile, HEAD_DIM))
@@ -521,7 +578,8 @@
         grid=(width // HEAD_DIM,),
         in_specs=bwd_specs(tile)
         + [row_spec(HEAD_DIM, tile), table, table]
-        + [kv_spec(tile)] * 3,
+        + [kv_spec(tile)] * 3
+        + [stack_spec(tile)] * 2,
         out_specs=[kv_spec(tile)] * 3 + [half_spec(tile)],
         out_shape=[
             jax.ShapeDtypeStruct((2, tile, width), BF16),
@@ -533,58 +591,30 @@
         compiler_params=params("arbitrary"),
         cost_estimate=bwd_cost(tile, 3 * tile, width),
         name="bwd_near",
-    )(info, q, dot, lse, delta, dq, cos, sin, up, own, down)
-
-
-def pair_sum_kernel(up, down, up_l, up_r, down_l, down_r, up_out, down_out):
-    for part, left, right, out in (
-        (up, up_l, up_r, up_out),
-        (down, down_l, down_r, down_out),
-    ):
-        total = part[...].astype(F32) + left[0].astype(F32) + right[0].astype(F32)
-        out[...] = total.astype(BF16)
-
-
-def pair_sum_call(up, down, left, right):
-    tile, width = up.shape[1:]
-    shape = jax.ShapeDtypeStruct((2, tile, width), BF16)
-    top = pl.BlockSpec((1, 2, tile, HEAD_DIM), lambda h: (0, 0, 0, h))
-    bottom = pl.BlockSpec((1, 2, tile, HEAD_DIM), lambda h: (2, 0, 0, h))
-    return pl.pallas_call(
-        pair_sum_kernel,
-        grid=(width // HEAD_DIM,),
-        in_specs=[kv_spec(tile)] * 2 + [top, top, bottom, bottom],
-        out_specs=[kv_spec(tile)] * 2,
-        out_shape=[shape] * 2,
-        compiler_params=params("arbitrary"),
-        name="pair_sum",
-    )(up, down, left, right, left, right)
-
-
-def finish_kernel(own, left, right, up, down, cos, sin, gk_out, gv_out):
-    total = own[...]
-    for other in (left[0], right[0], up[...], down[...]):
-        total = total + other.astype(F32)
+    )(info, q, dot, lse, delta, dq, cos, sin, up, own, down, left, right)
+
+
+def finish_kernel(own, up, down, cos, sin, gk_out, gv_out):
+    total = own[...] + up[...].astype(F32) + down[...].astype(F32)
     x = total[0]
     lane = lax.broadcasted_iota(jnp.int32, x.shape, 1)
     gk_out[...] = (x * cos[...] - partner(x, lane) * sin[...]).astype(BF16)
     gv_out[...] = total[1].astype(BF16)
 
 
-def finish_call(own, left, right, up, down, cos, sin):
+def finish_call(own, up, down, cos, sin):
     tile, width = own.shape[1:]
     table = whole((tile, HEAD_DIM))
-    middle = pl.BlockSpec((1, 2, tile, HEAD_DIM), lambda h: (1, 0, 0, h))
     shape = jax.ShapeDtypeStruct((tile, width), BF16)
     return pl.pallas_call(
         finish_kernel,
         grid=(width // HEAD_DIM,),
-        in_specs=[kv_spec(tile), middle, middle, kv_spec(tile), kv_spec(tile), table, table],
+        in_specs=[kv_spec(tile)] * 3 + [table, table],
         out_specs=[half_spec(tile)] * 2,
         out_shape=[shape, shape],
-        compiler_params=params("arbitrary", limit=SMALL),
+        compiler_params=params("arbitrary"),
         name="finish",
-    )(own, left, right, up, down, cos, sin)
+    )(own, up, down, cos, sin)
 
 
 def split_pair(values):
@@ -635,7 +665,7 @@
         in_specs=[pl.BlockSpec(memory_space=pltpu.VMEM)],
         out_specs=pl.BlockSpec(memory_space=pltpu.VMEM),
         out_shape=jax.ShapeDtypeStruct(got.shape, BF16),
-        compiler_params=params(),
+        compiler_params=params(limit=SMALL),
         name="chunk_sum",
     )(got)
 
@@ -725,17 +755,28 @@
         sizes, window_reach, tile_map, query_in, key_in, value_in
     )
 
+    partial = fwd_own_call(q, kv, text_keys, text_values, mask)
+
     kv_up, kv_down = shift(kv, "z", 1), shift(kv, "z", -1)
     gy_x = spread(g_y, "x")
     stack = stack_call(kv_up, kv, kv_down)
     kv_left, kv_right = shift(stack, COL, 1), shift(stack, COL, -1)
 
-    partial = fwd_near_call(info, q, kv, kv_up, kv_down, text_keys, text_values, mask)
-    acc = proj_call(False, sizes, info, out_weight, gate, g_x)
-    dot = proj_call(True, sizes, info, out_weight, gate, gy_x, acc)
-    ot, lse, delta = fwd_side_call(info, q, kv_left, kv_right, *partial, dot)
-
-    gate_terms = gate_call(sizes, info, out_weight, ot, g_x, gy_x)
+    acc = proj_call(sizes, info, out_weight, gate, g_x)
+    partial = fwd_rows_call(info, q, kv_up, kv_down, *partial)
+    dot, _, lse, delta, gate_terms = middle_call(
+        sizes,
+        info,
+        out_weight,
+        g_x,
+        gy_x,
+        kv_left,
+        kv_right,
+        gate,
+        q,
+        acc,
+        partial,
+    )
     gate_terms = lax.all_to_all(gate_terms, ("core", *HEAD), 0, 0, tiled=True)
 
     common = (info, q, dot, lse, delta)
@@ -747,9 +788,9 @@
     back_right = shift(right, COL, 1)
     packed = pack_call(keep, taken, gate_terms, lax.axis_size(CHIPS))
     got = lax.all_to_all(packed, CHIPS, 0, 0, tiled=True)
-    up, own, down, grad_query = bwd_near_call(common, dq, cos, sin, kv_up, kv, kv_down)
-
-    up, down = pair_sum_call(up, down, back_left, back_right)
+    up, own, down, grad_query = bwd_near_call(
+        common, dq, cos, sin, kv_up, kv, kv_down, back_left, back_right
+    )
     up = shift(up, "z", -1)
     down = shift(down, "z", 1)
 
@@ -757,7 +798,7 @@
     summed = lax.all_to_all(chunk, CHIPS, 0, 0, tiled=True)
     own_text, grad_gate = unpack_call(summed, width, out_weight.shape[1] // 128)
     other_text = swap(own_text, "core", 1)
-    grad_key, grad_value = finish_call(own, back_left, back_right, up, down, cos, sin)
+    grad_key, grad_value = finish_call(own, up, down, cos, sin)
     grad_text_keys, grad_text_values = choose_call(info, own_text, other_text)
     return (
         grad_query,

time: 159 us -> 158 us (level)
  the two profiles are of different devices: /device:TPU:64 before, /device:TPU:120 now
where the time goes in v3:
time: 158 us; the launch traced here: 157 us
  starting transfers between devices  56 us (35%)
  Pallas kernels  36.9 us (23%)
  waiting for transfers between devices  32.2 us (20%)
  blocking collectives  23.7 us (15%)
  local copies, waits for them, and re-layouts  6.93 us (4%)
    all_to_all x1, blocking collectives, on_device(): got = lax.all_to_all(packed, CHIPS, 0, 0, tiled=True)  23.7 us
    ppermute x8, starting transfers between devices, shift(): return lax.ppermute(array, axis, pairs)  22 us
    all_to_all x1, waiting for transfers between devices, on_device(): gate_terms = lax.all_to_all(gate_terms, ('core', *HEAD), 0, 0, tiled=True)  11.2 us
    ppermute x8, waiting for transfers between devices, shift(): return lax.ppermute(array, axis, pairs)  9.99 us
    all_to_all x1, starting transfers between devices, on_device(): gate_terms = lax.all_to_all(gate_terms, ('core', *HEAD), 0, 0, tiled=True)  9.81 us
    all_to_all x2, starting transfers between devices, spread(): return lax.all_to_all(copies, axis, 0, 0, tiled=True)  8.88 us
    ppermute x3, starting transfers between devices, swap(): return lax.ppermute(array, axis, [(i, i ^ bit) for i in range(length)])  8.64 us
    pallas_call x1, Pallas kernels, middle_call(): pl.pallas_call(functools.partial(middle_kernel, ys, xs), in_specs=[smem()...  8.19 us
  transfers between devices with their start and end apart: 15, of which 9 were waited for; matrix products, arithmetic and copies ran while one was open for 1% of the time, Pallas kernels for 13%

profile of v3, /device:TPU:120, one launch (start us, length us, event | category | flops | bytes accessed | tf_op | source)
XLA Modules:
  0.0 156.6 jit_solution(1825406093907137215)
XLA Ops:
  0.6 2.1 %broadcast_in_dim.4 = bf16[4,384,384]{2,1,0:T(8,128)(2,1)} broadcast(bf16[384,384]{1,0:T(8,128)(2,1)} %param.22), dimensions={1,2} | broadcast | bytes 1474560 | tf_op jit(solution)/shard_map/broadcast_in_dim | solution.py:729
  2.7 0.0 copy-start.8
  2.7 4.4 %all-to-all-start = ((bf16[4,384,384]{2,1,0:T(8,128)(2,1)}), bf16[4,384,384]{2,1,0:T(8,128)(2,1)}, u32[]{:S(2)}, u32[]{:S(2)}) async-start(bf16[4,384,384]{2,1,0:T(8,128)(2,1)} %broadcast_in_dim.4), calls=%async_computation | async-start | bytes 2359296 | tf_op jit(solution)/shard_map/all_to_all | solution.py:730
  7.2 2.5 %rot.1 = (bf16[384,256]{1,0:T(8,128)(2,1)}, bf16[2,384,256]{2,1,0:T(8,128)(2,1)}, f32[384,128]{1,0:T(8,128)}, f32[384,128]{1,0:T(8,128)}, s32[24]{0:T(128)}) custom-call(s32[2,2]{1,0:T(2,128)} %reach.1, s32[3,64]{1,0:T(4,128)} %bitcast.6, f32[8,128]{1,0:T(8,128)} %constant.2.clone.freq, bf16[384,256]{1,0:T(8,128)(2,1)} %q.1, bf16[384,256]{1,0:T(8,128)(2,1)} %k.1, ...), custom_call_target="tpu_custom_call" | custom-call | tf_op jit(solution)/shard_map/rot/pallas_call | solution.py:133
  9.7 4.3 %collective-permute-start.1 = (bf16[2,384,256]{2,1,0:T(8,128)(2,1)}, bf16[2,384,256]{2,1,0:T(8,128)(2,1)S(1)}, u32[]{:S(2)}, u32[]{:S(2)}) collective-permute-start(bf16[2,384,256]{2,1,0:T(8,128)(2,1)} %get-tuple-element.38.own), channel_id=1, source_target_pairs={{0,64},{64,128},{128,192},{192,256},{256,320},{320,384},{384,448},... | collective-permute-start | bytes 1179656 | tf_op jit(solution)/shard_map/ppermute | solution.py:720
  13.9 1.9 %collective-permute-start.2 = (bf16[2,384,256]{2,1,0:T(8,128)(2,1)}, bf16[2,384,256]{2,1,0:T(8,128)(2,1)S(1)}, u32[]{:S(2)}, u32[]{:S(2)}) collective-permute-start(bf16[2,384,256]{2,1,0:T(8,128)(2,1)} %get-tuple-element.38.own), channel_id=1, source_target_pairs={{64,0},{128,64},{192,128},{256,192},{320,256},{384,320},{448,384},... | collective-permute-start | bytes 1179656 | tf_op jit(solution)/shard_map/ppermute | solution.py:720
  15.9 0.0 copy-done.8
  15.9 4.7 %collective-permute-start = (bf16[384,384]{1,0:T(8,128)(2,1)S(1)}, bf16[384,384]{1,0:T(8,128)(2,1)S(1)}, u32[]{:S(2)}, u32[]{:S(2)}) collective-permute-start(bf16[384,384]{1,0:T(8,128)(2,1)S(1)} %copy-done.8), channel_id=1, source_target_pairs={{0,4},{4,0},{1,5},{5,1},{2,6},{6,2},{3,7},{7,3},{8,12},{12,8},{9,1... | collective-permute-start | bytes 884744 | tf_op jit(solution)/shard_map/ppermute | solution.py:725
  20.6 2.0 %collective-permute-done.1.up = bf16[2,384,256]{2,1,0:T(8,128)(2,1)S(1)} collective-permute-done((bf16[2,384,256]{2,1,0:T(8,128)(2,1)}, bf16[2,384,256]{2,1,0:T(8,128)(2,1)S(1)}, u32[]{:S(2)}, u32[]{:S(2)}) %collective-permute-start.1) | collective-permute-done | bytes 393248 | tf_op jit(solution)/shard_map/ppermute | solution.py:720
  22.6 0.0 copy-start
  22.6 4.6 %collective-permute-done.2.down = bf16[2,384,256]{2,1,0:T(8,128)(2,1)S(1)} collective-permute-done((bf16[2,384,256]{2,1,0:T(8,128)(2,1)}, bf16[2,384,256]{2,1,0:T(8,128)(2,1)S(1)}, u32[]{:S(2)}, u32[]{:S(2)}) %collective-permute-start.2) | collective-permute-done | bytes 393248 | tf_op jit(solution)/shard_map/ppermute | solution.py:720
  27.3 0.0 copy-start.2
  27.3 1.0 copy-done.2
  28.3 0.0 copy-start.1
  28.3 1.3 stack.1
  29.6 1.9 %collective-permute-start.3 = (bf16[3,2,384,256]{3,2,1,0:T(8,128)(2,1)}, bf16[3,2,384,256]{3,2,1,0:T(8,128)(2,1)}, u32[]{:S(2)}, u32[]{:S(2)}) collective-permute-start(bf16[3,2,384,256]{3,2,1,0:T(8,128)(2,1)} %stack.1), channel_id=1, source_target_pairs={{0,8},{8,16},{16,24},{24,32},{32,40},{40,48},{48,56},{1,9},{9,17},... | collective-permute-start | bytes 3538952 | tf_op jit(solution)/shard_map/ppermute | solution.py:720
  31.5 3.6 %collective-permute-start.4 = (bf16[3,2,384,256]{3,2,1,0:T(8,128)(2,1)}, bf16[3,2,384,256]{3,2,1,0:T(8,128)(2,1)}, u32[]{:S(2)}, u32[]{:S(2)}) collective-permute-start(bf16[3,2,384,256]{3,2,1,0:T(8,128)(2,1)} %stack.1), channel_id=1, source_target_pairs={{8,0},{16,8},{24,16},{32,24},{40,32},{48,40},{56,48},{9,1},{17,9},... | collective-permute-start | bytes 3538952 | tf_op jit(solution)/shard_map/ppermute | solution.py:720
  35.2 1.4 collective-permute-done
  36.5 0.0 all-to-all-done.pieces.refs_2_
  36.5 1.1 broadcast_in_dim.5
  37.6 0.0 copy-done
  37.6 0.0 copy-done.1
  37.6 4.5 %all-to-all-start.1 = ((bf16[4,384,384]{2,1,0:T(8,128)(2,1)}), bf16[4,384,384]{2,1,0:T(8,128)(2,1)}, u32[]{:S(2)}, u32[]{:S(2)}) async-start(bf16[4,384,384]{2,1,0:T(8,128)(2,1)} %broadcast_in_dim.5), calls=%async_computation.1 | async-start | bytes 2359296 | tf_op jit(solution)/shard_map/all_to_all | solution.py:730
  42.1 3.5 %fwd_own.1 = (f32[256,384]{1,0:T(8,128)}, f32[16,384]{1,0:T(8,128)}, f32[16,384]{1,0:T(8,128)}) custom-call(bf16[384,256]{1,0:T(8,128)(2,1)} %get-tuple-element.37.q.refs_7_, bf16[2,384,256]{2,1,0:T(8,128)(2,1)} %get-tuple-element.38.own, bf16[256,256]{1,0:T(8,128)(2,1)} %tk.3, bf16[256,256]{1,0:T(8,128)(2,1)} %tv.3, s32[1,256]{1,0:T(1,128)} %bitcast.8), custom_call_target="tpu_custom_call" | custom-call | flops 251658240 | bytes 655360 | tf_op jit(solution)/shard_map/fwd_own/pallas_call | solution.py:221
  45.6 2.2 %fwd_rows.1 = (f32[256,384]{1,0:T(8,128)}, f32[16,384]{1,0:T(8,128)}, f32[16,384]{1,0:T(8,128)}) custom-call(s32[24]{0:T(128)} %get-tuple-element.36.info.refs_0_, bf16[384,256]{1,0:T(8,128)(2,1)} %get-tuple-element.37.q.refs_7_, bf16[2,384,256]{2,1,0:T(8,128)(2,1)} %copy-done, bf16[2,384,256]{2,1,0:T(8,128)(2,1)} %copy-done.1, ...), custom_call_target="tpu_custom_call" | custom-call | flops 301989888 | bytes 786432 | tf_op jit(solution)/shard_map/fwd_rows/pallas_call | solution.py:245
  47.9 3.8 %proj.1.refs_8_ = f32[256,384]{1,0:T(8,128)} custom-call(s32[24]{0:T(128)} %get-tuple-element.36.info.refs_0_, bf16[256,3072]{1,0:T(8,128)(2,1)} %refs_1_.1, f32[1,3072]{1,0:T(1,128)} %bitcast.4, bf16[4,384,384]{2,1,0:T(8,128)(2,1)} %all-to-all-done.pieces.refs_2_), custom_call_target="tpu_custom_call" | custom-call | flops 301989888 | bytes 1966080 | tf_op jit(solution)/shard_map/proj/pallas_call | solution.py:323
  51.7 7.0 %all-to-all-done.1.refs_3_ = bf16[4,384,384]{2,1,0:T(8,128)(2,1)} async-done(((bf16[4,384,384]{2,1,0:T(8,128)(2,1)}), bf16[4,384,384]{2,1,0:T(8,128)(2,1)}, u32[]{:S(2)}, u32[]{:S(2)}) %all-to-all-start.1) | async-done | bytes 1179680 | tf_op jit(solution)/shard_map/all_to_all | solution.py:730
  58.7 0.0 collective-permute-done.3.refs_4_.left
  58.7 0.0 collective-permute-done.4.refs_5_.right
  58.7 8.2 %middle.1 = (bf16[256,384]{1,0:T(8,128)(2,1)}, bf16[256,384]{1,0:T(8,128)(2,1)}, f32[16,384]{1,0:T(8,128)}, f32[16,384]{1,0:T(8,128)}, f32[16,24,128]{2,1,0:T(8,128)}) custom-call(s32[24]{0:T(128)} %get-tuple-element.36.info.refs_0_, bf16[256,3072]{1,0:T(8,128)(2,1)} %refs_1_.1, bf16[4,384,384]{2,1,0:T(8,128)(2,1)} %all-to-all-done.pieces.refs_2_, ...), custom_call_target="tpu_custom_call" | custom-call | flops 905969664 | bytes 4718592 | tf_op jit(solution)/shard_map/middle/pallas_call | solution.py:424
  66.9 5.3 %bwd_side.1 = (bf16[3,2,384,256]{3,2,1,0:T(8,128)(2,1)}, bf16[3,2,384,256]{3,2,1,0:T(8,128)(2,1)}, f32[256,256]{1,0:T(8,128)}, bf16[256,256]{1,0:T(8,128)(2,1)}, f32[256,384]{1,0:T(8,128)}) custom-call(s32[24]{0:T(128)} %get-tuple-element.36.info.refs_0_, bf16[384,256]{1,0:T(8,128)(2,1)} %get-tuple-element.37.q.refs_7_, ...), custom_call_target="tpu_custom_call" | custom-call | flops 2516582400 | bytes 5242880 | tf_op jit(solution)/shard_map/bwd_side/pallas_call | solution.py:551
  72.2 1.9 %collective-permute-start.5 = (bf16[3,2,384,256]{3,2,1,0:T(8,128)(2,1)}, bf16[3,2,384,256]{3,2,1,0:T(8,128)(2,1)S(1)}, u32[]{:S(2)}, u32[]{:S(2)}) collective-permute-start(bf16[3,2,384,256]{3,2,1,0:T(8,128)(2,1)} %get-tuple-element.51), channel_id=1, source_target_pairs={{8,0},{16,8},{24,16},{32,24},{40,32},{48,40},{56,48},{9,1},{17,9},... | collective-permute-start | bytes 3538952 | tf_op jit(solution)/shard_map/ppermute | solution.py:720
  74.1 2.5 %collective-permute-start.6 = (bf16[3,2,384,256]{3,2,1,0:T(8,128)(2,1)}, bf16[3,2,384,256]{3,2,1,0:T(8,128)(2,1)}, u32[]{:S(2)}, u32[]{:S(2)}) collective-permute-start(bf16[3,2,384,256]{3,2,1,0:T(8,128)(2,1)} %get-tuple-element.52), channel_id=1, source_target_pairs={{0,8},{8,16},{16,24},{24,32},{32,40},{40,48},{48,56},{1,9},{9,17},... | collective-permute-start | bytes 3538952 | tf_op jit(solution)/shard_map/ppermute | solution.py:720
  76.6 9.8 %all-to-all-start.2 = ((f32[16,24,128]{2,1,0:T(8,128)}), f32[16,24,128]{2,1,0:T(8,128)S(1)}, u32[]{:S(2)}, u32[]{:S(2)}) async-start(f32[16,24,128]{2,1,0:T(8,128)} %get-tuple-element.61), calls=%async_computation.2 | async-start | bytes 393216 | tf_op jit(solution)/shard_map/all_to_all | solution.py:780
  86.4 2.0 %collective-permute-start.9 = (bf16[256,256]{1,0:T(8,128)(2,1)}, bf16[256,256]{1,0:T(8,128)(2,1)S(1)}, u32[]{:S(2)}, u32[]{:S(2)}) collective-permute-start(bf16[256,256]{1,0:T(8,128)(2,1)} %get-tuple-element.60), channel_id=1, source_target_pairs={{0,8},{8,0},{1,9},{9,1},{2,10},{10,2},{3,11},{11,3},{4,12},{12,4},... | collective-permute-start | bytes 393224 | tf_op jit(solution)/shard_map/ppermute | solution.py:725
  88.4 1.4 collective-permute-done.9.got
  89.8 11.2 %all-to-all-done.2.gate = f32[16,24,128]{2,1,0:T(8,128)S(1)} async-done(((f32[16,24,128]{2,1,0:T(8,128)}), f32[16,24,128]{2,1,0:T(8,128)S(1)}, u32[]{:S(2)}, u32[]{:S(2)}) %all-to-all-start.2) | async-done | bytes 196640 | tf_op jit(solution)/shard_map/all_to_all | solution.py:780
  101.0 0.0 copy-start.3
  101.0 0.9 copy-done.3
  102.0 0.1 pack.1
  102.0 23.7 %all_to_all.25.got = bf16[32,8,384]{2,1,0:T(8,128)(2,1)S(1)} all-to-all(bf16[32,8,384]{2,1,0:T(8,128)(2,1)S(1)} %pack.1), channel_id=1, replica_groups=mesh['z'=8,'y'=4,'core'=2,'yhi'=2,'x'=4] {'z','y'}, dimensions={0} | all-to-all | bytes 393216 | tf_op jit(solution)/shard_map/all_to_all | solution.py:790
  125.8 0.7 chunk_sum.1
  126.5 6.6 %all-to-all-start.4 = ((bf16[32,8,384]{2,1,0:T(8,128)(2,1)}), bf16[32,8,384]{2,1,0:T(8,128)(2,1)S(1)}, u32[]{:S(2)}, u32[]{:S(2)}) async-start(bf16[32,8,384]{2,1,0:T(8,128)(2,1)} %chunk_sum.1), calls=%async_computation.4 | async-start | bytes 393216 | tf_op jit(solution)/shard_map/all_to_all | solution.py:798
  133.2 0.0 collective-permute-done.5.left
  133.2 0.0 copy-start.5
  133.2 0.0 collective-permute-done.6.right
  133.2 1.0 copy-done.5
  134.2 0.0 copy-start.4
  134.2 4.7 %bwd_near.1 = (bf16[2,384,256]{2,1,0:T(8,128)(2,1)}, f32[2,384,256]{2,1,0:T(8,128)}, bf16[2,384,256]{2,1,0:T(8,128)(2,1)}, bf16[384,256]{1,0:T(8,128)(2,1)}) custom-call(s32[24]{0:T(128)} %get-tuple-element.36.info.refs_0_, bf16[384,256]{1,0:T(8,128)(2,1)} %get-tuple-element.37.q.refs_7_, bf16[256,384]{1,0:T(8,128)(2,1)} %get-tuple-element.45.dot, ...), custom_call_target="tpu_custom_call" | custom-call | flops 1132462080 | bytes 2359296 | tf_op jit(solution)/shard_map/bwd_near/pallas_call | solution.py:576
  139.0 2.4 %collective-permute-start.7 = (bf16[2,384,256]{2,1,0:T(8,128)(2,1)}, bf16[2,384,256]{2,1,0:T(8,128)(2,1)S(1)}, u32[]{:S(2)}, u32[]{:S(2)}) collective-permute-start(bf16[2,384,256]{2,1,0:T(8,128)(2,1)} %get-tuple-element.55), channel_id=1, source_target_pairs={{64,0},{128,64},{192,128},{256,192},{320,256},{384,320},{448,384},... | collective-permute-start | bytes 1179656 | tf_op jit(solution)/shard_map/ppermute | solution.py:720
  141.4 3.4 %collective-permute-start.8 = (bf16[2,384,256]{2,1,0:T(8,128)(2,1)}, bf16[2,384,256]{2,1,0:T(8,128)(2,1)S(1)}, u32[]{:S(2)}, u32[]{:S(2)}) collective-permute-start(bf16[2,384,256]{2,1,0:T(8,128)(2,1)} %get-tuple-element.56), channel_id=1, source_target_pairs={{0,64},{64,128},{128,192},{192,256},{256,320},{320,384},{384,448},... | collective-permute-start | bytes 1179656 | tf_op jit(solution)/shard_map/ppermute | solution.py:720
  144.8 0.0 all-to-all-done.4.got
  144.8 0.6 unpack.1
  145.4 1.9 %collective-permute-start.10 = (bf16[256,256]{1,0:T(8,128)(2,1)S(1)}, bf16[256,256]{1,0:T(8,128)(2,1)S(1)}, u32[]{:S(2)}, u32[]{:S(2)}) collective-permute-start(bf16[256,256]{1,0:T(8,128)(2,1)S(1)} %get-tuple-element.62.own), channel_id=1, source_target_pairs={{0,8},{8,0},{1,9},{9,1},{2,10},{10,2},{3,11},{11,3},{4,12},{12,4},... | collective-permute-start | bytes 393224 | tf_op jit(solution)/shard_map/ppermute | solution.py:725
  147.4 1.3 collective-permute-done.10.other
  148.7 0.0 copy-done.4
  148.7 1.3 choose.1
  149.9 1.1 collective-permute-done.7.up
  151.1 0.0 copy-start.6
  151.1 2.2 %collective-permute-done.8.down = bf16[2,384,256]{2,1,0:T(8,128)(2,1)S(1)} collective-permute-done((bf16[2,384,256]{2,1,0:T(8,128)(2,1)}, bf16[2,384,256]{2,1,0:T(8,128)(2,1)S(1)}, u32[]{:S(2)}, u32[]{:S(2)}) %collective-permute-start.8) | collective-permute-done | bytes 393248 | tf_op jit(solution)/shard_map/ppermute | solution.py:720
  153.3 0.0 copy-start.7
  153.3 0.0 copy-done.6
  153.3 0.7 copy-done.7
  154.0 2.6 %finish.1 = (bf16[384,256]{1,0:T(8,128)(2,1)}, bf16[384,256]{1,0:T(8,128)(2,1)}) custom-call(f32[2,384,256]{2,1,0:T(8,128)} %get-tuple-element.54.own, bf16[2,384,256]{2,1,0:T(8,128)(2,1)} %copy-done.6, bf16[2,384,256]{2,1,0:T(8,128)(2,1)} %copy-done.7, f32[384,128]{1,0:T(8,128)} %get-tuple-element.49.cos, f32[384,128]{1,0:T(8,128)} %get-tuple-element.50.sin), custom_call_target="tpu_custom_call" | custom-call | tf_op jit(solution)/shard_map/finish/pallas_call | solution.py:609
Async XLA Ops:
  2.7 13.1 %copy-start.8 = (bf16[384,384]{1,0:T(8,128)(2,1)S(1)}, bf16[384,384]{1,0:T(8,128)(2,1)}, u32[]{:S(2)}) copy-start(bf16[384,384]{1,0:T(8,128)(2,1)} %param.22) | copy-start | bytes 884740
  2.7 33.8 %all-to-all-start = ((bf16[4,384,384]{2,1,0:T(8,128)(2,1)}), bf16[4,384,384]{2,1,0:T(8,128)(2,1)}, u32[]{:S(2)}, u32[]{:S(2)}) async-start(bf16[4,384,384]{2,1,0:T(8,128)(2,1)} %broadcast_in_dim.4), calls=%async_computation | async-start | bytes 2359296 | tf_op jit(solution)/shard_map/all_to_all | solution.py:730
  9.7 13.0 %collective-permute-start.1 = (bf16[2,384,256]{2,1,0:T(8,128)(2,1)}, bf16[2,384,256]{2,1,0:T(8,128)(2,1)S(1)}, u32[]{:S(2)}, u32[]{:S(2)}) collective-permute-start(bf16[2,384,256]{2,1,0:T(8,128)(2,1)} %get-tuple-element.38.own), channel_id=1, source_target_pairs={{0,64},{64,128},{128,192},{192,256},{256,320},{320,384},{384,448},... | collective-permute-start | bytes 1179656 | tf_op jit(solution)/shard_map/ppermute | solution.py:720
  13.9 13.3 %collective-permute-start.2 = (bf16[2,384,256]{2,1,0:T(8,128)(2,1)}, bf16[2,384,256]{2,1,0:T(8,128)(2,1)S(1)}, u32[]{:S(2)}, u32[]{:S(2)}) collective-permute-start(bf16[2,384,256]{2,1,0:T(8,128)(2,1)} %get-tuple-element.38.own), channel_id=1, source_target_pairs={{64,0},{128,64},{192,128},{256,192},{320,256},{384,320},{448,384},... | collective-permute-start | bytes 1179656 | tf_op jit(solution)/shard_map/ppermute | solution.py:720
  15.9 20.6 %collective-permute-start = (bf16[384,384]{1,0:T(8,128)(2,1)S(1)}, bf16[384,384]{1,0:T(8,128)(2,1)S(1)}, u32[]{:S(2)}, u32[]{:S(2)}) collective-permute-start(bf16[384,384]{1,0:T(8,128)(2,1)S(1)} %copy-done.8), channel_id=1, source_target_pairs={{0,4},{4,0},{1,5},{5,1},{2,6},{6,2},{3,7},{7,3},{8,12},{12,8},{9,1... | collective-permute-start | bytes 884744 | tf_op jit(solution)/shard_map/ppermute | solution.py:725
  22.6 15.0 %copy-start = (bf16[2,384,256]{2,1,0:T(8,128)(2,1)}, bf16[2,384,256]{2,1,0:T(8,128)(2,1)S(1)}, u32[]{:S(2)}) copy-start(bf16[2,384,256]{2,1,0:T(8,128)(2,1)S(1)} %collective-permute-done.1.up) | copy-start | bytes 1179652
  27.3 1.0 copy-start.2
  28.3 9.4 %copy-start.1 = (bf16[2,384,256]{2,1,0:T(8,128)(2,1)}, bf16[2,384,256]{2,1,0:T(8,128)(2,1)S(1)}, u32[]{:S(2)}) copy-start(bf16[2,384,256]{2,1,0:T(8,128)(2,1)S(1)} %collective-permute-done.2.down) | copy-start | bytes 1179652
  29.6 29.1 %collective-permute-start.3 = (bf16[3,2,384,256]{3,2,1,0:T(8,128)(2,1)}, bf16[3,2,384,256]{3,2,1,0:T(8,128)(2,1)}, u32[]{:S(2)}, u32[]{:S(2)}) collective-permute-start(bf16[3,2,384,256]{3,2,1,0:T(8,128)(2,1)} %stack.1), channel_id=1, source_target_pairs={{0,8},{8,16},{16,24},{24,32},{32,40},{40,48},{48,56},{1,9},{9,17},... | collective-permute-start | bytes 3538952 | tf_op jit(solution)/shard_map/ppermute | solution.py:720
  31.5 27.2 %collective-permute-start.4 = (bf16[3,2,384,256]{3,2,1,0:T(8,128)(2,1)}, bf16[3,2,384,256]{3,2,1,0:T(8,128)(2,1)}, u32[]{:S(2)}, u32[]{:S(2)}) collective-permute-start(bf16[3,2,384,256]{3,2,1,0:T(8,128)(2,1)} %stack.1), channel_id=1, source_target_pairs={{8,0},{16,8},{24,16},{32,24},{40,32},{48,40},{56,48},{9,1},{17,9},... | collective-permute-start | bytes 3538952 | tf_op jit(solution)/shard_map/ppermute | solution.py:720
  37.6 21.0 %all-to-all-start.1 = ((bf16[4,384,384]{2,1,0:T(8,128)(2,1)}), bf16[4,384,384]{2,1,0:T(8,128)(2,1)}, u32[]{:S(2)}, u32[]{:S(2)}) async-start(bf16[4,384,384]{2,1,0:T(8,128)(2,1)} %broadcast_in_dim.5), calls=%async_computation.1 | async-start | bytes 2359296 | tf_op jit(solution)/shard_map/all_to_all | solution.py:730
  72.2 61.0 %collective-permute-start.5 = (bf16[3,2,384,256]{3,2,1,0:T(8,128)(2,1)}, bf16[3,2,384,256]{3,2,1,0:T(8,128)(2,1)S(1)}, u32[]{:S(2)}, u32[]{:S(2)}) collective-permute-start(bf16[3,2,384,256]{3,2,1,0:T(8,128)(2,1)} %get-tuple-element.51), channel_id=1, source_target_pairs={{8,0},{16,8},{24,16},{32,24},{40,32},{48,40},{56,48},{9,1},{17,9},... | collective-permute-start | bytes 3538952 | tf_op jit(solution)/shard_map/ppermute | solution.py:720
  74.1 59.1 %collective-permute-start.6 = (bf16[3,2,384,256]{3,2,1,0:T(8,128)(2,1)}, bf16[3,2,384,256]{3,2,1,0:T(8,128)(2,1)}, u32[]{:S(2)}, u32[]{:S(2)}) collective-permute-start(bf16[3,2,384,256]{3,2,1,0:T(8,128)(2,1)} %get-tuple-element.52), channel_id=1, source_target_pairs={{0,8},{8,16},{16,24},{24,32},{32,40},{40,48},{48,56},{1,9},{9,17},... | collective-permute-start | bytes 3538952 | tf_op jit(solution)/shard_map/ppermute | solution.py:720
  76.6 24.4 %all-to-all-start.2 = ((f32[16,24,128]{2,1,0:T(8,128)}), f32[16,24,128]{2,1,0:T(8,128)S(1)}, u32[]{:S(2)}, u32[]{:S(2)}) async-start(f32[16,24,128]{2,1,0:T(8,128)} %get-tuple-element.61), calls=%async_computation.2 | async-start | bytes 393216 | tf_op jit(solution)/shard_map/all_to_all | solution.py:780
  86.4 3.4 %collective-permute-start.9 = (bf16[256,256]{1,0:T(8,128)(2,1)}, bf16[256,256]{1,0:T(8,128)(2,1)S(1)}, u32[]{:S(2)}, u32[]{:S(2)}) collective-permute-start(bf16[256,256]{1,0:T(8,128)(2,1)} %get-tuple-element.60), channel_id=1, source_target_pairs={{0,8},{8,0},{1,9},{9,1},{2,10},{10,2},{3,11},{11,3},{4,12},{12,4},... | collective-permute-start | bytes 393224 | tf_op jit(solution)/shard_map/ppermute | solution.py:725
  101.0 1.0 copy-start.3
  126.5 18.3 %all-to-all-start.4 = ((bf16[32,8,384]{2,1,0:T(8,128)(2,1)}), bf16[32,8,384]{2,1,0:T(8,128)(2,1)S(1)}, u32[]{:S(2)}, u32[]{:S(2)}) async-start(bf16[32,8,384]{2,1,0:T(8,128)(2,1)} %chunk_sum.1), calls=%async_computation.4 | async-start | bytes 393216 | tf_op jit(solution)/shard_map/all_to_all | solution.py:798
  133.2 1.0 copy-start.5
  134.2 14.5 %copy-start.4 = (s32[24]{0:T(128)S(1)}, s32[24]{0:T(128)}, u32[]{:S(2)}) copy-start(s32[24]{0:T(128)} %get-tuple-element.36.info.refs_0_) | copy-start | bytes 292
  139.0 12.1 %collective-permute-start.7 = (bf16[2,384,256]{2,1,0:T(8,128)(2,1)}, bf16[2,384,256]{2,1,0:T(8,128)(2,1)S(1)}, u32[]{:S(2)}, u32[]{:S(2)}) collective-permute-start(bf16[2,384,256]{2,1,0:T(8,128)(2,1)} %get-tuple-element.55), channel_id=1, source_target_pairs={{64,0},{128,64},{192,128},{256,192},{320,256},{384,320},{448,384},... | collective-permute-start | bytes 1179656 | tf_op jit(solution)/shard_map/ppermute | solution.py:720
  141.4 11.9 %collective-permute-start.8 = (bf16[2,384,256]{2,1,0:T(8,128)(2,1)}, bf16[2,384,256]{2,1,0:T(8,128)(2,1)S(1)}, u32[]{:S(2)}, u32[]{:S(2)}) collective-permute-start(bf16[2,384,256]{2,1,0:T(8,128)(2,1)} %get-tuple-element.56), channel_id=1, source_target_pairs={{0,64},{64,128},{128,192},{192,256},{256,320},{320,384},{384,448},... | collective-permute-start | bytes 1179656 | tf_op jit(solution)/shard_map/ppermute | solution.py:720
  145.4 3.2 %collective-permute-start.10 = (bf16[256,256]{1,0:T(8,128)(2,1)S(1)}, bf16[256,256]{1,0:T(8,128)(2,1)S(1)}, u32[]{:S(2)}, u32[]{:S(2)}) collective-permute-start(bf16[256,256]{1,0:T(8,128)(2,1)S(1)} %get-tuple-element.62.own), channel_id=1, source_target_pairs={{0,8},{8,0},{1,9},{9,1},{2,10},{10,2},{3,11},{11,3},{4,12},{12,4},... | collective-permute-start | bytes 393224 | tf_op jit(solution)/shard_map/ppermute | solution.py:725
  151.1 2.2 %copy-start.6 = (bf16[2,384,256]{2,1,0:T(8,128)(2,1)}, bf16[2,384,256]{2,1,0:T(8,128)(2,1)S(1)}, u32[]{:S(2)}) copy-start(bf16[2,384,256]{2,1,0:T(8,128)(2,1)S(1)} %collective-permute-done.7.up) | copy-start | bytes 1179652
  153.3 0.8 copy-start.7
